TPU v7x, 256 devices: a whole 4x4x8 slice. The times are simulated.
256 devices in a mesh: agg: 64 (over x, z, core), col: 4 (over y).
Axes of the slice: x: 4, y: 4, z: 8, core: 2. Of those that a mesh axis runs over, the one named last changes fastest.
Arguments:
- fine_tiles: bfloat16 [1024, 4, 192, 192], P('agg', 'col')
- fine_cols: int32 [1024, 4], P('agg', 'col'), may hold values from 0 to 1023, as said below
- agg_of: int32 [1024], P('agg'), may hold values from 0 to 255, as said below
- prolong: bfloat16 [1024, 192, 192], P('agg'), may hold values from -0.21875 to 0.21875
- coarse_cols: int32 [256, 4], P('agg'), may hold values from 0 to 255, as said below
Outputs:
- coarse_tiles: float32 [256, 4, 192, 192], P('agg', 'col')
- factor_tiles: float32 [256, 4, 192, 192], P('agg', 'col')
Inputs may be any that keep to these rules, and one draw needn't show every extreme that they name: Fine block row i belongs to an aggregate of its own index of agg: i // 16 * 4 <= agg_of[i] < i // 16 * 4 + 4; every aggregate has at least one fine row. `coarse_cols`: slot 0 of aggregate row c is c itself; the other slots are distinct aggregates c + o with 1 <= |o| <= 4. `fine_cols`: slot 0 of fine row i is i; for slots 1 and above the aggregate of the named fine row is one of the slots 1 and above of row agg_of[i] of coarse_cols.
All inputs are finite; a program needn't handle non-finite values.
Results may differ from a plain program's by a relative error of at most 0.0055.
Values may be sent and summed in bfloat16 or wider, within the bound.
No kernel may reach another device: no remote copies, remote signals or barrier semaphores. Data moves between devices by JAX's collectives and lax.ppermute only.
A program may use at most 128 MiB of HBM per device.

v0:
```python
import jax
import jax.numpy as jnp
from jax import lax
from jax.sharding import PartitionSpec as P

SWEEPS = 2


HIGHEST = lax.Precision.HIGHEST


def with_halo(cells, sides, width):
    for axis, dim in sides:
        count = lax.axis_size(axis)
        ends = count - 1
        head = lax.slice_in_dim(cells, 0, width, axis=dim)
        tail = lax.slice_in_dim(cells, cells.shape[dim] - width, cells.shape[dim], axis=dim)
        cells = jnp.concatenate(
            [
                lax.ppermute(tail, axis, [(i, (i + 1) % count) for i in range(ends)]),
                cells,
                lax.ppermute(head, axis, [((i + 1) % count, i) for i in range(ends)]),
            ],
            axis=dim,
        )
    return cells


def cut_along(x, dim, devices):
    before, after = (x.shape[:dim], x.shape[dim + 1 :])
    return jnp.moveaxis(x.reshape(*before, devices, -1, *after), dim, 0)


def sum_at_owner(x, axis, dim):
    pieces = cut_along(x, dim, lax.axis_size(axis))
    arrived = lax.all_to_all(pieces, axis, split_axis=0, concat_axis=0, tiled=True)
    return arrived.sum(axis=0)


def joined_along(pieces, dim):
    dims = list(pieces.shape[1:])
    dims[dim] *= pieces.shape[0]
    return jnp.moveaxis(pieces, 0, dim).reshape(dims)


def sent_to_all(x, axis):
    copies = jnp.broadcast_to(x, (lax.axis_size(axis), *x.shape))
    return lax.all_to_all(copies, axis, split_axis=0, concat_axis=0, tiled=True)


def gathered_copies(x, axis, dim):
    return joined_along(sent_to_all(x, axis), dim)


def passed_along(block, axis, distance):
    devices = range(lax.axis_size(axis))
    route = [(i - distance, i) for i in devices if i - distance in devices]
    return lax.ppermute(block, axis, route)


def relax_rows(
    target_coarse,
    target_old,
    target_cols,
    row_full,
    row_cols,
    ext_full,
    ext_cols,
    row_base,
    ext_base,
):
    row_count = row_cols.shape[0]
    ext_count = ext_full.shape[0]
    width = row_full.shape[-1]
    row_ids = row_base + jnp.arange(row_count, dtype=jnp.int32)
    lowest = jnp.minimum(row_ids[:, None], target_cols)
    prior_index = jnp.clip(row_cols - ext_base, 0, ext_count - 1).astype(jnp.int32)
    further = ext_full[prior_index]
    further_cols = ext_cols[prior_index]
    matched = (further_cols[:, None, :, :] == target_cols[:, :, None, None]) & (
        row_cols[:, None, :, None] < lowest[:, :, None, None]
    )
    chosen = jnp.einsum(
        "rqmn,rmnab->rqmab", matched.astype(jnp.float32), further, precision=HIGHEST
    )
    through = jnp.einsum("rmab,rqmbc->rqac", row_full, chosen, precision=HIGHEST)
    own_diag = row_full[:, 0]
    diag_index = jnp.clip(target_cols - ext_base, 0, ext_count - 1).astype(jnp.int32)
    their_diag = ext_full[diag_index, 0]
    upper_mask = jnp.arange(width)[None, :] > jnp.arange(width)[:, None]
    lower_mask = upper_mask.T
    upper_tile = row_ids[:, None] < target_cols
    lower_tile = row_ids[:, None] > target_cols
    on_diagonal = row_ids[:, None] == target_cols
    right_factor = jnp.where(
        upper_tile[:, :, None, None], target_old, jnp.where(upper_mask, own_diag, 0.0)[:, None]
    )
    lower_term = jnp.einsum(
        "rab,rqbc->rqac", jnp.where(lower_mask, own_diag, 0.0), right_factor, precision=HIGHEST
    )
    upper_term = jnp.einsum(
        "rqab,rqbc->rqac", target_old, jnp.where(upper_mask, their_diag, 0.0), precision=HIGHEST
    )
    edge_term = jnp.where(lower_tile[:, :, None, None], upper_term, lower_term)
    residue = target_coarse - through - edge_term
    pivots = jnp.maximum(jnp.diagonal(their_diag, axis1=-2, axis2=-1), 1.0)
    scaled = lower_tile[:, :, None, None] | on_diagonal[:, :, None, None] & lower_mask[None, None]
    return jnp.where(scaled, residue / pivots[:, :, None, :], residue)


def on_device(fine_tiles, fine_cols, agg_of, prolong, coarse_cols):
    agg_index = lax.axis_index("agg")
    col_index = lax.axis_index("col")
    rows_here = prolong.shape[0]
    coarse_here = coarse_cols.shape[0]
    nearby, nearby_labels = (
        with_halo(prolong, (("agg", 0),), rows_here),
        with_halo(agg_of, (("agg", 0),), rows_here),
    )
    local_index = fine_cols - (agg_index - 1) * rows_here
    remote = nearby[local_index]
    targets = nearby_labels[local_index]
    carried = jnp.einsum(
        "isab,isbc->isac", fine_tiles, remote, preferred_element_type=jnp.float32
    ).astype(jnp.bfloat16)
    lifted = jnp.einsum("iba,isbc->isac", prolong, carried, preferred_element_type=jnp.float32)
    owned_rows = agg_index * coarse_here + jnp.arange(coarse_here, dtype=jnp.int32)
    weights = (
        (agg_of[:, None] == owned_rows[None, :])[:, None, :, None]
        & (coarse_cols[None, None, :, :] == targets[:, :, None, None])
    ).astype(jnp.float32)
    partial_value = jnp.einsum("isrq,isac->rqac", weights, lifted, precision=HIGHEST)
    coarse_own = sum_at_owner(partial_value, "col", 1)
    slot_count = coarse_own.shape[1]
    target_cols = lax.dynamic_slice_in_dim(coarse_cols, col_index * slot_count, slot_count, 1)
    row_base = agg_index * coarse_here
    ext_base = row_base - coarse_here
    current = coarse_own
    for sweep_step in range(SWEEPS):
        full_rows = gathered_copies(current, "col", 1)
        prior_full, prior_cols = passed_along((full_rows, coarse_cols), "agg", 1)
        ext_full = jnp.concatenate([prior_full, full_rows], axis=0)
        ext_cols = jnp.concatenate([prior_cols, coarse_cols], axis=0)
        current = relax_rows(
            coarse_own,
            current,
            target_cols,
            full_rows,
            coarse_cols,
            ext_full,
            ext_cols,
            row_base,
            ext_base,
        )
    return (coarse_own, current)


def solution(mesh):
    in_specs = (
        P("agg", "col", None, None),
        P("agg", "col"),
        P("agg"),
        P("agg", None, None),
        P("agg", None),
    )
    out_specs = (P("agg", "col", None, None), P("agg", "col", None, None))
    return jax.shard_map(
        on_device, mesh=mesh, in_specs=in_specs, out_specs=out_specs, check_vma=False
    )
```

profile of v0, /device:TPU:6, one launch (start us, length us, event | category | flops | bytes accessed | tf_op | source)
XLA Modules:
  0.0 348.7 jit_solution(97111097748446025)
XLA Ops:
  0.6 7.6 %collective-permute-start.3 = (bf16[16,192,192]{2,1,0:T(8,128)(2,1)}, bf16[16,192,192]{2,1,0:T(8,128)(2,1)S(1)}, u32[]{:S(2)}, u32[]{:S(2)}) collective-permute-start(bf16[16,192,192]{2,1,0:T(8,128)(2,1)} %param.8), channel_id=1, source_target_pairs={{4,0},{8,4},{12,8},{16,12},{20,16},{24,20},{28,24},{32,28},{36,32}... | collective-permute-start | bytes 3538952 | tf_op jit(solution)/shard_map/ppermute | solution.py:22
  10.2 5.8 %collective-permute-start.1 = (s32[16]{0:T(128)}, s32[16]{0:T(128)S(1)}, u32[]{:S(2)}, u32[]{:S(2)}) collective-permute-start(s32[16]{0:T(128)} %param.7), channel_id=1, source_target_pairs={{4,0},{8,4},{12,8},{16,12},{20,16},{24,20},{28,24},{32,28},{36,32}... | collective-permute-start | bytes 200 | tf_op jit(solution)/shard_map/ppermute | solution.py:22
  19.3 7.2 %collective-permute-done.1 = s32[16]{0:T(128)S(1)} collective-permute-done((s32[16]{0:T(128)}, s32[16]{0:T(128)S(1)}, u32[]{:S(2)}, u32[]{:S(2)}) %collective-permute-start.1) | collective-permute-done | bytes 96 | tf_op jit(solution)/shard_map/ppermute | solution.py:22
  26.5 5.9 %collective-permute-done = s32[16]{0:T(128)S(1)} collective-permute-done((s32[16]{0:T(128)}, s32[16]{0:T(128)S(1)}, u32[]{:S(2)}, u32[]{:S(2)}) %collective-permute-start) | collective-permute-done | bytes 96 | tf_op jit(solution)/shard_map/ppermute | solution.py:20
  33.8 4.0 %pad_maximum_fusion.2 = bf16[48,192,192]{2,1,0:T(8,128)(2,1)} fusion(bf16[16,192,192]{2,1,0:T(8,128)(2,1)S(1)} %collective-permute-done.3, bf16[16,192,192]{2,1,0:T(8,128)(2,1)} %param.8, bf16[16,192,192]{2,1,0:T(8,128)(2,1)} %collective-permute-done.2), kind=kLoop, calls=%fused_computation.13 | loop fusion | flops 3538944 | bytes 7077888 | tf_op jit(solution)/shard_map/concatenate | solution.py:18
  37.8 4.3 %gather_fusion.1 = bf16[16,192,192]{2,1,0:T(8,128)(2,1)} fusion(bf16[48,192,192]{2,1,0:T(8,128)(2,1)} %pad_maximum_fusion.2, s32[1024]{0:T(1024)S(1)} %pad_clamp_fusion.1), kind=kCustom, calls=%fused_computation.1 | custom fusion | bytes 2359360 | tf_op jit(solution)/shard_map/gather | solution.py:121
  42.1 4.3 %convolution_bitcast_fusion = f32[16,192,192]{1,2,0:T(8,128)} fusion(bf16[16,192,192]{2,1,0:T(8,128)(2,1)S(1)} %copy-done.6, bf16[16,192,192]{2,1,0:T(8,128)(2,1)} %gather_fusion.1, bf16[16,1,192,192]{3,2,1,0:T(8,128)(2,1)S(1)} %copy-done), kind=kOutput, calls=%fused_computation.20 | convolution fusion | flops 453574656 | bytes 5898240 | tf_op jit(solution)/shard_map/iba,isbc->isac/dot_general | solution.py:126
  46.3 4.1 %copy.42 = f32[16,192,192]{2,0,1:T(8,128)} copy(f32[16,192,192]{1,2,0:T(8,128)} %convolution_bitcast_fusion) | data formatting | bytes 4718592 | tf_op jit(solution)/shard_map/reshape.14
  50.4 4.2 %fusion.4 = f32[4,4,1,192,192]{4,0,3,1,2:T(4,128)S(1)} fusion(f32[16,192,192]{2,0,1:T(8,128)} %copy.42, s32[16]{0:T(128)S(1)} %gather_fusion, s32[4,4]{1,0:T(4,128)S(1)} %copy-done.8, pred[16,4]{0,1:T(4,128)(4,1)S(1)} %broadcast_compare_fusion.1), kind=kOutput, calls=%fused_computation.19 | convolution fusion | flops 113246720 | bytes 4718784 | tf_op jit(solution)/shard_map/isrq,isac->rqac/dot_general | solution.py:132
  55.3 34.0 %all_to_all.15 = f32[4,4,1,192,192]{4,3,1,2,0:T(8,128)} all-to-all(f32[4,4,1,192,192]{4,3,1,2,0:T(8,128)S(1)} %copy.43), channel_id=1, replica_groups=mesh['agg'=64,'col'=4] {'col'}, dimensions={0} | all-to-all | bytes 4718592 | tf_op jit(solution)/shard_map/all_to_all | solution.py:36
  89.3 2.2 reduce_sum.11
  91.8 31.3 %all_to_all.16 = f32[4,4,1,192,192]{4,3,1,2,0:T(8,128)S(1)} all-to-all(f32[4,4,1,192,192]{4,3,1,2,0:T(8,128)S(1)} %broadcast_in_dim.117), channel_id=1, replica_groups=mesh['agg'=64,'col'=4] {'col'}, dimensions={0} | all-to-all | bytes 4718592 | tf_op jit(solution)/shard_map/all_to_all | solution.py:48
  127.6 11.8 %collective-permute-start.5 = (s32[4,4]{1,0:T(4,128)S(1)}, s32[4,4]{1,0:T(4,128)S(1)}, u32[]{:S(2)}, u32[]{:S(2)}) collective-permute-start(s32[4,4]{1,0:T(4,128)S(1)} %copy-done.8), channel_id=1, source_target_pairs={{0,4},{4,8},{8,12},{12,16},{16,20},{20,24},{24,28},{28,32},{32,36}... | collective-permute-start | bytes 200 | tf_op jit(solution)/shard_map/ppermute | solution.py:58
  139.9 37.4 %collective-permute-done.5 = s32[4,4]{1,0:T(4,128)S(1)} collective-permute-done((s32[4,4]{1,0:T(4,128)S(1)}, s32[4,4]{1,0:T(4,128)S(1)}, u32[]{:S(2)}, u32[]{:S(2)}) %collective-permute-start.5) | collective-permute-done | bytes 96 | tf_op jit(solution)/shard_map/ppermute | solution.py:58
  178.2 2.5 convolution_bitcast_fusion.3
  180.7 6.2 %pad_maximum_fusion = f32[8,4,192,192]{3,2,1,0:T(8,128)} fusion(f32[4,4,192,192]{3,2,1,0:T(8,128)} %bitcast.141, f32[4,4,192,192]{3,2,1,0:T(8,128)} %collective-permute-done.4), kind=kLoop, calls=%fused_computation.11 | loop fusion | flops 1179648 | bytes 9437184 | tf_op jit(solution)/shard_map/concatenate | solution.py:142
  186.8 8.7 %gather_fusion.2 = f32[16,4,192,192]{3,2,1,0:T(8,128)} fusion(f32[8,4,192,192]{3,2,1,0:T(8,128)} %pad_maximum_fusion, s32[1024]{0:T(1024)S(1)} %pad_clamp_fusion), kind=kCustom, calls=%fused_computation.2 | custom fusion | bytes 18874432 | tf_op jit(solution)/shard_map/gather | solution.py:78
  195.5 3.4 gather_fusion.4
  198.9 9.7 %copy.51 = f32[4,192,192]{0,2,1:T(8,128)} copy(f32[4,192,192]{2,1,0:T(8,128)S(1)} %gather_fusion.4) | data formatting | bytes 1179648 | tf_op jit(solution)/shard_map/gather | solution.py:89
  208.6 4.7 %gather_fusion.5 = f32[192,4]{1,0:T(8,128)S(1)} fusion(f32[4,192,192]{0,2,1:T(8,128)} %copy.51, s32[192]{0:T(256)S(1)} %bitcast.147), kind=kCustom, calls=%fused_computation.5 | custom fusion | bytes 7680 | tf_op jit(solution)/shard_map/jit(diagonal)/gather | solution.py:106
  214.3 6.8 %multiply_reduce_fusion.1 = f32[4,4,192,192]{3,2,1,0:T(8,128)S(1)} fusion(f32[4,4,4,192,192]{4,3,2,1,0:T(8,128)} %bitcast.142, f32[4,4,4]{2,1,0:T(4,128)S(1)} %copy.88), kind=kLoop, calls=%fused_computation.10 | loop fusion | flops 4128768 | bytes 11796736 | tf_op jit(solution)/shard_map/rqmn,rmnab->rqmab/dot_general | solution.py:83
  221.1 3.3 divide_select_fusion.1
  224.8 35.0 %all_to_all.17 = f32[4,4,1,192,192]{4,3,1,2,0:T(8,128)S(1)} all-to-all(f32[4,4,1,192,192]{4,3,1,2,0:T(8,128)S(1)} %broadcast_in_dim.127), channel_id=1, replica_groups=mesh['agg'=64,'col'=4] {'col'}, dimensions={0} | all-to-all | bytes 4718592 | tf_op jit(solution)/shard_map/all_to_all | solution.py:48
  263.9 36.6 %collective-permute-done.6 = f32[4,4,192,192]{3,2,0,1:T(8,128)S(1)} collective-permute-done((f32[4,4,192,192]{3,2,0,1:T(8,128)S(1)}, f32[4,4,192,192]{3,2,0,1:T(8,128)S(1)}, u32[]{:S(2)}, u32[]{:S(2)}) %collective-permute-start.6) | collective-permute-done | bytes 2359328 | tf_op jit(solution)/shard_map/ppermute | solution.py:58
  300.5 3.2 pad_maximum_fusion.1
  303.7 3.4 gather_fusion.7
  307.1 8.7 %gather_fusion.6 = f32[16,4,192,192]{3,2,1,0:T(8,128)} fusion(f32[8,4,192,192]{3,2,0,1:T(8,128)} %pad_maximum_fusion.1, s32[1024]{0:T(1024)S(1)} %pad_clamp_fusion), kind=kCustom, calls=%fused_computation.6 | custom fusion | bytes 18874432 | tf_op jit(solution)/shard_map/gather | solution.py:78
  315.8 9.6 %copy.58 = f32[4,192,192]{0,2,1:T(8,128)} copy(f32[4,192,192]{2,1,0:T(8,128)S(1)} %gather_fusion.7) | data formatting | bytes 1179648 | tf_op jit(solution)/shard_map/gather | solution.py:89
  325.4 3.0 fusion.22
  328.4 8.4 %multiply_reduce_fusion = f32[4,4,192,192]{3,2,1,0:T(8,128)} fusion(f32[4,4,4,192,192]{4,3,2,1,0:T(8,128)} %bitcast.143, f32[4,4,4]{2,1,0:T(4,128)S(1)} %copy.88), kind=kLoop, calls=%fused_computation.9 | loop fusion | flops 4128768 | bytes 11796736 | tf_op jit(solution)/shard_map/rqmn,rmnab->rqmab/dot_general | solution.py:83
  336.8 4.7 %gather_fusion.8 = f32[192,4]{1,0:T(8,128)S(1)} fusion(f32[4,192,192]{0,2,1:T(8,128)} %copy.58, s32[192]{0:T(256)S(1)} %bitcast.148), kind=kCustom, calls=%fused_computation.8 | custom fusion | bytes 7680 | tf_op jit(solution)/shard_map/jit(diagonal)/gather | solution.py:106
  341.6 7.1 %fusion.25 = f32[4,1,192,192]{3,2,1,0:T(8,128)} fusion(f32[4,1,192,192]{3,2,0,1:T(8,128)S(1)} %copy-done.7, f32[4,4,192,192]{3,2,1,0:T(8,128)} %multiply_reduce_fusion, f32[4,192,192]{2,1,0:T(8,128)S(1)} %reduce_sum.11, f32[4,192]{1,0:T(4,128)S(1)} %copy.59, pred[4]{0:T(512)(128)(4,1)S(1)} %get-tuple-element.10, ...), kind=kOutput, calls=%fused_computation.37 | convolution fusion | flops 1359839232 | bytes 6528008 | tf_op jit(solution)/shard_map/rmab,rqmbc->rqac/dot_general | solution.py:86
  (59 shorter events, 18.9 us)
Async XLA Ops:
  0.6 41.4 %copy-start = (bf16[16,1,192,192]{3,2,1,0:T(8,128)(2,1)S(1)}, bf16[16,1,192,192]{3,2,1,0:T(8,128)(2,1)}, u32[]{:S(2)}) copy-start(bf16[16,1,192,192]{3,2,1,0:T(8,128)(2,1)} %param.5) | copy-start | bytes 3538948
  0.6 33.2 %collective-permute-start.3 = (bf16[16,192,192]{2,1,0:T(8,128)(2,1)}, bf16[16,192,192]{2,1,0:T(8,128)(2,1)S(1)}, u32[]{:S(2)}, u32[]{:S(2)}) collective-permute-start(bf16[16,192,192]{2,1,0:T(8,128)(2,1)} %param.8), channel_id=1, source_target_pairs={{4,0},{8,4},{12,8},{16,12},{20,16},{24,20},{28,24},{32,28},{36,32}... | collective-permute-start | bytes 3538952 | tf_op jit(solution)/shard_map/ppermute | solution.py:22
  8.3 25.6 %collective-permute-start.2 = (bf16[16,192,192]{2,1,0:T(8,128)(2,1)}, bf16[16,192,192]{2,1,0:T(8,128)(2,1)}, u32[]{:S(2)}, u32[]{:S(2)}) collective-permute-start(bf16[16,192,192]{2,1,0:T(8,128)(2,1)} %param.8), channel_id=1, source_target_pairs={{0,4},{4,8},{8,12},{12,16},{16,20},{20,24},{24,28},{28,32},{32,36}... | collective-permute-start | bytes 3538952 | tf_op jit(solution)/shard_map/ppermute | solution.py:20
  10.2 16.3 %collective-permute-start.1 = (s32[16]{0:T(128)}, s32[16]{0:T(128)S(1)}, u32[]{:S(2)}, u32[]{:S(2)}) collective-permute-start(s32[16]{0:T(128)} %param.7), channel_id=1, source_target_pairs={{4,0},{8,4},{12,8},{16,12},{20,16},{24,20},{28,24},{32,28},{36,32}... | collective-permute-start | bytes 200 | tf_op jit(solution)/shard_map/ppermute | solution.py:22
  15.9 16.5 %collective-permute-start = (s32[16]{0:T(128)}, s32[16]{0:T(128)S(1)}, u32[]{:S(2)}, u32[]{:S(2)}) collective-permute-start(s32[16]{0:T(128)} %param.7), channel_id=1, source_target_pairs={{0,4},{4,8},{8,12},{12,16},{16,20},{20,24},{24,28},{28,32},{32,36}... | collective-permute-start | bytes 200 | tf_op jit(solution)/shard_map/ppermute | solution.py:20
  37.8 4.3 %copy-start.6 = (bf16[16,192,192]{2,1,0:T(8,128)(2,1)S(1)}, bf16[16,192,192]{2,1,0:T(8,128)(2,1)}, u32[]{:S(2)}) copy-start(bf16[16,192,192]{2,1,0:T(8,128)(2,1)} %param.8) | copy-start | bytes 3538948
  46.3 4.1 %copy-start.8 = (s32[4,4]{1,0:T(4,128)S(1)}, s32[4,4]{1,0:T(4,128)}, u32[]{:S(2)}) copy-start(s32[4,4]{1,0:T(4,128)} %param.9) | copy-start | bytes 196
  91.5 250.1 %copy-start.5 = (f32[4,192,192]{2,1,0:T(8,128)}, f32[4,192,192]{2,1,0:T(8,128)S(1)}, u32[]{:S(2)}) copy-start(f32[4,192,192]{2,1,0:T(8,128)S(1)} %reduce_sum.11) | copy-start | bytes 1769476
  123.1 2.6 copy-start.3
  125.7 55.0 %collective-permute-start.4 = (f32[4,4,192,192]{3,2,1,0:T(8,128)}, f32[4,4,192,192]{3,2,1,0:T(8,128)}, u32[]{:S(2)}, u32[]{:S(2)}) collective-permute-start(f32[4,4,192,192]{3,2,1,0:T(8,128)} %bitcast.141), channel_id=1, source_target_pairs={{0,4},{4,8},{8,12},{12,16},{16,20},{20,24},{24,28},{28,32},{32,36}... | collective-permute-start | bytes 7077896 | tf_op jit(solution)/shard_map/ppermute | solution.py:58
  127.6 49.7 %collective-permute-start.5 = (s32[4,4]{1,0:T(4,128)S(1)}, s32[4,4]{1,0:T(4,128)S(1)}, u32[]{:S(2)}, u32[]{:S(2)}) collective-permute-start(s32[4,4]{1,0:T(4,128)S(1)} %copy-done.8), channel_id=1, source_target_pairs={{0,4},{4,8},{8,12},{12,16},{16,20},{20,24},{24,28},{28,32},{32,36}... | collective-permute-start | bytes 200 | tf_op jit(solution)/shard_map/ppermute | solution.py:58
  214.3 6.8 %copy-start.4 = (f32[4,4,1,192,192]{4,3,1,2,0:T(8,128)S(1)}, f32[4,4,1,192,192]{4,3,1,2,0:T(8,128)}, u32[]{:S(2)}) copy-start(f32[4,4,1,192,192]{4,3,1,2,0:T(8,128)} %copy-done.3) | copy-start | bytes 7077892
  259.8 40.7 %copy-start.2 = (f32[4,4,1,192,192]{4,3,1,2,0:T(8,128)}, f32[4,4,1,192,192]{4,3,1,2,0:T(8,128)S(1)}, u32[]{:S(2)}) copy-start(f32[4,4,1,192,192]{4,3,1,2,0:T(8,128)S(1)} %all_to_all.17) | copy-start | bytes 7077892
  259.8 40.7 %collective-permute-start.6 = (f32[4,4,192,192]{3,2,0,1:T(8,128)S(1)}, f32[4,4,192,192]{3,2,0,1:T(8,128)S(1)}, u32[]{:S(2)}, u32[]{:S(2)}) collective-permute-start(f32[4,4,192,192]{3,2,0,1:T(8,128)S(1)} %bitcast.144), channel_id=1, source_target_pairs={{0,4},{4,8},{8,12},{12,16},{16,20},{20,24},{24,28},{28,32},{32,36}... | collective-permute-start | bytes 7077896 | tf_op jit(solution)/shard_map/ppermute | solution.py:58
  328.4 13.2 %copy-start.7 = (f32[4,1,192,192]{3,2,0,1:T(8,128)S(1)}, f32[4,1,192,192]{3,2,0,1:T(8,128)}, u32[]{:S(2)}) copy-start(f32[4,1,192,192]{3,2,0,1:T(8,128)} %fusion.22) | copy-start | bytes 1769476
  341.5 7.2 %copy-start.1 = (bf16[16,1,192,192]{3,2,1,0:T(8,128)(2,1)S(1)}, bf16[16,1,192,192]{3,2,1,0:T(8,128)(2,1)}, u32[]{:S(2)}) copy-start(bf16[16,1,192,192]{3,2,1,0:T(8,128)(2,1)} %param.5) | copy-start | bytes 3538948
where the time goes:
time: 350 us; the launch traced here: 349 us
  blocking collectives  100 us (29%)
  waiting for transfers between devices  87.1 us (25%)
  local copies, waits for them, and re-layouts  66.8 us (19%)
  other arithmetic  33.2 us (9%)
  starting transfers between devices  33 us (9%)
  matrix products  27.3 us (8%)
    ppermute x3, waiting for transfers between devices, passed_along(): return lax.ppermute(block, axis, route)  74 us
    all_to_all x2, blocking collectives, sent_to_all(): return lax.all_to_all(copies, axis, split_axis=0, concat_axis=0, tiled=True)  66.3 us
    all_to_all x1, blocking collectives, sum_at_owner(): lax.all_to_all(pieces, axis, split_axis=0, concat_axis=0, tiled=True)  34 us
    gather x4, local copies, waits for them, and re-layouts, relax_rows(): their_diag = ext_full[diag_index, 0]  26.1 us
    gather x2, local copies, waits for them, and re-layouts, relax_rows(): further = ext_full[prior_index]  17.4 us
    ppermute x3, starting transfers between devices, passed_along(): return lax.ppermute(block, axis, route)  15.8 us
    dot_general x2, other arithmetic, relax_rows(): jnp.einsum('rqmn,rmnab->rqmab', matched.astype(jnp.float32), further, pre...  15.2 us
    ppermute x2, starting transfers between devices, with_halo(): lax.ppermute(head, axis, [((i + 1) % count, i) for i in range(ends)])  13.4 us
  transfers between devices with their start and end apart: 7, of which 4 were waited for; matrix products, arithmetic and copies ran while one was open for 2% of the time, Pallas kernels for 0%

commit v1 on v0

v1 whole, which is shorter than its diff:
```python
import functools

import jax
import jax.numpy as jnp
from jax import lax
from jax.experimental import pallas as pl
from jax.experimental.pallas import tpu as pltpu
from jax.sharding import PartitionSpec as P

F32 = jnp.float32
BF16 = jnp.bfloat16
VMEM = pl.BlockSpec(memory_space=pltpu.VMEM)
SMEM = pl.BlockSpec(memory_space=pltpu.SMEM)
ANY = pl.BlockSpec(memory_space=pl.ANY)

ROWS = 12
LIST1 = 16
LIST2 = 160
TILES = 192
KINDS = 240
PLAN = 256
ZERO1 = 64
ZERO2 = 48


def iota(shape, dim):
    return lax.broadcasted_iota(jnp.int32, shape, dim)


def lift_kernel(
    ids, cols, labels, left_labels, right_labels, pattern, tiles, own, left, right, mine, ahead, behind, total, remote
):
    agg, col = ids[0], ids[1]
    total[...] = jnp.zeros_like(total)

    def step(i, carry):
        place = cols[i] - (agg - 1) * 16
        within = place & 15
        side = place >> 4
        target = jnp.where(side == 0, left_labels[within], jnp.where(side == 1, labels[within], right_labels[within]))
        row = labels[i] - agg * 4
        slot = jnp.int32(0)
        for q in range(1, 4):
            slot = jnp.where(pattern[row, q] == target, q, slot)

        @pl.when(side == 0)
        def _():
            remote[...] = left[within]

        @pl.when(side == 1)
        def _():
            remote[...] = own[within]

        @pl.when(side == 2)
        def _():
            remote[...] = right[within]

        carried = jnp.dot(tiles[i], remote[...], preferred_element_type=F32).astype(BF16)
        lifted = lax.dot_general(own[i], carried, (((0,), (0,)), ((), ())), preferred_element_type=F32)
        total[slot, row] += lifted
        return carry

    lax.fori_loop(0, 16, step, 0)
    first = jnp.where(col == 3, 1, col + 1)
    second = jnp.where(col <= 1, 3, col - 1)
    for r in range(4):
        mine[r] = total[col, r]
        ahead[r] = total[first, r].astype(BF16)
        behind[r] = total[second, r].astype(BF16)


def plan_kernel(ids, pattern, near, far, plan, pat, need):
    agg, col = ids[0], ids[1]
    base = (agg - 2) * 4
    for r in range(4):
        for q in range(4):
            pat[4 * r + q] = far[r, q]
            pat[16 + 4 * r + q] = near[r, q]
            pat[32 + 4 * r + q] = pattern[r, q]
    for k in range(32):
        need[k] = 0

    def through(row, index, target, m):
        inner = pat[4 * row + m]
        at = jnp.clip(inner - base, 0, ROWS - 1)
        n = jnp.int32(0)
        for q in range(1, 4):
            n = jnp.where(pat[4 * at + q] == target, q, n)
        valid = (inner < jnp.minimum(index, target)) & (n > 0)
        return at, n, valid

    count = jnp.int32(0)
    for r in range(4):
        row = 8 + r
        index = base + row
        target = pat[4 * row + col]
        lower = target < index
        diagonal = jnp.where(lower, jnp.clip(target - base, 4, ROWS - 1), row) - 4
        need[col * 8 + row - 4] = 1
        need[diagonal] = 1
        for m in range(1, 4):
            at, n, valid = through(row, index, target, m)
            x, y = m * 8 + row - 4, n * 8 + jnp.maximum(at - 4, 0)
            plan[LIST2 + count] = x | (y << 8) | (r << 16)
            count = count + valid.astype(jnp.int32)

            @pl.when(valid)
            def _():
                need[x] = 1
                need[y] = 1

        own = col * 8 + row - 4
        x = jnp.where(lower, own, 40 + row - 4)
        y = jnp.where(target > index, own, 32 + diagonal)
        plan[LIST2 + count] = x | (y << 8) | (r << 16)
        count = count + 1
        kind = jnp.where(lower, 1, jnp.where(target == index, 2, 0))
        plan[KINDS + r] = kind | (diagonal << 8)
    plan[1] = count

    def tile(t, carry):
        @pl.when(need[t] == 1)
        def _():
            products, tiles = plan[0], plan[2]
            row = (t & 7) + 4
            slot = t >> 3
            index = base + row
            target = pat[4 * row + slot]
            lower = target < index
            diagonal = jnp.where(lower, jnp.clip(target - base, 4, ROWS - 1), row) - 4
            for m in range(1, 4):
                at, n, valid = through(row, index, target, m)
                plan[LIST1 + products] = (m * ROWS + row) | ((n * ROWS + at) << 8) | (t << 16)
                products = products + valid.astype(jnp.int32)
            own = slot * ROWS + row
            x = jnp.where(lower, own, 56 + row - 4)
            y = jnp.where(target > index, own, 48 + diagonal)
            plan[LIST1 + products] = x | (y << 8) | (t << 16)
            plan[0] = products + 1
            kind = jnp.where(lower, 1, jnp.where(target == index, 2, 0))
            plan[TILES + tiles] = t | (kind << 8) | (diagonal << 16)
            plan[2] = tiles + 1

        return carry

    plan[0] = 0
    plan[2] = 0
    lax.fori_loop(0, 32, tile, 0)
    plan[LIST1 + plan[0]] = ZERO1 | (ZERO1 << 8) | (32 << 16)


def sweep_kernel(ids, plan, coarse, *refs):
    pieces, (out, first, work, high, low, pivots, pivots_next, sems) = refs[:12], refs[12:]
    col = ids[1]
    width = coarse.shape[-1]
    copies = []
    for k, piece in enumerate(pieces):
        block, shift = k // 4, (0, 3, 1, 2)[k % 4]
        slot = (col + shift) & 3
        start = slot * ROWS + block * 4
        copies.append(pltpu.make_async_copy(piece, first.at[pl.ds(start, 4)], sems.at[k]))
        copies[-1].start()
    first[ZERO1] = jnp.zeros((width, width), BF16)
    lines, columns = iota((width, width), 0), iota((width, width), 1)
    upper, lower, equal = columns > lines, lines > columns, lines == columns

    def reciprocal(tile):
        return 1.0 / jnp.maximum(jnp.sum(jnp.where(equal, tile, 0.0), axis=0, keepdims=True), 1.0)

    for copy in copies:
        copy.wait()

    def prepare(k, carry):
        diagonal = first[4 + k].astype(F32)
        first[48 + k] = jnp.where(upper, diagonal, 0.0).astype(BF16)
        first[56 + k] = jnp.where(lower, diagonal, 0.0).astype(BF16)
        pivots[k] = reciprocal(diagonal)
        return carry

    lax.fori_loop(0, 8, prepare, 0)

    def begin(k, carry):
        t = plan[TILES + k] & 255
        work[t] = first[(t >> 3) * ROWS + (t & 7) + 4].astype(F32)
        return carry

    lax.fori_loop(0, plan[2], begin, 0)

    def multiply(k, carry):
        a, b = plan[LIST1 + 2 * k], plan[LIST1 + 2 * k + 1]
        one = jnp.dot(first[a & 255], first[(a >> 8) & 255], preferred_element_type=F32)
        two = jnp.dot(first[b & 255], first[(b >> 8) & 255], preferred_element_type=F32)
        work[a >> 16] -= one
        work[b >> 16] -= two
        return carry

    lax.fori_loop(0, (plan[0] + 1) >> 1, multiply, 0)

    def scaled(tile, kind, row):
        factor = jnp.where((kind == 1) | ((kind == 2) & lower), row, 1.0)
        return tile * factor

    def split(t, tile):
        top = tile.astype(BF16)
        high[t] = top
        low[t] = (tile - top.astype(F32)).astype(BF16)

    def finish(k, carry):
        entry = plan[TILES + k]
        t, kind, diagonal = entry & 255, (entry >> 8) & 255, entry >> 16
        tile = scaled(work[t], kind, pivots[diagonal])
        split(t, tile)

        @pl.when(t < 8)
        def _():
            split(32 + t, jnp.where(upper, tile, 0.0))
            split(40 + t, jnp.where(lower, tile, 0.0))
            pivots_next[t] = reciprocal(tile)

        return carry

    lax.fori_loop(0, plan[2], finish, 0)
    out[...] = coarse[...]

    def again(k, carry):
        entry = plan[LIST2 + k]
        x, y, r = entry & 255, (entry >> 8) & 255, entry >> 16
        product = jnp.dot(high[x], high[y], preferred_element_type=F32)
        product += jnp.dot(high[x], low[y], preferred_element_type=F32)
        product += jnp.dot(low[x], high[y], preferred_element_type=F32)
        out[r] -= product
        return carry

    lax.fori_loop(0, plan[1], again, 0)
    for r in range(4):
        entry = plan[KINDS + r]
        out[r] = scaled(out[r], entry & 255, pivots_next[entry >> 8])


def along(block, axis, distance, ring=False):
    count = lax.axis_size(axis)
    pairs = [(i, (i + distance) % count) for i in range(count) if ring or 0 <= i + distance < count]
    return lax.ppermute(block, axis, pairs)


def on_device(fine_tiles, fine_cols, agg_of, prolong, coarse_cols):
    width = prolong.shape[-1]
    agg, col = lax.axis_index("agg"), lax.axis_index("col")
    ids = jnp.stack([agg, col]).astype(jnp.int32)
    left, right = along(prolong, "agg", 1), along(prolong, "agg", -1)
    left_labels, right_labels = along(agg_of, "agg", 1), along(agg_of, "agg", -1)
    near, far = along(coarse_cols, "agg", 1), along(coarse_cols, "agg", 2)

    def call(kernel, ins, outs, out_specs, scratch, name):
        return pl.pallas_call(
            kernel,
            out_shape=outs,
            in_specs=ins,
            out_specs=out_specs,
            scratch_shapes=scratch,
            name=name,
            compiler_params=pltpu.CompilerParams(vmem_limit_bytes=60 << 20),
        )

    four = (4, width, width)
    mine, ahead, behind = call(
        lift_kernel,
        [SMEM] * 6 + [VMEM] * 4,
        (jax.ShapeDtypeStruct(four, F32), jax.ShapeDtypeStruct(four, BF16), jax.ShapeDtypeStruct(four, BF16)),
        (VMEM, VMEM, VMEM),
        [pltpu.VMEM((4, *four), F32), pltpu.VMEM((width, width), BF16)],
        "lift",
    )(
        ids,
        fine_cols.reshape(-1),
        agg_of,
        left_labels,
        right_labels,
        coarse_cols,
        fine_tiles.reshape(-1, width, width),
        prolong,
        left,
        right,
    )
    plan = call(
        plan_kernel,
        [SMEM] * 4,
        jax.ShapeDtypeStruct((PLAN,), jnp.int32),
        SMEM,
        [pltpu.SMEM((48,), jnp.int32), pltpu.SMEM((32,), jnp.int32)],
        "plan",
    )(ids, coarse_cols, near, far)

    came_ahead = lax.ppermute(ahead, "col", [(1, 2), (2, 3), (3, 1)])
    came_behind = lax.ppermute(behind, "col", [(1, 3), (2, 1), (3, 2)])
    coarse = mine + came_ahead.astype(F32) + came_behind.astype(F32)
    sent = coarse.astype(BF16)

    def spread(x):
        return [x, along(x, "col", 1, True), along(x, "col", -1, True), along(x, "col", 2, True)]

    here = spread(sent)
    far_sent = along(sent, "agg", 2)
    before = [along(x, "agg", 1) for x in here]
    further = spread(far_sent)
    factor = call(
        sweep_kernel,
        [SMEM] * 2 + [VMEM] + [ANY] * 12,
        jax.ShapeDtypeStruct(four, F32),
        VMEM,
        [
            pltpu.VMEM((65, width, width), BF16),
            pltpu.VMEM((33, width, width), F32),
            pltpu.VMEM((49, width, width), BF16),
            pltpu.VMEM((49, width, width), BF16),
            pltpu.VMEM((8, 1, width), F32),
            pltpu.VMEM((8, 1, width), F32),
            pltpu.SemaphoreType.DMA((12,)),
        ],
        "sweep",
    )(ids, plan, coarse, *further, *before, *here)
    return (coarse[:, None], factor[:, None])


def solution(mesh):
    in_specs = (
        P("agg", "col", None, None),
        P("agg", "col"),
        P("agg"),
        P("agg", None, None),
        P("agg", None),
    )
    out_specs = (P("agg", "col", None, None), P("agg", "col", None, None))
    return jax.shard_map(
        on_device, mesh=mesh, in_specs=in_specs, out_specs=out_specs, check_vma=False
    )
```

time: 350 us -> 123 us (0.35)
  blocking collectives: 100 us -> 0 us
  local copies, waits for them, and re-layouts: 66.8 us -> 1.67 us
  waiting for transfers between devices: 87.1 us -> 27.9 us
  starting transfers between devices: 33 us -> 65.9 us
  other arithmetic: 33.2 us -> 2.81 us
  matrix products: 27.3 us -> 0 us
  Pallas kernels: 0 us -> 22.3 us
    all_to_all x3 -> x0, blocking collectives: 100 us -> none  [the longest x2 66.3 us: sent_to_all(): return lax.all_to_all(copies, axis, split_axis=0, concat_axis=0, tiled=True)]
    ppermute x7 -> x19, waiting for transfers between devices: 87.1 us -> 27.9 us  [the longest x17 27.9 us: along(): return lax.ppermute(block, axis, pairs)]
    gather x12 -> x0, local copies, waits for them, and re-layouts: 58.4 us -> none  [the longest x4 26.1 us: relax_rows(): their_diag = ext_full[diag_index, 0]]
    ppermute x7 -> x19, starting transfers between devices: 33 us -> 65.9 us  [the longest x17 64.4 us: along(): return lax.ppermute(block, axis, pairs)]
    dot_general x8 -> x0, matrix products: 27.3 us -> none  [the longest x2 10.4 us: relax_rows(): jnp.einsum('rmab,rqmbc->rqac', row_full, chosen, precision=HIGHEST)]
    pallas_call x0 -> x3, Pallas kernels: none -> 22.3 us  [the longest x1 10.5 us: on_device(): call(lift_kernel, [SMEM] * 6 + [VMEM] * 4, (jax.ShapeDtypeStruct(four, F3...]
    dot_general x2 -> x0, other arithmetic: 15.2 us -> none  [relax_rows(): jnp.einsum('rqmn,rmnab->rqmab', matched.astype(jnp.float32), further, pre...]
    concatenate x7 -> x0, other arithmetic: 14.1 us -> none  [the longest x2 9.37 us: on_device(): ext_full = jnp.concatenate([prior_full, full_rows], axis=0)]
  transfers between devices with their start and end apart: 7 -> 19, of which waited for: 4 -> 10; matrix products, arithmetic and copies ran while one was open for 2% -> 1% of each run, Pallas kernels for 0% -> 2%
where the time goes in v1:
time: 123 us; the launch traced here: 121 us
  starting transfers between devices  65.9 us (54%)
  waiting for transfers between devices  27.9 us (23%)
  Pallas kernels  22.3 us (18%)
  other arithmetic  2.81 us (2%)
  local copies, waits for them, and re-layouts  1.67 us (1%)
    ppermute x17, starting transfers between devices, along(): return lax.ppermute(block, axis, pairs)  64.4 us
    ppermute x17, waiting for transfers between devices, along(): return lax.ppermute(block, axis, pairs)  27.9 us
    pallas_call x1, Pallas kernels, on_device(): call(lift_kernel, [SMEM] * 6 + [VMEM] * 4, (jax.ShapeDtypeStruct(four, F3...  10.5 us
    pallas_call x1, Pallas kernels, on_device(): call(sweep_kernel, [SMEM] * 2 + [VMEM] + [ANY] * 12, jax.ShapeDtypeStruct...  9.47 us
  transfers between devices with their start and end apart: 19, of which 10 were waited for; matrix products, arithmetic and copies ran while one was open for 1% of the time, Pallas kernels for 2%

profile of v1, /device:TPU:6, one launch (start us, length us, event | category | flops | bytes accessed | tf_op | source)
XLA Modules:
  0.0 121.5 jit_solution(16001943511586168772)
XLA Ops:
  0.6 1.9 %collective-permute-start.2 = (bf16[16,192,192]{2,1,0:T(8,128)(2,1)}, bf16[16,192,192]{2,1,0:T(8,128)(2,1)S(1)}, u32[]{:S(2)}, u32[]{:S(2)}) collective-permute-start(bf16[16,192,192]{2,1,0:T(8,128)(2,1)} %own.1), channel_id=1, source_target_pairs={{0,4},{4,8},{8,12},{12,16},{16,20},{20,24},{24,28},{28,32},{32,36}... | collective-permute-start | bytes 3538952 | tf_op jit(solution)/shard_map/ppermute | solution.py:243
  2.6 7.5 %collective-permute-start.3 = (bf16[16,192,192]{2,1,0:T(8,128)(2,1)}, bf16[16,192,192]{2,1,0:T(8,128)(2,1)S(1)}, u32[]{:S(2)}, u32[]{:S(2)}) collective-permute-start(bf16[16,192,192]{2,1,0:T(8,128)(2,1)} %own.1), channel_id=1, source_target_pairs={{4,0},{8,4},{12,8},{16,12},{20,16},{24,20},{28,24},{32,28},{36,32}... | collective-permute-start | bytes 3538952 | tf_op jit(solution)/shard_map/ppermute | solution.py:243
  10.0 1.9 %collective-permute-start = (s32[16]{0:T(128)}, s32[16]{0:T(128)S(1)}, u32[]{:S(2)}, u32[]{:S(2)}) collective-permute-start(s32[16]{0:T(128)} %labels.1), channel_id=1, source_target_pairs={{0,4},{4,8},{8,12},{12,16},{16,20},{20,24},{24,28},{28,32},{32,36}... | collective-permute-start | bytes 200 | tf_op jit(solution)/shard_map/ppermute | solution.py:243
  12.0 5.8 %collective-permute-start.1 = (s32[16]{0:T(128)}, s32[16]{0:T(128)S(1)}, u32[]{:S(2)}, u32[]{:S(2)}) collective-permute-start(s32[16]{0:T(128)} %labels.1), channel_id=1, source_target_pairs={{4,0},{8,4},{12,8},{16,12},{20,16},{24,20},{28,24},{32,28},{36,32}... | collective-permute-start | bytes 200 | tf_op jit(solution)/shard_map/ppermute | solution.py:243
  17.7 0.7 pad_add_fusion.ids
  18.4 8.1 %collective-permute-done.left_labels = s32[16]{0:T(128)S(1)} collective-permute-done((s32[16]{0:T(128)}, s32[16]{0:T(128)S(1)}, u32[]{:S(2)}, u32[]{:S(2)}) %collective-permute-start) | collective-permute-done | bytes 96 | tf_op jit(solution)/shard_map/ppermute | solution.py:243
  26.5 1.8 %collective-permute-done.1.right_labels = s32[16]{0:T(128)S(1)} collective-permute-done((s32[16]{0:T(128)}, s32[16]{0:T(128)S(1)}, u32[]{:S(2)}, u32[]{:S(2)}) %collective-permute-start.1) | collective-permute-done | bytes 96 | tf_op jit(solution)/shard_map/ppermute | solution.py:243
  28.8 0.7 copy-done
  29.9 10.5 %lift.1 = (f32[4,192,192]{2,1,0:T(8,128)}, bf16[4,192,192]{2,1,0:T(8,128)(2,1)}, bf16[4,192,192]{2,1,0:T(8,128)(2,1)}) custom-call(s32[2]{0:T(128)} %pad_add_fusion.ids, s32[16]{0:T(128)} %bitcast.13, s32[16]{0:T(128)} %labels.1, s32[16]{0:T(128)} %copy-done.15, s32[16]{0:T(128)} %copy-done.16, s32[4,4]{1,0:T(4,128)} %pattern.3, ...), custom_call_target="tpu_custom_call" | custom-call | tf_op jit(solution)/shard_map/lift/pallas_call | solution.py:266
  40.4 0.8 collective-permute-start.4
  41.2 0.7 collective-permute-start.5
  41.9 2.1 %fusion = (bf16[4,192,192]{2,1,0:T(8,128)(2,1)S(1)}, f32[4,192,192]{2,1,0:T(8,128)}) fusion(bf16[4,192,192]{2,1,0:T(8,128)(2,1)S(1)} %collective-permute-done.5, f32[4,192,192]{2,1,0:T(8,128)} %get-tuple-element.5, bf16[4,192,192]{2,1,0:T(8,128)(2,1)S(1)} %collective-permute-done.4), kind=kLoop, calls=%fused_computation.2 | loop fusion | flops 737280 | bytes 2064384 | tf_op jit(solution)/shard_map/convert_element_type | solution.py:297
  44.1 22.2 %collective-permute-start.17 = (bf16[4,192,192]{2,1,0:T(8,128)(2,1)S(1)}, bf16[4,192,192]{2,1,0:T(8,128)(2,1)S(1)}, u32[]{:S(2)}, u32[]{:S(2)}) collective-permute-start(bf16[4,192,192]{2,1,0:T(8,128)(2,1)S(1)} %get-tuple-element.10.refs_8_), channel_id=1, source_target_pairs={{0,2},{1,3},{2,0},{3,1},{4,6},{5,7},{6,4},{7,5},{8,10},{9,11},{10,... | collective-permute-start | bytes 884744 | tf_op jit(solution)/shard_map/ppermute | solution.py:243
  66.3 1.9 %collective-permute-start.6 = (s32[4,4]{1,0:T(4,128)S(1)}, s32[4,4]{1,0:T(4,128)S(1)}, u32[]{:S(2)}, u32[]{:S(2)}) collective-permute-start(s32[4,4]{1,0:T(4,128)S(1)} %copy-done.12), channel_id=1, source_target_pairs={{0,4},{4,8},{8,12},{12,16},{16,20},{20,24},{24,28},{28,32},{32,36}... | collective-permute-start | bytes 200 | tf_op jit(solution)/shard_map/ppermute | solution.py:243
  68.2 2.1 %collective-permute-start.15 = (bf16[4,192,192]{2,1,0:T(8,128)(2,1)S(1)}, bf16[4,192,192]{2,1,0:T(8,128)(2,1)S(1)}, u32[]{:S(2)}, u32[]{:S(2)}) collective-permute-start(bf16[4,192,192]{2,1,0:T(8,128)(2,1)S(1)} %get-tuple-element.10.refs_8_), channel_id=1, source_target_pairs={{0,3},{1,0},{2,1},{3,2},{4,7},{5,4},{6,5},{7,6},{8,11},{9,8},{10,9... | collective-permute-start | bytes 884744 | tf_op jit(solution)/shard_map/ppermute | solution.py:243
  70.3 2.5 %collective-permute-start.7 = (s32[4,4]{1,0:T(4,128)S(1)}, s32[4,4]{1,0:T(4,128)S(1)}, u32[]{:S(2)}, u32[]{:S(2)}) collective-permute-start(s32[4,4]{1,0:T(4,128)S(1)} %copy-done.12), channel_id=1, source_target_pairs={{0,8},{4,12},{8,16},{12,20},{16,24},{20,28},{24,32},{28,36},{32,40... | collective-permute-start | bytes 200 | tf_op jit(solution)/shard_map/ppermute | solution.py:243
  73.5 3.3 %collective-permute-start.8 = (bf16[4,192,192]{2,1,0:T(8,128)(2,1)S(1)}, bf16[4,192,192]{2,1,0:T(8,128)(2,1)S(1)}, u32[]{:S(2)}, u32[]{:S(2)}) collective-permute-start(bf16[4,192,192]{2,1,0:T(8,128)(2,1)S(1)} %get-tuple-element.10.refs_8_), channel_id=1, source_target_pairs={{0,8},{4,12},{8,16},{12,20},{16,24},{20,28},{24,32},{28,36},{32,40... | collective-permute-start | bytes 884744 | tf_op jit(solution)/shard_map/ppermute | solution.py:243
  76.8 1.8 %collective-permute-done.7.far = s32[4,4]{1,0:T(4,128)S(1)} collective-permute-done((s32[4,4]{1,0:T(4,128)S(1)}, s32[4,4]{1,0:T(4,128)S(1)}, u32[]{:S(2)}, u32[]{:S(2)}) %collective-permute-start.7) | collective-permute-done | bytes 96 | tf_op jit(solution)/shard_map/ppermute | solution.py:243
  78.6 1.9 %collective-permute-start.12 = (bf16[4,192,192]{2,1,0:T(8,128)(2,1)S(1)}, bf16[4,192,192]{2,1,0:T(8,128)(2,1)S(1)}, u32[]{:S(2)}, u32[]{:S(2)}) collective-permute-start(bf16[4,192,192]{2,1,0:T(8,128)(2,1)S(1)} %get-tuple-element.10.refs_8_), channel_id=1, source_target_pairs={{0,4},{4,8},{8,12},{12,16},{16,20},{20,24},{24,28},{28,32},{32,36}... | collective-permute-start | bytes 884744 | tf_op jit(solution)/shard_map/ppermute | solution.py:243
  80.5 1.9 %collective-permute-start.18 = (bf16[4,192,192]{2,1,0:T(8,128)(2,1)S(1)}, bf16[4,192,192]{2,1,0:T(8,128)(2,1)S(1)}, u32[]{:S(2)}, u32[]{:S(2)}) collective-permute-start(bf16[4,192,192]{2,1,0:T(8,128)(2,1)S(1)} %collective-permute-done.17.refs_11_), channel_id=1, source_target_pairs={{0,4},{4,8},{8,12},{12,16},{16,20},{20,24},{24,28},{28,32},{32,36}... | collective-permute-start | bytes 884744 | tf_op jit(solution)/shard_map/ppermute | solution.py:243
  82.4 0.9 collective-permute-done.15.refs_10_
  83.4 4.0 %collective-permute-start.16 = (bf16[4,192,192]{2,1,0:T(8,128)(2,1)S(1)}, bf16[4,192,192]{2,1,0:T(8,128)(2,1)S(1)}, u32[]{:S(2)}, u32[]{:S(2)}) collective-permute-start(bf16[4,192,192]{2,1,0:T(8,128)(2,1)S(1)} %collective-permute-done.15.refs_10_), channel_id=1, source_target_pairs={{0,4},{4,8},{8,12},{12,16},{16,20},{20,24},{24,28},{28,32},{32,36}... | collective-permute-start | bytes 884744 | tf_op jit(solution)/shard_map/ppermute | solution.py:243
  87.4 2.8 %collective-permute-start.14 = (bf16[4,192,192]{2,1,0:T(8,128)(2,1)S(1)}, bf16[4,192,192]{2,1,0:T(8,128)(2,1)S(1)}, u32[]{:S(2)}, u32[]{:S(2)}) collective-permute-start(bf16[4,192,192]{2,1,0:T(8,128)(2,1)S(1)} %collective-permute-done.13.refs_9_), channel_id=1, source_target_pairs={{0,4},{4,8},{8,12},{12,16},{16,20},{20,24},{24,28},{28,32},{32,36}... | collective-permute-start | bytes 884744 | tf_op jit(solution)/shard_map/ppermute | solution.py:243
  90.2 1.8 %collective-permute-start.11 = (bf16[4,192,192]{2,1,0:T(8,128)(2,1)S(1)}, bf16[4,192,192]{2,1,0:T(8,128)(2,1)S(1)}, u32[]{:S(2)}, u32[]{:S(2)}) collective-permute-start(bf16[4,192,192]{2,1,0:T(8,128)(2,1)S(1)} %collective-permute-done.8.refs_0_), channel_id=1, source_target_pairs={{0,2},{1,3},{2,0},{3,1},{4,6},{5,7},{6,4},{7,5},{8,10},{9,11},{10,... | collective-permute-start | bytes 884744 | tf_op jit(solution)/shard_map/ppermute | solution.py:243
  92.0 1.6 %collective-permute-done.12.refs_4_ = bf16[4,192,192]{2,1,0:T(8,128)(2,1)S(1)} collective-permute-done((bf16[4,192,192]{2,1,0:T(8,128)(2,1)S(1)}, bf16[4,192,192]{2,1,0:T(8,128)(2,1)S(1)}, u32[]{:S(2)}, u32[]{:S(2)}) %collective-permute-start.12) | collective-permute-done | bytes 294944 | tf_op jit(solution)/shard_map/ppermute | solution.py:243
  93.6 2.8 %collective-permute-start.10 = (bf16[4,192,192]{2,1,0:T(8,128)(2,1)S(1)}, bf16[4,192,192]{2,1,0:T(8,128)(2,1)}, u32[]{:S(2)}, u32[]{:S(2)}) collective-permute-start(bf16[4,192,192]{2,1,0:T(8,128)(2,1)S(1)} %collective-permute-done.8.refs_0_), channel_id=1, source_target_pairs={{0,3},{1,0},{2,1},{3,2},{4,7},{5,4},{6,5},{7,6},{8,11},{9,8},{10,9... | collective-permute-start | bytes 884744 | tf_op jit(solution)/shard_map/ppermute | solution.py:243
  96.4 1.4 %collective-permute-done.18.refs_7_ = bf16[4,192,192]{2,1,0:T(8,128)(2,1)S(1)} collective-permute-done((bf16[4,192,192]{2,1,0:T(8,128)(2,1)S(1)}, bf16[4,192,192]{2,1,0:T(8,128)(2,1)S(1)}, u32[]{:S(2)}, u32[]{:S(2)}) %collective-permute-start.18) | collective-permute-done | bytes 294944 | tf_op jit(solution)/shard_map/ppermute | solution.py:243
  97.9 2.4 %plan.1 = s32[256]{0:T(256)} custom-call(s32[2]{0:T(128)} %pad_add_fusion.ids, s32[4,4]{1,0:T(4,128)} %pattern.3, s32[4,4]{1,0:T(4,128)} %copy-done.13, s32[4,4]{1,0:T(4,128)} %copy-done.14), custom_call_target="tpu_custom_call" | custom-call | tf_op jit(solution)/shard_map/plan/pallas_call | solution.py:285
  100.3 1.8 %collective-permute-done.16.refs_6_ = bf16[4,192,192]{2,1,0:T(8,128)(2,1)S(1)} collective-permute-done((bf16[4,192,192]{2,1,0:T(8,128)(2,1)S(1)}, bf16[4,192,192]{2,1,0:T(8,128)(2,1)S(1)}, u32[]{:S(2)}, u32[]{:S(2)}) %collective-permute-start.16) | collective-permute-done | bytes 294944 | tf_op jit(solution)/shard_map/ppermute | solution.py:243
  102.1 4.2 %collective-permute-done.14.refs_5_ = bf16[4,192,192]{2,1,0:T(8,128)(2,1)S(1)} collective-permute-done((bf16[4,192,192]{2,1,0:T(8,128)(2,1)S(1)}, bf16[4,192,192]{2,1,0:T(8,128)(2,1)S(1)}, u32[]{:S(2)}, u32[]{:S(2)}) %collective-permute-start.14) | collective-permute-done | bytes 294944 | tf_op jit(solution)/shard_map/ppermute | solution.py:243
  106.3 5.7 %collective-permute-done.10.refs_2_ = bf16[4,192,192]{2,1,0:T(8,128)(2,1)} collective-permute-done((bf16[4,192,192]{2,1,0:T(8,128)(2,1)S(1)}, bf16[4,192,192]{2,1,0:T(8,128)(2,1)}, u32[]{:S(2)}, u32[]{:S(2)}) %collective-permute-start.10) | collective-permute-done | bytes 294944 | tf_op jit(solution)/shard_map/ppermute | solution.py:243
  112.0 9.5 %sweep.1 = f32[4,192,192]{2,1,0:T(8,128)} custom-call(s32[2]{0:T(128)} %pad_add_fusion.ids, s32[256]{0:T(256)} %plan.1, f32[4,192,192]{2,1,0:T(8,128)} %get-tuple-element.11.coarse, bf16[4,192,192]{2,1,0:T(8,128)(2,1)} %copy-done.6, bf16[4,192,192]{2,1,0:T(8,128)(2,1)} %collective-permute-done.9.refs_1_, ...), custom_call_target="tpu_custom_call" | custom-call | tf_op jit(solution)/shard_map/sweep/pallas_call | solution.py:306
  (45 shorter events, 1.7 us)
Async XLA Ops:
  0.6 27.6 %collective-permute-start.2 = (bf16[16,192,192]{2,1,0:T(8,128)(2,1)}, bf16[16,192,192]{2,1,0:T(8,128)(2,1)S(1)}, u32[]{:S(2)}, u32[]{:S(2)}) collective-permute-start(bf16[16,192,192]{2,1,0:T(8,128)(2,1)} %own.1), channel_id=1, source_target_pairs={{0,4},{4,8},{8,12},{12,16},{16,20},{20,24},{24,28},{28,32},{32,36}... | collective-permute-start | bytes 3538952 | tf_op jit(solution)/shard_map/ppermute | solution.py:243
  2.6 25.7 %collective-permute-start.3 = (bf16[16,192,192]{2,1,0:T(8,128)(2,1)}, bf16[16,192,192]{2,1,0:T(8,128)(2,1)S(1)}, u32[]{:S(2)}, u32[]{:S(2)}) collective-permute-start(bf16[16,192,192]{2,1,0:T(8,128)(2,1)} %own.1), channel_id=1, source_target_pairs={{4,0},{8,4},{12,8},{16,12},{20,16},{24,20},{28,24},{32,28},{36,32}... | collective-permute-start | bytes 3538952 | tf_op jit(solution)/shard_map/ppermute | solution.py:243
  10.0 16.5 %collective-permute-start = (s32[16]{0:T(128)}, s32[16]{0:T(128)S(1)}, u32[]{:S(2)}, u32[]{:S(2)}) collective-permute-start(s32[16]{0:T(128)} %labels.1), channel_id=1, source_target_pairs={{0,4},{4,8},{8,12},{12,16},{16,20},{20,24},{24,28},{28,32},{32,36}... | collective-permute-start | bytes 200 | tf_op jit(solution)/shard_map/ppermute | solution.py:243
  12.0 16.3 %collective-permute-start.1 = (s32[16]{0:T(128)}, s32[16]{0:T(128)S(1)}, u32[]{:S(2)}, u32[]{:S(2)}) collective-permute-start(s32[16]{0:T(128)} %labels.1), channel_id=1, source_target_pairs={{4,0},{8,4},{12,8},{16,12},{20,16},{24,20},{28,24},{32,28},{36,32}... | collective-permute-start | bytes 200 | tf_op jit(solution)/shard_map/ppermute | solution.py:243
  40.4 25.9 %copy-start.12 = (s32[4,4]{1,0:T(4,128)S(1)}, s32[4,4]{1,0:T(4,128)}, u32[]{:S(2)}) copy-start(s32[4,4]{1,0:T(4,128)} %pattern.3) | copy-start | bytes 196
  40.4 1.5 %collective-permute-start.4 = (bf16[4,192,192]{2,1,0:T(8,128)(2,1)}, bf16[4,192,192]{2,1,0:T(8,128)(2,1)S(1)}, u32[]{:S(2)}, u32[]{:S(2)}) collective-permute-start(bf16[4,192,192]{2,1,0:T(8,128)(2,1)} %get-tuple-element.6), channel_id=1, source_target_pairs={{1,2},{2,3},{3,1},{5,6},{6,7},{7,5},{9,10},{10,11},{11,9},{13,14},... | collective-permute-start | bytes 884744 | tf_op jit(solution)/shard_map/ppermute | solution.py:294
  41.2 0.7 collective-permute-start.5
  44.1 67.9 %copy-start.2 = (bf16[4,192,192]{2,1,0:T(8,128)(2,1)}, bf16[4,192,192]{2,1,0:T(8,128)(2,1)S(1)}, u32[]{:S(2)}) copy-start(bf16[4,192,192]{2,1,0:T(8,128)(2,1)S(1)} %get-tuple-element.10.refs_8_) | copy-start | bytes 884740
  44.1 36.4 %collective-permute-start.17 = (bf16[4,192,192]{2,1,0:T(8,128)(2,1)S(1)}, bf16[4,192,192]{2,1,0:T(8,128)(2,1)S(1)}, u32[]{:S(2)}, u32[]{:S(2)}) collective-permute-start(bf16[4,192,192]{2,1,0:T(8,128)(2,1)S(1)} %get-tuple-element.10.refs_8_), channel_id=1, source_target_pairs={{0,2},{1,3},{2,0},{3,1},{4,6},{5,7},{6,4},{7,5},{8,10},{9,11},{10,... | collective-permute-start | bytes 884744 | tf_op jit(solution)/shard_map/ppermute | solution.py:243
  66.3 7.2 %collective-permute-start.6 = (s32[4,4]{1,0:T(4,128)S(1)}, s32[4,4]{1,0:T(4,128)S(1)}, u32[]{:S(2)}, u32[]{:S(2)}) collective-permute-start(s32[4,4]{1,0:T(4,128)S(1)} %copy-done.12), channel_id=1, source_target_pairs={{0,4},{4,8},{8,12},{12,16},{16,20},{20,24},{24,28},{28,32},{32,36}... | collective-permute-start | bytes 200 | tf_op jit(solution)/shard_map/ppermute | solution.py:243
  68.2 15.2 %collective-permute-start.15 = (bf16[4,192,192]{2,1,0:T(8,128)(2,1)S(1)}, bf16[4,192,192]{2,1,0:T(8,128)(2,1)S(1)}, u32[]{:S(2)}, u32[]{:S(2)}) collective-permute-start(bf16[4,192,192]{2,1,0:T(8,128)(2,1)S(1)} %get-tuple-element.10.refs_8_), channel_id=1, source_target_pairs={{0,3},{1,0},{2,1},{3,2},{4,7},{5,4},{6,5},{7,6},{8,11},{9,8},{10,9... | collective-permute-start | bytes 884744 | tf_op jit(solution)/shard_map/ppermute | solution.py:243
  70.3 8.3 %collective-permute-start.7 = (s32[4,4]{1,0:T(4,128)S(1)}, s32[4,4]{1,0:T(4,128)S(1)}, u32[]{:S(2)}, u32[]{:S(2)}) collective-permute-start(s32[4,4]{1,0:T(4,128)S(1)} %copy-done.12), channel_id=1, source_target_pairs={{0,8},{4,12},{8,16},{12,20},{16,24},{20,28},{24,32},{28,36},{32,40... | collective-permute-start | bytes 200 | tf_op jit(solution)/shard_map/ppermute | solution.py:243
  72.8 14.6 %collective-permute-start.13 = (bf16[4,192,192]{2,1,0:T(8,128)(2,1)S(1)}, bf16[4,192,192]{2,1,0:T(8,128)(2,1)S(1)}, u32[]{:S(2)}, u32[]{:S(2)}) collective-permute-start(bf16[4,192,192]{2,1,0:T(8,128)(2,1)S(1)} %get-tuple-element.10.refs_8_), channel_id=1, source_target_pairs={{0,1},{1,2},{2,3},{3,0},{4,5},{5,6},{6,7},{7,4},{8,9},{9,10},{10,1... | collective-permute-start | bytes 884744 | tf_op jit(solution)/shard_map/ppermute | solution.py:243
  73.5 24.4 %copy-start.13 = (s32[4,4]{1,0:T(4,128)}, s32[4,4]{1,0:T(4,128)S(1)}, u32[]{:S(2)}) copy-start(s32[4,4]{1,0:T(4,128)S(1)} %collective-permute-done.6.near) | copy-start | bytes 196
  73.5 16.7 %collective-permute-start.8 = (bf16[4,192,192]{2,1,0:T(8,128)(2,1)S(1)}, bf16[4,192,192]{2,1,0:T(8,128)(2,1)S(1)}, u32[]{:S(2)}, u32[]{:S(2)}) collective-permute-start(bf16[4,192,192]{2,1,0:T(8,128)(2,1)S(1)} %get-tuple-element.10.refs_8_), channel_id=1, source_target_pairs={{0,8},{4,12},{8,16},{12,20},{16,24},{20,28},{24,32},{28,36},{32,40... | collective-permute-start | bytes 884744 | tf_op jit(solution)/shard_map/ppermute | solution.py:243
  78.6 19.3 %copy-start.14 = (s32[4,4]{1,0:T(4,128)}, s32[4,4]{1,0:T(4,128)S(1)}, u32[]{:S(2)}) copy-start(s32[4,4]{1,0:T(4,128)S(1)} %collective-permute-done.7.far) | copy-start | bytes 196
  78.6 15.0 %collective-permute-start.12 = (bf16[4,192,192]{2,1,0:T(8,128)(2,1)S(1)}, bf16[4,192,192]{2,1,0:T(8,128)(2,1)S(1)}, u32[]{:S(2)}, u32[]{:S(2)}) collective-permute-start(bf16[4,192,192]{2,1,0:T(8,128)(2,1)S(1)} %get-tuple-element.10.refs_8_), channel_id=1, source_target_pairs={{0,4},{4,8},{8,12},{12,16},{16,20},{20,24},{24,28},{28,32},{32,36}... | collective-permute-start | bytes 884744 | tf_op jit(solution)/shard_map/ppermute | solution.py:243
  80.5 31.4 %copy-start.3 = (bf16[4,192,192]{2,1,0:T(8,128)(2,1)}, bf16[4,192,192]{2,1,0:T(8,128)(2,1)S(1)}, u32[]{:S(2)}) copy-start(bf16[4,192,192]{2,1,0:T(8,128)(2,1)S(1)} %collective-permute-done.17.refs_11_) | copy-start | bytes 884740
  80.5 17.3 %collective-permute-start.18 = (bf16[4,192,192]{2,1,0:T(8,128)(2,1)S(1)}, bf16[4,192,192]{2,1,0:T(8,128)(2,1)S(1)}, u32[]{:S(2)}, u32[]{:S(2)}) collective-permute-start(bf16[4,192,192]{2,1,0:T(8,128)(2,1)S(1)} %collective-permute-done.17.refs_11_), channel_id=1, source_target_pairs={{0,4},{4,8},{8,12},{12,16},{16,20},{20,24},{24,28},{28,32},{32,36}... | collective-permute-start | bytes 884744 | tf_op jit(solution)/shard_map/ppermute | solution.py:243
  83.4 28.6 %copy-start.4 = (bf16[4,192,192]{2,1,0:T(8,128)(2,1)}, bf16[4,192,192]{2,1,0:T(8,128)(2,1)S(1)}, u32[]{:S(2)}) copy-start(bf16[4,192,192]{2,1,0:T(8,128)(2,1)S(1)} %collective-permute-done.15.refs_10_) | copy-start | bytes 884740
  83.4 18.7 %collective-permute-start.16 = (bf16[4,192,192]{2,1,0:T(8,128)(2,1)S(1)}, bf16[4,192,192]{2,1,0:T(8,128)(2,1)S(1)}, u32[]{:S(2)}, u32[]{:S(2)}) collective-permute-start(bf16[4,192,192]{2,1,0:T(8,128)(2,1)S(1)} %collective-permute-done.15.refs_10_), channel_id=1, source_target_pairs={{0,4},{4,8},{8,12},{12,16},{16,20},{20,24},{24,28},{28,32},{32,36}... | collective-permute-start | bytes 884744 | tf_op jit(solution)/shard_map/ppermute | solution.py:243
  87.4 24.5 %copy-start.5 = (bf16[4,192,192]{2,1,0:T(8,128)(2,1)}, bf16[4,192,192]{2,1,0:T(8,128)(2,1)S(1)}, u32[]{:S(2)}) copy-start(bf16[4,192,192]{2,1,0:T(8,128)(2,1)S(1)} %collective-permute-done.13.refs_9_) | copy-start | bytes 884740
  87.4 18.8 %collective-permute-start.14 = (bf16[4,192,192]{2,1,0:T(8,128)(2,1)S(1)}, bf16[4,192,192]{2,1,0:T(8,128)(2,1)S(1)}, u32[]{:S(2)}, u32[]{:S(2)}) collective-permute-start(bf16[4,192,192]{2,1,0:T(8,128)(2,1)S(1)} %collective-permute-done.13.refs_9_), channel_id=1, source_target_pairs={{0,4},{4,8},{8,12},{12,16},{16,20},{20,24},{24,28},{28,32},{32,36}... | collective-permute-start | bytes 884744 | tf_op jit(solution)/shard_map/ppermute | solution.py:243
  90.2 21.8 %copy-start.6 = (bf16[4,192,192]{2,1,0:T(8,128)(2,1)}, bf16[4,192,192]{2,1,0:T(8,128)(2,1)S(1)}, u32[]{:S(2)}) copy-start(bf16[4,192,192]{2,1,0:T(8,128)(2,1)S(1)} %collective-permute-done.8.refs_0_) | copy-start | bytes 884740
  90.2 16.1 %collective-permute-start.11 = (bf16[4,192,192]{2,1,0:T(8,128)(2,1)S(1)}, bf16[4,192,192]{2,1,0:T(8,128)(2,1)S(1)}, u32[]{:S(2)}, u32[]{:S(2)}) collective-permute-start(bf16[4,192,192]{2,1,0:T(8,128)(2,1)S(1)} %collective-permute-done.8.refs_0_), channel_id=1, source_target_pairs={{0,2},{1,3},{2,0},{3,1},{4,6},{5,7},{6,4},{7,5},{8,10},{9,11},{10,... | collective-permute-start | bytes 884744 | tf_op jit(solution)/shard_map/ppermute | solution.py:243
  93.6 18.3 %copy-start.7 = (bf16[4,192,192]{2,1,0:T(8,128)(2,1)}, bf16[4,192,192]{2,1,0:T(8,128)(2,1)S(1)}, u32[]{:S(2)}) copy-start(bf16[4,192,192]{2,1,0:T(8,128)(2,1)S(1)} %collective-permute-done.12.refs_4_) | copy-start | bytes 884740
  93.6 18.3 %collective-permute-start.10 = (bf16[4,192,192]{2,1,0:T(8,128)(2,1)S(1)}, bf16[4,192,192]{2,1,0:T(8,128)(2,1)}, u32[]{:S(2)}, u32[]{:S(2)}) collective-permute-start(bf16[4,192,192]{2,1,0:T(8,128)(2,1)S(1)} %collective-permute-done.8.refs_0_), channel_id=1, source_target_pairs={{0,3},{1,0},{2,1},{3,2},{4,7},{5,4},{6,5},{7,6},{8,11},{9,8},{10,9... | collective-permute-start | bytes 884744 | tf_op jit(solution)/shard_map/ppermute | solution.py:243
  97.8 14.1 %copy-start.8 = (bf16[4,192,192]{2,1,0:T(8,128)(2,1)}, bf16[4,192,192]{2,1,0:T(8,128)(2,1)S(1)}, u32[]{:S(2)}) copy-start(bf16[4,192,192]{2,1,0:T(8,128)(2,1)S(1)} %collective-permute-done.18.refs_7_) | copy-start | bytes 884740
  97.8 14.1 %collective-permute-start.9 = (bf16[4,192,192]{2,1,0:T(8,128)(2,1)S(1)}, bf16[4,192,192]{2,1,0:T(8,128)(2,1)}, u32[]{:S(2)}, u32[]{:S(2)}) collective-permute-start(bf16[4,192,192]{2,1,0:T(8,128)(2,1)S(1)} %collective-permute-done.8.refs_0_), channel_id=1, source_target_pairs={{0,1},{1,2},{2,3},{3,0},{4,5},{5,6},{6,7},{7,4},{8,9},{9,10},{10,1... | collective-permute-start | bytes 884744 | tf_op jit(solution)/shard_map/ppermute | solution.py:243
  102.0 9.9 %copy-start.9 = (bf16[4,192,192]{2,1,0:T(8,128)(2,1)}, bf16[4,192,192]{2,1,0:T(8,128)(2,1)S(1)}, u32[]{:S(2)}) copy-start(bf16[4,192,192]{2,1,0:T(8,128)(2,1)S(1)} %collective-permute-done.16.refs_6_) | copy-start | bytes 884740
  106.3 5.7 %copy-start.10 = (bf16[4,192,192]{2,1,0:T(8,128)(2,1)}, bf16[4,192,192]{2,1,0:T(8,128)(2,1)S(1)}, u32[]{:S(2)}) copy-start(bf16[4,192,192]{2,1,0:T(8,128)(2,1)S(1)} %collective-permute-done.14.refs_5_) | copy-start | bytes 884740
  106.3 5.7 %copy-start.11 = (bf16[4,192,192]{2,1,0:T(8,128)(2,1)}, bf16[4,192,192]{2,1,0:T(8,128)(2,1)S(1)}, u32[]{:S(2)}) copy-start(bf16[4,192,192]{2,1,0:T(8,128)(2,1)S(1)} %collective-permute-done.11.refs_3_) | copy-start | bytes 884740
  (4 other events, 5.1 us)

commit v2 on v1

--- a/solution.py
+++ b/solution.py
@@ -18,67 +18,144 @@
 LIST2 = 160
 TILES = 192
 KINDS = 240
-PLAN = 256
+CLOSE = 256
+DISTANT = 288
+PLAN = 320
+STEP = 4
 ZERO1 = 64
-ZERO2 = 48
+SPARE = 16
 
 
 def iota(shape, dim):
     return lax.broadcasted_iota(jnp.int32, shape, dim)
 
 
-def lift_kernel(
-    ids, cols, labels, left_labels, right_labels, pattern, tiles, own, left, right, mine, ahead, behind, total, remote
-):
-    agg, col = ids[0], ids[1]
+def packed_shape(width):
+    return (width * width // 128, 128)
+
+
+def store_packed(ref, tile):
+    width, half = tile.shape[0], tile.shape[0] // 2
+    ref[:width] = tile[:, :128]
+    ref[width:] = jnp.concatenate([tile[:half, 128:], tile[half:, 128:]], axis=1)
+
+
+def store_unpacked(ref, packed, width):
+    half, rest = width // 2, width - 128
+    ref[:, :128] = packed[:width]
+    ref[:half, 128:] = packed[width:, :rest]
+    ref[half:, 128:] = packed[width:, rest:]
+
+
+def pack_kernel(tiles, packed):
+    for i in range(tiles.shape[0]):
+        store_packed(packed.at[i], tiles[i])
+
+
+def entries_of(plan, start, k):
+    return [plan[start + STEP * k + u] for u in range(STEP)]
+
+
+def add_lifted(entries, tiles, turned, remote, total):
+    carried = [
+        jnp.dot(tiles[e & 255], remote(u, (e >> 8) & 255), preferred_element_type=F32).astype(BF16)
+        for u, e in enumerate(entries)
+    ]
+    lifted = [
+        jnp.dot(turned[e & 255], c, preferred_element_type=F32) for e, c in zip(entries, carried)
+    ]
+    for e, tile in zip(entries, lifted):
+        total[e >> 16] += tile
+
+
+def close_kernel(plan, tiles, own, total, turned):
     total[...] = jnp.zeros_like(total)
 
-    def step(i, carry):
-        place = cols[i] - (agg - 1) * 16
-        within = place & 15
-        side = place >> 4
-        target = jnp.where(side == 0, left_labels[within], jnp.where(side == 1, labels[within], right_labels[within]))
-        row = labels[i] - agg * 4
-        slot = jnp.int32(0)
-        for q in range(1, 4):
-            slot = jnp.where(pattern[row, q] == target, q, slot)
-
-        @pl.when(side == 0)
-        def _():
-            remote[...] = left[within]
-
-        @pl.when(side == 1)
-        def _():
-            remote[...] = own[within]
-
-        @pl.when(side == 2)
-        def _():
-            remote[...] = right[within]
-
-        carried = jnp.dot(tiles[i], remote[...], preferred_element_type=F32).astype(BF16)
-        lifted = lax.dot_general(own[i], carried, (((0,), (0,)), ((), ())), preferred_element_type=F32)
-        total[slot, row] += lifted
-        return carry
-
-    lax.fori_loop(0, 16, step, 0)
+    def turn(i, carry):
+        turned[i] = own[i].T
+        return carry
+
+    lax.fori_loop(0, 16, turn, 0)
+
+    def step(k, carry):
+        add_lifted(entries_of(plan, CLOSE, k), tiles, turned, lambda u, place: own[place], total)
+        return carry
+
+    lax.fori_loop(0, (plan[3] + STEP - 1) // STEP, step, 0)
+
+
+def distant_kernel(ids, plan, tiles, turned, left, right, begun, mine, ahead, behind, total, remote):
+    col = ids[1]
+    total[...] = begun[...]
+    width = tiles.shape[-1]
+
+    def step(k, carry):
+        entries = entries_of(plan, DISTANT, k)
+        for u, e in enumerate(entries):
+            place = (e >> 8) & 255
+
+            @pl.when(place < 16)
+            def _():
+                store_unpacked(remote.at[u], left[place], width)
+
+            @pl.when(place >= 16)
+            def _():
+                store_unpacked(remote.at[u], right[place - 16], width)
+
+        add_lifted(entries, tiles, turned, lambda u, place: remote[u], total)
+        return carry
+
+    lax.fori_loop(0, (plan[4] + STEP - 1) // STEP, step, 0)
     first = jnp.where(col == 3, 1, col + 1)
     second = jnp.where(col <= 1, 3, col - 1)
     for r in range(4):
-        mine[r] = total[col, r]
-        ahead[r] = total[first, r].astype(BF16)
-        behind[r] = total[second, r].astype(BF16)
-
-
-def plan_kernel(ids, pattern, near, far, plan, pat, need):
+        mine[r] = total[col * 4 + r]
+        store_packed(ahead.at[r], total[first * 4 + r].astype(BF16))
+        store_packed(behind.at[r], total[second * 4 + r].astype(BF16))
+
+
+def combine_kernel(mine, ahead, behind, coarse, sent, wide):
+    width = mine.shape[-1]
+    for r in range(4):
+        store_unpacked(wide, ahead[r].astype(F32) + behind[r].astype(F32), width)
+        tile = mine[r] + wide[...]
+        coarse[r] = tile
+        store_packed(sent.at[r], tile.astype(BF16))
+
+
+def plan_kernel(ids, cols, labels, pattern, near, right_labels, far, plan, pat, need):
     agg, col = ids[0], ids[1]
     base = (agg - 2) * 4
     for r in range(4):
         for q in range(4):
             pat[4 * r + q] = far[r, q]
-            pat[16 + 4 * r + q] = near[r, q]
+            pat[16 + 4 * r + q] = near[16 + 4 * r + q]
             pat[32 + 4 * r + q] = pattern[r, q]
     for k in range(32):
         need[k] = 0
+
+    def fine(i, carry):
+        close, distant = carry
+        place = cols[i] - (agg - 1) * 16
+        within = place & 15
+        side = place >> 4
+        target = jnp.where(side == 0, near[within], jnp.where(side == 1, labels[within], right_labels[within]))
+        row = labels[i] - agg * 4
+        slot = jnp.int32(0)
+        for q in range(1, 4):
+            slot = jnp.where(pat[32 + 4 * row + q] == target, q, slot)
+        entry = i | ((slot * 4 + row) << 16)
+        plan[CLOSE + close] = entry | (within << 8)
+        plan[DISTANT + distant] = entry | ((within + jnp.where(side == 0, 0, 16)) << 8)
+        here = (side == 1).astype(jnp.int32)
+        return close + here, distant + 1 - here
+
+    close, distant = lax.fori_loop(0, 16, fine, (jnp.int32(0), jnp.int32(0)))
+    plan[3] = close
+    plan[4] = distant
+    for u in range(STEP - 1):
+        plan[CLOSE + close + u] = SPARE << 16
+        plan[DISTANT + distant + u] = SPARE << 16
 
     def through(row, index, target, m):
         inner = pat[4 * row + m]
@@ -146,19 +223,17 @@
     plan[0] = 0
     plan[2] = 0
     lax.fori_loop(0, 32, tile, 0)
-    plan[LIST1 + plan[0]] = ZERO1 | (ZERO1 << 8) | (32 << 16)
+    for u in range(STEP - 1):
+        plan[LIST1 + plan[0] + u] = ZERO1 | (ZERO1 << 8) | (32 << 16)
 
 
 def sweep_kernel(ids, plan, coarse, *refs):
-    pieces, (out, first, work, high, low, pivots, pivots_next, sems) = refs[:12], refs[12:]
+    pieces, (out, arrived, first, work, high, low, pivots, pivots_next, sems) = refs[:12], refs[12:]
     col = ids[1]
     width = coarse.shape[-1]
     copies = []
     for k, piece in enumerate(pieces):
-        block, shift = k // 4, (0, 3, 1, 2)[k % 4]
-        slot = (col + shift) & 3
-        start = slot * ROWS + block * 4
-        copies.append(pltpu.make_async_copy(piece, first.at[pl.ds(start, 4)], sems.at[k]))
+        copies.append(pltpu.make_async_copy(piece, arrived.at[pl.ds(4 * k, 4)], sems.at[k]))
         copies[-1].start()
     first[ZERO1] = jnp.zeros((width, width), BF16)
     lines, columns = iota((width, width), 0), iota((width, width), 1)
@@ -167,8 +242,11 @@
     def reciprocal(tile):
         return 1.0 / jnp.maximum(jnp.sum(jnp.where(equal, tile, 0.0), axis=0, keepdims=True), 1.0)
 
-    for copy in copies:
+    for k, copy in enumerate(copies):
         copy.wait()
+        start = ((col + (0, 3, 1, 2)[k % 4]) & 3) * ROWS + k // 4 * 4
+        for r in range(4):
+            store_unpacked(first.at[start + r], arrived[4 * k + r], width)
 
     def prepare(k, carry):
         diagonal = first[4 + k].astype(F32)
@@ -187,14 +265,13 @@
     lax.fori_loop(0, plan[2], begin, 0)
 
     def multiply(k, carry):
-        a, b = plan[LIST1 + 2 * k], plan[LIST1 + 2 * k + 1]
-        one = jnp.dot(first[a & 255], first[(a >> 8) & 255], preferred_element_type=F32)
-        two = jnp.dot(first[b & 255], first[(b >> 8) & 255], preferred_element_type=F32)
-        work[a >> 16] -= one
-        work[b >> 16] -= two
-        return carry
-
-    lax.fori_loop(0, (plan[0] + 1) >> 1, multiply, 0)
+        entries = entries_of(plan, LIST1, k)
+        products = [jnp.dot(first[e & 255], first[(e >> 8) & 255], preferred_element_type=F32) for e in entries]
+        for e, product in zip(entries, products):
+            work[e >> 16] -= product
+        return carry
+
+    lax.fori_loop(0, (plan[0] + STEP - 1) // STEP, multiply, 0)
 
     def scaled(tile, kind, row):
         factor = jnp.where((kind == 1) | ((kind == 2) & lower), row, 1.0)
@@ -237,21 +314,23 @@
         out[r] = scaled(out[r], entry & 255, pivots_next[entry >> 8])
 
 
-def along(block, axis, distance, ring=False):
+def along(block, axis, distance, ring=False, sources=None):
     count = lax.axis_size(axis)
     pairs = [(i, (i + distance) % count) for i in range(count) if ring or 0 <= i + distance < count]
-    return lax.ppermute(block, axis, pairs)
+    return lax.ppermute(block, axis, [pair for pair in pairs if sources is None or pair[0] in sources])
 
 
 def on_device(fine_tiles, fine_cols, agg_of, prolong, coarse_cols):
-    width = prolong.shape[-1]
+    rows, width = prolong.shape[0], prolong.shape[-1]
     agg, col = lax.axis_index("agg"), lax.axis_index("col")
     ids = jnp.stack([agg, col]).astype(jnp.int32)
-    left, right = along(prolong, "agg", 1), along(prolong, "agg", -1)
-    left_labels, right_labels = along(agg_of, "agg", 1), along(agg_of, "agg", -1)
-    near, far = along(coarse_cols, "agg", 1), along(coarse_cols, "agg", 2)
-
-    def call(kernel, ins, outs, out_specs, scratch, name):
+    packed = packed_shape(width)
+    four, four_packed = (4, width, width), (4, *packed)
+
+    def array(shape, dtype):
+        return jax.ShapeDtypeStruct(shape, dtype)
+
+    def call(kernel, ins, outs, out_specs, scratch, name, mebibytes):
         return pl.pallas_call(
             kernel,
             out_shape=outs,
@@ -259,56 +338,68 @@
             out_specs=out_specs,
             scratch_shapes=scratch,
             name=name,
-            compiler_params=pltpu.CompilerParams(vmem_limit_bytes=60 << 20),
+            compiler_params=pltpu.CompilerParams(vmem_limit_bytes=mebibytes << 20),
         )
 
-    four = (4, width, width)
-    mine, ahead, behind = call(
-        lift_kernel,
-        [SMEM] * 6 + [VMEM] * 4,
-        (jax.ShapeDtypeStruct(four, F32), jax.ShapeDtypeStruct(four, BF16), jax.ShapeDtypeStruct(four, BF16)),
-        (VMEM, VMEM, VMEM),
-        [pltpu.VMEM((4, *four), F32), pltpu.VMEM((width, width), BF16)],
-        "lift",
-    )(
-        ids,
-        fine_cols.reshape(-1),
-        agg_of,
-        left_labels,
-        right_labels,
-        coarse_cols,
-        fine_tiles.reshape(-1, width, width),
-        prolong,
-        left,
-        right,
-    )
+    about = jnp.concatenate([agg_of, coarse_cols.reshape(-1)])
+    near, far = along(about, "agg", 1), along(coarse_cols, "agg", 2)
+    right_labels = along(agg_of, "agg", -1)
+    halo = call(pack_kernel, [VMEM], array((rows, *packed), BF16), VMEM, [], "pack", 10)(prolong)
+    left, right = along(halo, "agg", 1), along(halo, "agg", -1)
+
     plan = call(
         plan_kernel,
-        [SMEM] * 4,
-        jax.ShapeDtypeStruct((PLAN,), jnp.int32),
+        [SMEM] * 7,
+        array((PLAN,), jnp.int32),
         SMEM,
         [pltpu.SMEM((48,), jnp.int32), pltpu.SMEM((32,), jnp.int32)],
         "plan",
-    )(ids, coarse_cols, near, far)
+        4,
+    )(ids, fine_cols.reshape(-1), agg_of, coarse_cols, near, right_labels, far)
+    tiles = fine_tiles.reshape(rows, width, width)
+    total, turned = call(
+        close_kernel,
+        [SMEM, VMEM, VMEM],
+        (array((SPARE + 1, width, width), F32), array((rows, width, width), BF16)),
+        (VMEM, VMEM),
+        [],
+        "close",
+        14,
+    )(plan, tiles, prolong)
+    mine, ahead, behind = call(
+        distant_kernel,
+        [SMEM] * 2 + [VMEM] * 5,
+        (array(four, F32), array(four_packed, BF16), array(four_packed, BF16)),
+        (VMEM,) * 3,
+        [pltpu.VMEM((SPARE + 1, width, width), F32), pltpu.VMEM((STEP, width, width), BF16)],
+        "distant",
+        22,
+    )(ids, plan, tiles, turned, left, right, total)
 
     came_ahead = lax.ppermute(ahead, "col", [(1, 2), (2, 3), (3, 1)])
     came_behind = lax.ppermute(behind, "col", [(1, 3), (2, 1), (3, 2)])
-    coarse = mine + came_ahead.astype(F32) + came_behind.astype(F32)
-    sent = coarse.astype(BF16)
-
-    def spread(x):
-        return [x, along(x, "col", 1, True), along(x, "col", -1, True), along(x, "col", 2, True)]
-
-    here = spread(sent)
-    far_sent = along(sent, "agg", 2)
+    coarse, sent = call(
+        combine_kernel,
+        [VMEM] * 3,
+        (array(four, F32), array(four_packed, BF16)),
+        (VMEM, VMEM),
+        [pltpu.VMEM((width, width), F32)],
+        "combine",
+        8,
+    )(mine, came_ahead, came_behind)
+
+    here = [sent] + [along(sent, "col", d, True) for d in (1, -1, 2)]
     before = [along(x, "agg", 1) for x in here]
-    further = spread(far_sent)
+    others = (1, 2, 3)
+    second = along(before[0], "agg", 1)
+    further = [second] + [along(second, "col", d, True, others) for d in (1, -1)] + [along(before[3], "agg", 1)]
     factor = call(
         sweep_kernel,
         [SMEM] * 2 + [VMEM] + [ANY] * 12,
-        jax.ShapeDtypeStruct(four, F32),
+        array(four, F32),
         VMEM,
         [
+            pltpu.VMEM((48, *packed), BF16),
             pltpu.VMEM((65, width, width), BF16),
             pltpu.VMEM((33, width, width), F32),
             pltpu.VMEM((49, width, width), BF16),
@@ -318,6 +409,7 @@
             pltpu.SemaphoreType.DMA((12,)),
         ],
         "sweep",
+        34,
     )(ids, plan, coarse, *further, *before, *here)
     return (coarse[:, None], factor[:, None])
 

time: 123 us -> 108 us (0.88)
  starting transfers between devices: 65.9 us -> 57.1 us
  Pallas kernels: 22.3 us -> 18.7 us
  other arithmetic: 2.81 us -> 0.15 us
  local copies, waits for them, and re-layouts: 1.67 us -> 4.04 us
  waiting for transfers between devices: 27.9 us -> 25.8 us
    ppermute x17 -> x16, starting transfers between devices: 64.4 us -> 55.7 us  [along(): lax.ppermute(block, axis, [pair for pair in pairs if sources is None or p...]
    pallas_call x3 -> x6, Pallas kernels: 22.3 us -> 18.7 us  [the longest x1 8.04 us: on_device(): call(sweep_kernel, [SMEM] * 2 + [VMEM] + [ANY] * 12, array(four, F32), VM...]
    unnamed x34 -> x14, local copies, waits for them, and re-layouts: 1.67 us -> 3.95 us
    convert_element_type x1 -> x0, other arithmetic: 2.15 us -> none  [on_device(): sent = coarse.astype(BF16)]
    ppermute x17 -> x16, waiting for transfers between devices: 27.9 us -> 25.8 us  [along(): lax.ppermute(block, axis, [pair for pair in pairs if sources is None or p...]
  transfers between devices with their start and end apart: 19 -> 18, of which waited for: 10 -> 13; matrix products, arithmetic and copies ran while one was open for 1% -> 0% of each run, Pallas kernels for 2% -> 6%
where the time goes in v2:
time: 108 us; the launch traced here: 107 us
  starting transfers between devices  57.1 us (53%)
  waiting for transfers between devices  25.8 us (24%)
  Pallas kernels  18.7 us (17%)
  local copies, waits for them, and re-layouts  4.04 us (4%)
    ppermute x16, starting transfers between devices, along(): lax.ppermute(block, axis, [pair for pair in pairs if sources is None or p...  55.7 us
    ppermute x16, waiting for transfers between devices, along(): lax.ppermute(block, axis, [pair for pair in pairs if sources is None or p...  25.8 us
    pallas_call x1, Pallas kernels, on_device(): call(sweep_kernel, [SMEM] * 2 + [VMEM] + [ANY] * 12, array(four, F32), VM...  8.04 us
    pallas_call x1, Pallas kernels, on_device(): call(close_kernel, [SMEM, VMEM, VMEM], (array((SPARE + 1, width, width),...  3.97 us
    unnamed x14, local copies, waits for them, and re-layouts  3.95 us
    pallas_call x1, Pallas kernels, on_device(): call(plan_kernel, [SMEM] * 7, array((PLAN,), jnp.int32), SMEM, [pltpu.SME...  2.6 us
  transfers between devices with their start and end apart: 18, of which 13 were waited for; matrix products, arithmetic and copies ran while one was open for 0% of the time, Pallas kernels for 6%

profile of v2, /device:TPU:6, one launch (start us, length us, event | category | flops | bytes accessed | tf_op | source)
XLA Modules:
  0.0 106.6 jit_solution(11412306019460931945)
XLA Ops:
  0.6 1.4 %copy-done.1 = bf16[16,192,192]{2,1,0:T(8,128)(2,1)S(1)} copy-done((bf16[16,192,192]{2,1,0:T(8,128)(2,1)S(1)}, bf16[16,192,192]{2,1,0:T(8,128)(2,1)}, u32[]{:S(2)}) %copy-start.1) | copy-done | bytes 1179672
  2.1 1.3 %pack.1 = bf16[16,288,128]{2,1,0:T(8,128)(2,1)} custom-call(bf16[16,192,192]{2,1,0:T(8,128)(2,1)S(1)} %copy-done.1), custom_call_target="tpu_custom_call" | custom-call | tf_op jit(solution)/shard_map/pack/pallas_call | solution.py:347
  3.4 7.5 %collective-permute-start.4 = (bf16[16,288,128]{2,1,0:T(8,128)(2,1)}, bf16[16,288,128]{2,1,0:T(8,128)(2,1)S(1)}, u32[]{:S(2)}, u32[]{:S(2)}) collective-permute-start(bf16[16,288,128]{2,1,0:T(8,128)(2,1)} %pack.1), channel_id=1, source_target_pairs={{4,0},{8,4},{12,8},{16,12},{20,16},{24,20},{28,24},{32,28},{36,32}... | collective-permute-start | bytes 3538952 | tf_op jit(solution)/shard_map/ppermute | solution.py:320
  10.8 1.9 %collective-permute-start.3 = (bf16[16,288,128]{2,1,0:T(8,128)(2,1)}, bf16[16,288,128]{2,1,0:T(8,128)(2,1)}, u32[]{:S(2)}, u32[]{:S(2)}) collective-permute-start(bf16[16,288,128]{2,1,0:T(8,128)(2,1)} %pack.1), channel_id=1, source_target_pairs={{0,4},{4,8},{8,12},{12,16},{16,20},{20,24},{24,28},{28,32},{32,36}... | collective-permute-start | bytes 3538952 | tf_op jit(solution)/shard_map/ppermute | solution.py:320
  12.8 5.8 %collective-permute-start.1 = (s32[16]{0:T(128)S(1)}, s32[16]{0:T(128)S(1)}, u32[]{:S(2)}, u32[]{:S(2)}) collective-permute-start(s32[16]{0:T(128)S(1)} %copy-done.6), channel_id=1, source_target_pairs={{4,0},{8,4},{12,8},{16,12},{20,16},{24,20},{28,24},{32,28},{36,32}... | collective-permute-start | bytes 200 | tf_op jit(solution)/shard_map/ppermute | solution.py:320
  18.5 1.9 %collective-permute-start.2 = (s32[4,4]{1,0:T(4,128)S(1)}, s32[4,4]{1,0:T(4,128)S(1)}, u32[]{:S(2)}, u32[]{:S(2)}) collective-permute-start(s32[4,4]{1,0:T(4,128)S(1)} %copy-done.4), channel_id=1, source_target_pairs={{0,8},{4,12},{8,16},{12,20},{16,24},{20,28},{24,32},{28,36},{32,40... | collective-permute-start | bytes 200 | tf_op jit(solution)/shard_map/ppermute | solution.py:320
  20.6 1.9 %collective-permute-start = (s32[32]{0:T(128)S(1)}, s32[32]{0:T(128)S(1)}, u32[]{:S(2)}, u32[]{:S(2)}) collective-permute-start(s32[32]{0:T(128)S(1)} %pad_add_fusion.1), channel_id=1, source_target_pairs={{0,4},{4,8},{8,12},{12,16},{16,20},{20,24},{24,28},{28,32},{32,36}... | collective-permute-start | bytes 392 | tf_op jit(solution)/shard_map/ppermute | solution.py:320
  22.6 2.2 %collective-permute-done.1.right_labels = s32[16]{0:T(128)S(1)} collective-permute-done((s32[16]{0:T(128)S(1)}, s32[16]{0:T(128)S(1)}, u32[]{:S(2)}, u32[]{:S(2)}) %collective-permute-start.1) | collective-permute-done | bytes 96 | tf_op jit(solution)/shard_map/ppermute | solution.py:320
  24.8 1.3 %collective-permute-done.2.far = s32[4,4]{1,0:T(4,128)S(1)} collective-permute-done((s32[4,4]{1,0:T(4,128)S(1)}, s32[4,4]{1,0:T(4,128)S(1)}, u32[]{:S(2)}, u32[]{:S(2)}) %collective-permute-start.2) | collective-permute-done | bytes 96 | tf_op jit(solution)/shard_map/ppermute | solution.py:320
  26.1 4.7 %collective-permute-done.near = s32[32]{0:T(128)S(1)} collective-permute-done((s32[32]{0:T(128)S(1)}, s32[32]{0:T(128)S(1)}, u32[]{:S(2)}, u32[]{:S(2)}) %collective-permute-start) | collective-permute-done | bytes 160 | tf_op jit(solution)/shard_map/ppermute | solution.py:320
  30.8 2.6 %plan.1 = s32[320]{0:T(512)S(1)} custom-call(s32[2]{0:T(128)S(1)} %pad_add_fusion.ids, s32[16]{0:T(128)S(1)} %bitcast.13, s32[16]{0:T(128)S(1)} %copy-done.6, s32[4,4]{1,0:T(4,128)S(1)} %copy-done.4, s32[32]{0:T(128)S(1)} %collective-permute-done.near, s32[16]{0:T(128)S(1)} %collective-permute-done.1.right_labels, s32[4,4]{1,0:T(4,128)S(1)} %collective-permute-done.2.far), custom_call_target="tpu_custom_call" | custom-call | tf_op jit(solution)/shard_map/plan/pallas_call | solution.py:350
  33.4 1.4 %copy-done.2 = bf16[16,192,192]{2,1,0:T(8,128)(2,1)S(1)} copy-done((bf16[16,192,192]{2,1,0:T(8,128)(2,1)S(1)}, bf16[16,192,192]{2,1,0:T(8,128)(2,1)}, u32[]{:S(2)}) %copy-start.2) | copy-done | bytes 1179672
  34.8 4.0 %close.1 = (f32[17,192,192]{2,1,0:T(8,128)S(1)}, bf16[16,192,192]{2,1,0:T(8,128)(2,1)S(1)}) custom-call(s32[320]{0:T(512)S(1)} %plan.1, bf16[16,192,192]{2,1,0:T(8,128)(2,1)S(1)} %bitcast.10, bf16[16,192,192]{2,1,0:T(8,128)(2,1)S(1)} %copy-done.2), custom_call_target="tpu_custom_call" | custom-call | tf_op jit(solution)/shard_map/close/pallas_call | solution.py:360
  38.8 1.6 %distant.1 = (f32[4,192,192]{2,1,0:T(8,128)S(1)}, bf16[4,288,128]{2,1,0:T(8,128)(2,1)S(1)}, bf16[4,288,128]{2,1,0:T(8,128)(2,1)S(1)}) custom-call(s32[2]{0:T(128)S(1)} %pad_add_fusion.ids, s32[320]{0:T(512)S(1)} %plan.1, bf16[16,192,192]{2,1,0:T(8,128)(2,1)S(1)} %bitcast.11, bf16[16,192,192]{2,1,0:T(8,128)(2,1)S(1)} %get-tuple-element.9.turned, ...), custom_call_target="tpu_custom_call" | custom-call | tf_op jit(solution)/shard_map/distant/pallas_call | solution.py:369
  41.9 1.1 %combine.1 = (f32[4,192,192]{2,1,0:T(8,128)}, bf16[4,288,128]{2,1,0:T(8,128)(2,1)S(1)}) custom-call(f32[4,192,192]{2,1,0:T(8,128)S(1)} %get-tuple-element.11.mine, bf16[4,288,128]{2,1,0:T(8,128)(2,1)S(1)} %collective-permute-done.5.ahead, bf16[4,288,128]{2,1,0:T(8,128)(2,1)S(1)} %collective-permute-done.6.behind), custom_call_target="tpu_custom_call" | custom-call | tf_op jit(solution)/shard_map/combine/pallas_call | solution.py:381
  43.0 20.6 %collective-permute-start.11 = (bf16[4,288,128]{2,1,0:T(8,128)(2,1)S(1)}, bf16[4,288,128]{2,1,0:T(8,128)(2,1)S(1)}, u32[]{:S(2)}, u32[]{:S(2)}) collective-permute-start(bf16[4,288,128]{2,1,0:T(8,128)(2,1)S(1)} %get-tuple-element.15.refs_8_), channel_id=1, source_target_pairs={{0,2},{1,3},{2,0},{3,1},{4,6},{5,7},{6,4},{7,5},{8,10},{9,11},{10,... | collective-permute-start | bytes 884744 | tf_op jit(solution)/shard_map/ppermute | solution.py:320
  63.6 1.9 %collective-permute-start.7 = (bf16[4,288,128]{2,1,0:T(8,128)(2,1)S(1)}, bf16[4,288,128]{2,1,0:T(8,128)(2,1)S(1)}, u32[]{:S(2)}, u32[]{:S(2)}) collective-permute-start(bf16[4,288,128]{2,1,0:T(8,128)(2,1)S(1)} %get-tuple-element.15.refs_8_), channel_id=1, source_target_pairs={{0,4},{4,8},{8,12},{12,16},{16,20},{20,24},{24,28},{28,32},{32,36}... | collective-permute-start | bytes 884744 | tf_op jit(solution)/shard_map/ppermute | solution.py:320
  65.6 2.1 %collective-permute-start.16 = (bf16[4,288,128]{2,1,0:T(8,128)(2,1)S(1)}, bf16[4,288,128]{2,1,0:T(8,128)(2,1)S(1)}, u32[]{:S(2)}, u32[]{:S(2)}) collective-permute-start(bf16[4,288,128]{2,1,0:T(8,128)(2,1)S(1)} %get-tuple-element.15.refs_8_), channel_id=1, source_target_pairs={{0,3},{1,0},{2,1},{3,2},{4,7},{5,4},{6,5},{7,6},{8,11},{9,8},{10,9... | collective-permute-start | bytes 884744 | tf_op jit(solution)/shard_map/ppermute | solution.py:320
  67.7 3.5 %collective-permute-done.11.refs_11_ = bf16[4,288,128]{2,1,0:T(8,128)(2,1)S(1)} collective-permute-done((bf16[4,288,128]{2,1,0:T(8,128)(2,1)S(1)}, bf16[4,288,128]{2,1,0:T(8,128)(2,1)S(1)}, u32[]{:S(2)}, u32[]{:S(2)}) %collective-permute-start.11) | collective-permute-done | bytes 294944 | tf_op jit(solution)/shard_map/ppermute | solution.py:320
  71.2 1.9 %collective-permute-start.12 = (bf16[4,288,128]{2,1,0:T(8,128)(2,1)S(1)}, bf16[4,288,128]{2,1,0:T(8,128)(2,1)S(1)}, u32[]{:S(2)}, u32[]{:S(2)}) collective-permute-start(bf16[4,288,128]{2,1,0:T(8,128)(2,1)S(1)} %collective-permute-done.11.refs_11_), channel_id=1, source_target_pairs={{0,4},{4,8},{8,12},{12,16},{16,20},{20,24},{24,28},{28,32},{32,36}... | collective-permute-start | bytes 884744 | tf_op jit(solution)/shard_map/ppermute | solution.py:320
  73.8 1.9 %collective-permute-start.8 = (bf16[4,288,128]{2,1,0:T(8,128)(2,1)S(1)}, bf16[4,288,128]{2,1,0:T(8,128)(2,1)S(1)}, u32[]{:S(2)}, u32[]{:S(2)}) collective-permute-start(bf16[4,288,128]{2,1,0:T(8,128)(2,1)S(1)} %collective-permute-done.7.refs_4_), channel_id=1, source_target_pairs={{0,4},{4,8},{8,12},{12,16},{16,20},{20,24},{24,28},{28,32},{32,36}... | collective-permute-start | bytes 884744 | tf_op jit(solution)/shard_map/ppermute | solution.py:320
  76.5 1.9 %collective-permute-start.17 = (bf16[4,288,128]{2,1,0:T(8,128)(2,1)S(1)}, bf16[4,288,128]{2,1,0:T(8,128)(2,1)S(1)}, u32[]{:S(2)}, u32[]{:S(2)}) collective-permute-start(bf16[4,288,128]{2,1,0:T(8,128)(2,1)S(1)} %collective-permute-done.16.refs_10_), channel_id=1, source_target_pairs={{0,4},{4,8},{8,12},{12,16},{16,20},{20,24},{24,28},{28,32},{32,36}... | collective-permute-start | bytes 884744 | tf_op jit(solution)/shard_map/ppermute | solution.py:320
  78.4 1.9 %collective-permute-start.15 = (bf16[4,288,128]{2,1,0:T(8,128)(2,1)S(1)}, bf16[4,288,128]{2,1,0:T(8,128)(2,1)S(1)}, u32[]{:S(2)}, u32[]{:S(2)}) collective-permute-start(bf16[4,288,128]{2,1,0:T(8,128)(2,1)S(1)} %collective-permute-done.14.refs_9_), channel_id=1, source_target_pairs={{0,4},{4,8},{8,12},{12,16},{16,20},{20,24},{24,28},{28,32},{32,36}... | collective-permute-start | bytes 884744 | tf_op jit(solution)/shard_map/ppermute | solution.py:320
  81.3 1.9 %collective-permute-start.13 = (bf16[4,288,128]{2,1,0:T(8,128)(2,1)S(1)}, bf16[4,288,128]{2,1,0:T(8,128)(2,1)S(1)}, u32[]{:S(2)}, u32[]{:S(2)}) collective-permute-start(bf16[4,288,128]{2,1,0:T(8,128)(2,1)S(1)} %collective-permute-done.12.refs_7_), channel_id=1, source_target_pairs={{0,4},{4,8},{8,12},{12,16},{16,20},{20,24},{24,28},{28,32},{32,36}... | collective-permute-start | bytes 884744 | tf_op jit(solution)/shard_map/ppermute | solution.py:320
  83.2 1.2 %collective-permute-done.8.refs_0_ = bf16[4,288,128]{2,1,0:T(8,128)(2,1)S(1)} collective-permute-done((bf16[4,288,128]{2,1,0:T(8,128)(2,1)S(1)}, bf16[4,288,128]{2,1,0:T(8,128)(2,1)S(1)}, u32[]{:S(2)}, u32[]{:S(2)}) %collective-permute-start.8) | collective-permute-done | bytes 294944 | tf_op jit(solution)/shard_map/ppermute | solution.py:320
  84.5 1.3 %collective-permute-start.10 = (bf16[4,288,128]{2,1,0:T(8,128)(2,1)S(1)}, bf16[4,288,128]{2,1,0:T(8,128)(2,1)S(1)}, u32[]{:S(2)}, u32[]{:S(2)}) collective-permute-start(bf16[4,288,128]{2,1,0:T(8,128)(2,1)S(1)} %collective-permute-done.8.refs_0_), channel_id=1, source_target_pairs={{1,0},{2,1},{3,2},{5,4},{6,5},{7,6},{9,8},{10,9},{11,10},{13,12},{... | collective-permute-start | bytes 884744 | tf_op jit(solution)/shard_map/ppermute | solution.py:320
  85.7 1.3 %collective-permute-start.9 = (bf16[4,288,128]{2,1,0:T(8,128)(2,1)S(1)}, bf16[4,288,128]{2,1,0:T(8,128)(2,1)S(1)}, u32[]{:S(2)}, u32[]{:S(2)}) collective-permute-start(bf16[4,288,128]{2,1,0:T(8,128)(2,1)S(1)} %collective-permute-done.8.refs_0_), channel_id=1, source_target_pairs={{1,2},{2,3},{3,0},{5,6},{6,7},{7,4},{9,10},{10,11},{11,8},{13,14},... | collective-permute-start | bytes 884744 | tf_op jit(solution)/shard_map/ppermute | solution.py:320
  87.6 3.2 %collective-permute-done.15.refs_5_ = bf16[4,288,128]{2,1,0:T(8,128)(2,1)S(1)} collective-permute-done((bf16[4,288,128]{2,1,0:T(8,128)(2,1)S(1)}, bf16[4,288,128]{2,1,0:T(8,128)(2,1)S(1)}, u32[]{:S(2)}, u32[]{:S(2)}) %collective-permute-start.15) | collective-permute-done | bytes 294944 | tf_op jit(solution)/shard_map/ppermute | solution.py:320
  90.8 3.2 %collective-permute-done.13.refs_3_ = bf16[4,288,128]{2,1,0:T(8,128)(2,1)S(1)} collective-permute-done((bf16[4,288,128]{2,1,0:T(8,128)(2,1)S(1)}, bf16[4,288,128]{2,1,0:T(8,128)(2,1)S(1)}, u32[]{:S(2)}, u32[]{:S(2)}) %collective-permute-start.13) | collective-permute-done | bytes 294944 | tf_op jit(solution)/shard_map/ppermute | solution.py:320
  94.7 2.8 %collective-permute-done.9.refs_1_ = bf16[4,288,128]{2,1,0:T(8,128)(2,1)S(1)} collective-permute-done((bf16[4,288,128]{2,1,0:T(8,128)(2,1)S(1)}, bf16[4,288,128]{2,1,0:T(8,128)(2,1)S(1)}, u32[]{:S(2)}, u32[]{:S(2)}) %collective-permute-start.9) | collective-permute-done | bytes 294944 | tf_op jit(solution)/shard_map/ppermute | solution.py:320
  97.5 1.1 %copy-done.3 = f32[4,192,192]{2,1,0:T(8,128)S(1)} copy-done((f32[4,192,192]{2,1,0:T(8,128)S(1)}, f32[4,192,192]{2,1,0:T(8,128)}, u32[]{:S(2)}) %copy-start.3) | copy-done | bytes 589848
  98.6 8.0 %sweep.1 = f32[4,192,192]{2,1,0:T(8,128)} custom-call(s32[2]{0:T(128)S(1)} %pad_add_fusion.ids, s32[320]{0:T(512)S(1)} %plan.1, f32[4,192,192]{2,1,0:T(8,128)S(1)} %copy-done.3, bf16[4,288,128]{2,1,0:T(8,128)(2,1)S(1)} %collective-permute-done.8.refs_0_, bf16[4,288,128]{2,1,0:T(8,128)(2,1)S(1)} %collective-permute-done.9.refs_1_, ...), custom_call_target="tpu_custom_call" | custom-call | tf_op jit(solution)/shard_map/sweep/pallas_call | solution.py:396
  (27 shorter events, 5.4 us)
Async XLA Ops:
  0.6 1.4 %copy-start.1 = (bf16[16,192,192]{2,1,0:T(8,128)(2,1)S(1)}, bf16[16,192,192]{2,1,0:T(8,128)(2,1)}, u32[]{:S(2)}) copy-start(bf16[16,192,192]{2,1,0:T(8,128)(2,1)} %tiles.1) | copy-start | bytes 3538948
  2.0 10.7 %copy-start.6 = (s32[16]{0:T(128)S(1)}, s32[16]{0:T(128)}, u32[]{:S(2)}) copy-start(s32[16]{0:T(128)} %labels.1) | copy-start | bytes 196
  2.0 16.5 %copy-start.4 = (s32[4,4]{1,0:T(4,128)S(1)}, s32[4,4]{1,0:T(4,128)}, u32[]{:S(2)}) copy-start(s32[4,4]{1,0:T(4,128)} %pattern.1) | copy-start | bytes 196
  2.0 28.8 %copy-start.5 = (s32[16,1]{0,1:T(1,128)S(1)}, s32[16,1]{0,1:T(1,128)}, u32[]{:S(2)}) copy-start(s32[16,1]{0,1:T(1,128)} %param.6) | copy-start | bytes 196
  2.0 31.4 %copy-start = (bf16[16,1,192,192]{3,2,1,0:T(8,128)(2,1)S(1)}, bf16[16,1,192,192]{3,2,1,0:T(8,128)(2,1)}, u32[]{:S(2)}) copy-start(bf16[16,1,192,192]{3,2,1,0:T(8,128)(2,1)} %param.5) | copy-start | bytes 3538948
  3.4 35.5 %collective-permute-start.4 = (bf16[16,288,128]{2,1,0:T(8,128)(2,1)}, bf16[16,288,128]{2,1,0:T(8,128)(2,1)S(1)}, u32[]{:S(2)}, u32[]{:S(2)}) collective-permute-start(bf16[16,288,128]{2,1,0:T(8,128)(2,1)} %pack.1), channel_id=1, source_target_pairs={{4,0},{8,4},{12,8},{16,12},{20,16},{24,20},{28,24},{32,28},{36,32}... | collective-permute-start | bytes 3538952 | tf_op jit(solution)/shard_map/ppermute | solution.py:320
  10.8 28.0 %collective-permute-start.3 = (bf16[16,288,128]{2,1,0:T(8,128)(2,1)}, bf16[16,288,128]{2,1,0:T(8,128)(2,1)}, u32[]{:S(2)}, u32[]{:S(2)}) collective-permute-start(bf16[16,288,128]{2,1,0:T(8,128)(2,1)} %pack.1), channel_id=1, source_target_pairs={{0,4},{4,8},{8,12},{12,16},{16,20},{20,24},{24,28},{28,32},{32,36}... | collective-permute-start | bytes 3538952 | tf_op jit(solution)/shard_map/ppermute | solution.py:320
  12.8 12.1 %collective-permute-start.1 = (s32[16]{0:T(128)S(1)}, s32[16]{0:T(128)S(1)}, u32[]{:S(2)}, u32[]{:S(2)}) collective-permute-start(s32[16]{0:T(128)S(1)} %copy-done.6), channel_id=1, source_target_pairs={{4,0},{8,4},{12,8},{16,12},{20,16},{24,20},{28,24},{32,28},{36,32}... | collective-permute-start | bytes 200 | tf_op jit(solution)/shard_map/ppermute | solution.py:320
  18.5 7.6 %collective-permute-start.2 = (s32[4,4]{1,0:T(4,128)S(1)}, s32[4,4]{1,0:T(4,128)S(1)}, u32[]{:S(2)}, u32[]{:S(2)}) collective-permute-start(s32[4,4]{1,0:T(4,128)S(1)} %copy-done.4), channel_id=1, source_target_pairs={{0,8},{4,12},{8,16},{12,20},{16,24},{20,28},{24,32},{28,36},{32,40... | collective-permute-start | bytes 200 | tf_op jit(solution)/shard_map/ppermute | solution.py:320
  20.6 10.2 %collective-permute-start = (s32[32]{0:T(128)S(1)}, s32[32]{0:T(128)S(1)}, u32[]{:S(2)}, u32[]{:S(2)}) collective-permute-start(s32[32]{0:T(128)S(1)} %pad_add_fusion.1), channel_id=1, source_target_pairs={{0,4},{4,8},{8,12},{12,16},{16,20},{20,24},{24,28},{28,32},{32,36}... | collective-permute-start | bytes 392 | tf_op jit(solution)/shard_map/ppermute | solution.py:320
  33.4 1.4 %copy-start.2 = (bf16[16,192,192]{2,1,0:T(8,128)(2,1)S(1)}, bf16[16,192,192]{2,1,0:T(8,128)(2,1)}, u32[]{:S(2)}) copy-start(bf16[16,192,192]{2,1,0:T(8,128)(2,1)} %tiles.1) | copy-start | bytes 3538948
  40.5 1.4 %collective-permute-start.5 = (bf16[4,288,128]{2,1,0:T(8,128)(2,1)S(1)}, bf16[4,288,128]{2,1,0:T(8,128)(2,1)S(1)}, u32[]{:S(2)}, u32[]{:S(2)}) collective-permute-start(bf16[4,288,128]{2,1,0:T(8,128)(2,1)S(1)} %get-tuple-element.12), channel_id=1, source_target_pairs={{1,2},{2,3},{3,1},{5,6},{6,7},{7,5},{9,10},{10,11},{11,9},{13,14},... | collective-permute-start | bytes 884744 | tf_op jit(solution)/shard_map/ppermute | solution.py:379
  41.2 0.7 collective-permute-start.6
  43.0 28.2 %collective-permute-start.11 = (bf16[4,288,128]{2,1,0:T(8,128)(2,1)S(1)}, bf16[4,288,128]{2,1,0:T(8,128)(2,1)S(1)}, u32[]{:S(2)}, u32[]{:S(2)}) collective-permute-start(bf16[4,288,128]{2,1,0:T(8,128)(2,1)S(1)} %get-tuple-element.15.refs_8_), channel_id=1, source_target_pairs={{0,2},{1,3},{2,0},{3,1},{4,6},{5,7},{6,4},{7,5},{8,10},{9,11},{10,... | collective-permute-start | bytes 884744 | tf_op jit(solution)/shard_map/ppermute | solution.py:320
  63.6 10.1 %collective-permute-start.7 = (bf16[4,288,128]{2,1,0:T(8,128)(2,1)S(1)}, bf16[4,288,128]{2,1,0:T(8,128)(2,1)S(1)}, u32[]{:S(2)}, u32[]{:S(2)}) collective-permute-start(bf16[4,288,128]{2,1,0:T(8,128)(2,1)S(1)} %get-tuple-element.15.refs_8_), channel_id=1, source_target_pairs={{0,4},{4,8},{8,12},{12,16},{16,20},{20,24},{24,28},{28,32},{32,36}... | collective-permute-start | bytes 884744 | tf_op jit(solution)/shard_map/ppermute | solution.py:320
  65.6 10.9 %collective-permute-start.16 = (bf16[4,288,128]{2,1,0:T(8,128)(2,1)S(1)}, bf16[4,288,128]{2,1,0:T(8,128)(2,1)S(1)}, u32[]{:S(2)}, u32[]{:S(2)}) collective-permute-start(bf16[4,288,128]{2,1,0:T(8,128)(2,1)S(1)} %get-tuple-element.15.refs_8_), channel_id=1, source_target_pairs={{0,3},{1,0},{2,1},{3,2},{4,7},{5,4},{6,5},{7,6},{8,11},{9,8},{10,9... | collective-permute-start | bytes 884744 | tf_op jit(solution)/shard_map/ppermute | solution.py:320
  67.7 10.8 %collective-permute-start.14 = (bf16[4,288,128]{2,1,0:T(8,128)(2,1)S(1)}, bf16[4,288,128]{2,1,0:T(8,128)(2,1)S(1)}, u32[]{:S(2)}, u32[]{:S(2)}) collective-permute-start(bf16[4,288,128]{2,1,0:T(8,128)(2,1)S(1)} %get-tuple-element.15.refs_8_), channel_id=1, source_target_pairs={{0,1},{1,2},{2,3},{3,0},{4,5},{5,6},{6,7},{7,4},{8,9},{9,10},{10,1... | collective-permute-start | bytes 884744 | tf_op jit(solution)/shard_map/ppermute | solution.py:320
  71.2 10.1 %collective-permute-start.12 = (bf16[4,288,128]{2,1,0:T(8,128)(2,1)S(1)}, bf16[4,288,128]{2,1,0:T(8,128)(2,1)S(1)}, u32[]{:S(2)}, u32[]{:S(2)}) collective-permute-start(bf16[4,288,128]{2,1,0:T(8,128)(2,1)S(1)} %collective-permute-done.11.refs_11_), channel_id=1, source_target_pairs={{0,4},{4,8},{8,12},{12,16},{16,20},{20,24},{24,28},{28,32},{32,36}... | collective-permute-start | bytes 884744 | tf_op jit(solution)/shard_map/ppermute | solution.py:320
  73.8 10.7 %collective-permute-start.8 = (bf16[4,288,128]{2,1,0:T(8,128)(2,1)S(1)}, bf16[4,288,128]{2,1,0:T(8,128)(2,1)S(1)}, u32[]{:S(2)}, u32[]{:S(2)}) collective-permute-start(bf16[4,288,128]{2,1,0:T(8,128)(2,1)S(1)} %collective-permute-done.7.refs_4_), channel_id=1, source_target_pairs={{0,4},{4,8},{8,12},{12,16},{16,20},{20,24},{24,28},{28,32},{32,36}... | collective-permute-start | bytes 884744 | tf_op jit(solution)/shard_map/ppermute | solution.py:320
  76.5 11.1 %collective-permute-start.17 = (bf16[4,288,128]{2,1,0:T(8,128)(2,1)S(1)}, bf16[4,288,128]{2,1,0:T(8,128)(2,1)S(1)}, u32[]{:S(2)}, u32[]{:S(2)}) collective-permute-start(bf16[4,288,128]{2,1,0:T(8,128)(2,1)S(1)} %collective-permute-done.16.refs_10_), channel_id=1, source_target_pairs={{0,4},{4,8},{8,12},{12,16},{16,20},{20,24},{24,28},{28,32},{32,36}... | collective-permute-start | bytes 884744 | tf_op jit(solution)/shard_map/ppermute | solution.py:320
  78.4 12.3 %collective-permute-start.15 = (bf16[4,288,128]{2,1,0:T(8,128)(2,1)S(1)}, bf16[4,288,128]{2,1,0:T(8,128)(2,1)S(1)}, u32[]{:S(2)}, u32[]{:S(2)}) collective-permute-start(bf16[4,288,128]{2,1,0:T(8,128)(2,1)S(1)} %collective-permute-done.14.refs_9_), channel_id=1, source_target_pairs={{0,4},{4,8},{8,12},{12,16},{16,20},{20,24},{24,28},{28,32},{32,36}... | collective-permute-start | bytes 884744 | tf_op jit(solution)/shard_map/ppermute | solution.py:320
  81.3 12.6 %collective-permute-start.13 = (bf16[4,288,128]{2,1,0:T(8,128)(2,1)S(1)}, bf16[4,288,128]{2,1,0:T(8,128)(2,1)S(1)}, u32[]{:S(2)}, u32[]{:S(2)}) collective-permute-start(bf16[4,288,128]{2,1,0:T(8,128)(2,1)S(1)} %collective-permute-done.12.refs_7_), channel_id=1, source_target_pairs={{0,4},{4,8},{8,12},{12,16},{16,20},{20,24},{24,28},{28,32},{32,36}... | collective-permute-start | bytes 884744 | tf_op jit(solution)/shard_map/ppermute | solution.py:320
  84.5 10.2 %collective-permute-start.10 = (bf16[4,288,128]{2,1,0:T(8,128)(2,1)S(1)}, bf16[4,288,128]{2,1,0:T(8,128)(2,1)S(1)}, u32[]{:S(2)}, u32[]{:S(2)}) collective-permute-start(bf16[4,288,128]{2,1,0:T(8,128)(2,1)S(1)} %collective-permute-done.8.refs_0_), channel_id=1, source_target_pairs={{1,0},{2,1},{3,2},{5,4},{6,5},{7,6},{9,8},{10,9},{11,10},{13,12},{... | collective-permute-start | bytes 884744 | tf_op jit(solution)/shard_map/ppermute | solution.py:320
  85.7 11.7 %collective-permute-start.9 = (bf16[4,288,128]{2,1,0:T(8,128)(2,1)S(1)}, bf16[4,288,128]{2,1,0:T(8,128)(2,1)S(1)}, u32[]{:S(2)}, u32[]{:S(2)}) collective-permute-start(bf16[4,288,128]{2,1,0:T(8,128)(2,1)S(1)} %collective-permute-done.8.refs_0_), channel_id=1, source_target_pairs={{1,2},{2,3},{3,0},{5,6},{6,7},{7,4},{9,10},{10,11},{11,8},{13,14},... | collective-permute-start | bytes 884744 | tf_op jit(solution)/shard_map/ppermute | solution.py:320
  97.5 1.1 %copy-start.3 = (f32[4,192,192]{2,1,0:T(8,128)S(1)}, f32[4,192,192]{2,1,0:T(8,128)}, u32[]{:S(2)}) copy-start(f32[4,192,192]{2,1,0:T(8,128)} %get-tuple-element.14.coarse) | copy-start | bytes 1769476

commit v3 on v2

--- a/solution.py
+++ b/solution.py
@@ -18,9 +18,7 @@
 LIST2 = 160
 TILES = 192
 KINDS = 240
-CLOSE = 256
-DISTANT = 288
-PLAN = 320
+PLAN = 256
 STEP = 4
 ZERO1 = 64
 SPARE = 16
@@ -47,9 +45,19 @@
     ref[half:, 128:] = packed[width:, rest:]
 
 
-def pack_kernel(tiles, packed):
-    for i in range(tiles.shape[0]):
-        store_packed(packed.at[i], tiles[i])
+def pack_kernel(labels, pattern, tiles, packed):
+    count, size = tiles.shape[0], tiles.shape[1] * tiles.shape[2] // 128
+    line, lane = iota((16, 128), 0), iota((16, 128), 1)
+    about = jnp.zeros((16, 128), F32)
+    for i in range(count):
+        about = jnp.where((line == 0) & (lane == i), (labels[i] & 3).astype(F32), about)
+    for r in range(4):
+        for q in range(1, 4):
+            offset = pattern[r, q] - pattern[r, 0]
+            about = jnp.where((line == 1) & (lane == 4 * r + q), offset.astype(F32), about)
+    packed[count * size :] = about.astype(BF16)
+    for i in range(count):
+        store_packed(packed.at[pl.ds(i * size, size)], tiles[i])
 
 
 def entries_of(plan, start, k):
@@ -68,7 +76,26 @@
         total[e >> 16] += tile
 
 
-def close_kernel(plan, tiles, own, total, turned):
+def slot_of(pattern, row, target):
+    slot = jnp.int32(0)
+    for q in range(1, 4):
+        slot = jnp.where(pattern[row, q] == target, q, slot)
+    return slot
+
+
+def close_kernel(ids, cols, labels, pattern, tiles, own, total, turned, work):
+    agg = ids[0]
+
+    def note(i, count):
+        place = cols[i] - agg * 16
+        row = labels[i] & 3
+        slot = slot_of(pattern, row, labels[place & 15])
+        work[count] = i | ((place & 15) << 8) | ((slot * 4 + row) << 16)
+        return count + (place >> 4 == 0).astype(jnp.int32)
+
+    count = lax.fori_loop(0, 16, note, jnp.int32(0))
+    for u in range(STEP - 1):
+        work[count + u] = SPARE << 16
     total[...] = jnp.zeros_like(total)
 
     def turn(i, carry):
@@ -78,34 +105,58 @@
     lax.fori_loop(0, 16, turn, 0)
 
     def step(k, carry):
-        add_lifted(entries_of(plan, CLOSE, k), tiles, turned, lambda u, place: own[place], total)
-        return carry
-
-    lax.fori_loop(0, (plan[3] + STEP - 1) // STEP, step, 0)
-
-
-def distant_kernel(ids, plan, tiles, turned, left, right, begun, mine, ahead, behind, total, remote):
-    col = ids[1]
+        add_lifted(entries_of(work, 0, k), tiles, turned, lambda u, place: own[place], total)
+        return carry
+
+    lax.fori_loop(0, (count + STEP - 1) // STEP, step, 0)
+
+
+def distant_kernel(ids, cols, labels, pattern, tiles, turned, left, right, begun, *refs):
+    mine, ahead, behind, near, total, remote, seen, about, work, sem = refs
+    agg, col = ids[0], ids[1]
+    width = tiles.shape[-1]
+    size = width * width // 128
+    end = 16 * size
+    seen[:16] = left[end:].astype(F32).astype(jnp.int32)
+    seen[16:] = right[end:].astype(F32).astype(jnp.int32)
+    copy = pltpu.make_async_copy(seen, about, sem)
+    copy.start()
     total[...] = begun[...]
-    width = tiles.shape[-1]
+    copy.wait()
+
+    def note(i, count):
+        place = cols[i] - (agg - 1) * 16
+        side, within = place >> 4, place & 15
+        target = jnp.where(side == 0, about[0, within] + 4 * agg - 4, about[16, within] + 4 * agg + 4)
+        row = labels[i] & 3
+        slot = slot_of(pattern, row, target)
+        work[count] = i | ((within + jnp.where(side == 0, 0, 16)) << 8) | ((slot * 4 + row) << 16)
+        return count + (side != 1).astype(jnp.int32)
+
+    count = lax.fori_loop(0, 16, note, jnp.int32(0))
+    for u in range(STEP - 1):
+        work[count + u] = SPARE << 16
+    for k in range(16):
+        near[k] = 4 * agg - 4 + k // 4 + about[1, k]
 
     def step(k, carry):
-        entries = entries_of(plan, DISTANT, k)
+        entries = entries_of(work, 0, k)
         for u, e in enumerate(entries):
             place = (e >> 8) & 255
+            start = pl.multiple_of((place & 15) * size, 16)
 
             @pl.when(place < 16)
             def _():
-                store_unpacked(remote.at[u], left[place], width)
+                store_unpacked(remote.at[u], left[pl.ds(start, size)], width)
 
             @pl.when(place >= 16)
             def _():
-                store_unpacked(remote.at[u], right[place - 16], width)
+                store_unpacked(remote.at[u], right[pl.ds(start, size)], width)
 
         add_lifted(entries, tiles, turned, lambda u, place: remote[u], total)
         return carry
 
-    lax.fori_loop(0, (plan[4] + STEP - 1) // STEP, step, 0)
+    lax.fori_loop(0, (count + STEP - 1) // STEP, step, 0)
     first = jnp.where(col == 3, 1, col + 1)
     second = jnp.where(col <= 1, 3, col - 1)
     for r in range(4):
@@ -114,48 +165,25 @@
         store_packed(behind.at[r], total[second * 4 + r].astype(BF16))
 
 
-def combine_kernel(mine, ahead, behind, coarse, sent, wide):
+def combine_kernel(plan, mine, ahead, behind, coarse, sent, kept, wide):
     width = mine.shape[-1]
     for r in range(4):
         store_unpacked(wide, ahead[r].astype(F32) + behind[r].astype(F32), width)
         tile = mine[r] + wide[...]
         coarse[r] = tile
+        kept[r] = tile
         store_packed(sent.at[r], tile.astype(BF16))
 
 
-def plan_kernel(ids, cols, labels, pattern, near, right_labels, far, plan, pat, need):
+def plan_kernel(ids, pattern, near, far, plan, pat, need):
     agg, col = ids[0], ids[1]
     base = (agg - 2) * 4
-    for r in range(4):
-        for q in range(4):
-            pat[4 * r + q] = far[r, q]
-            pat[16 + 4 * r + q] = near[16 + 4 * r + q]
-            pat[32 + 4 * r + q] = pattern[r, q]
+    for k in range(16):
+        pat[k] = far[k]
+        pat[16 + k] = near[k]
+        pat[32 + k] = pattern[k // 4, k % 4]
     for k in range(32):
         need[k] = 0
-
-    def fine(i, carry):
-        close, distant = carry
-        place = cols[i] - (agg - 1) * 16
-        within = place & 15
-        side = place >> 4
-        target = jnp.where(side == 0, near[within], jnp.where(side == 1, labels[within], right_labels[within]))
-        row = labels[i] - agg * 4
-        slot = jnp.int32(0)
-        for q in range(1, 4):
-            slot = jnp.where(pat[32 + 4 * row + q] == target, q, slot)
-        entry = i | ((slot * 4 + row) << 16)
-        plan[CLOSE + close] = entry | (within << 8)
-        plan[DISTANT + distant] = entry | ((within + jnp.where(side == 0, 0, 16)) << 8)
-        here = (side == 1).astype(jnp.int32)
-        return close + here, distant + 1 - here
-
-    close, distant = lax.fori_loop(0, 16, fine, (jnp.int32(0), jnp.int32(0)))
-    plan[3] = close
-    plan[4] = distant
-    for u in range(STEP - 1):
-        plan[CLOSE + close + u] = SPARE << 16
-        plan[DISTANT + distant + u] = SPARE << 16
 
     def through(row, index, target, m):
         inner = pat[4 * row + m]
@@ -341,52 +369,60 @@
             compiler_params=pltpu.CompilerParams(vmem_limit_bytes=mebibytes << 20),
         )
 
-    about = jnp.concatenate([agg_of, coarse_cols.reshape(-1)])
-    near, far = along(about, "agg", 1), along(coarse_cols, "agg", 2)
-    right_labels = along(agg_of, "agg", -1)
-    halo = call(pack_kernel, [VMEM], array((rows, *packed), BF16), VMEM, [], "pack", 10)(prolong)
+    cols = fine_cols.reshape(-1)
+    tiles = fine_tiles.reshape(rows, width, width)
+    halo_shape = (rows * packed[0] + 16, 128)
+    halo = call(pack_kernel, [SMEM] * 2 + [VMEM], array(halo_shape, BF16), VMEM, [], "pack", 10)(
+        agg_of, coarse_cols, prolong
+    )
     left, right = along(halo, "agg", 1), along(halo, "agg", -1)
-
+    total, turned = call(
+        close_kernel,
+        [SMEM] * 4 + [VMEM] * 2,
+        (array((SPARE + 1, width, width), F32), array((rows, width, width), BF16)),
+        (VMEM, VMEM),
+        [pltpu.SMEM((20,), jnp.int32)],
+        "close",
+        14,
+    )(ids, cols, agg_of, coarse_cols, tiles, prolong)
+    mine, ahead, behind, near = call(
+        distant_kernel,
+        [SMEM] * 4 + [VMEM] * 5,
+        (array(four, F32), array(four_packed, BF16), array(four_packed, BF16), array((16,), jnp.int32)),
+        (VMEM, VMEM, VMEM, SMEM),
+        [
+            pltpu.VMEM((SPARE + 1, width, width), F32),
+            pltpu.VMEM((STEP, width, width), BF16),
+            pltpu.VMEM((32, 128), jnp.int32),
+            pltpu.SMEM((32, 128), jnp.int32),
+            pltpu.SMEM((20,), jnp.int32),
+            pltpu.SemaphoreType.DMA,
+        ],
+        "distant",
+        22,
+    )(ids, cols, agg_of, coarse_cols, tiles, turned, left, right, total)
+
+    came_ahead = lax.ppermute(ahead, "col", [(1, 2), (2, 3), (3, 1)])
+    came_behind = lax.ppermute(behind, "col", [(1, 3), (2, 1), (3, 2)])
+    far = along(near, "agg", 1)
     plan = call(
         plan_kernel,
-        [SMEM] * 7,
+        [SMEM] * 4,
         array((PLAN,), jnp.int32),
         SMEM,
         [pltpu.SMEM((48,), jnp.int32), pltpu.SMEM((32,), jnp.int32)],
         "plan",
         4,
-    )(ids, fine_cols.reshape(-1), agg_of, coarse_cols, near, right_labels, far)
-    tiles = fine_tiles.reshape(rows, width, width)
-    total, turned = call(
-        close_kernel,
-        [SMEM, VMEM, VMEM],
-        (array((SPARE + 1, width, width), F32), array((rows, width, width), BF16)),
-        (VMEM, VMEM),
-        [],
-        "close",
-        14,
-    )(plan, tiles, prolong)
-    mine, ahead, behind = call(
-        distant_kernel,
-        [SMEM] * 2 + [VMEM] * 5,
-        (array(four, F32), array(four_packed, BF16), array(four_packed, BF16)),
-        (VMEM,) * 3,
-        [pltpu.VMEM((SPARE + 1, width, width), F32), pltpu.VMEM((STEP, width, width), BF16)],
-        "distant",
-        22,
-    )(ids, plan, tiles, turned, left, right, total)
-
-    came_ahead = lax.ppermute(ahead, "col", [(1, 2), (2, 3), (3, 1)])
-    came_behind = lax.ppermute(behind, "col", [(1, 3), (2, 1), (3, 2)])
-    coarse, sent = call(
+    )(ids, coarse_cols, near, far)
+    coarse, sent, kept = call(
         combine_kernel,
-        [VMEM] * 3,
-        (array(four, F32), array(four_packed, BF16)),
-        (VMEM, VMEM),
+        [SMEM] + [VMEM] * 3,
+        (array(four, F32), array(four_packed, BF16), array(four, F32)),
+        (VMEM, VMEM, VMEM),
         [pltpu.VMEM((width, width), F32)],
         "combine",
         8,
-    )(mine, came_ahead, came_behind)
+    )(plan, mine, came_ahead, came_behind)
 
     here = [sent] + [along(sent, "col", d, True) for d in (1, -1, 2)]
     before = [along(x, "agg", 1) for x in here]
@@ -410,7 +446,7 @@
         ],
         "sweep",
         34,
-    )(ids, plan, coarse, *further, *before, *here)
+    )(ids, plan, kept, *further, *before, *here)
     return (coarse[:, None], factor[:, None])
 
 

time: 108 us -> 101 us (0.935)
  starting transfers between devices: 57.1 us -> 39.4 us
  waiting for transfers between devices: 25.8 us -> 33.9 us
  Pallas kernels: 18.7 us -> 21.1 us
    ppermute x16 -> x14, starting transfers between devices: 55.7 us -> 38 us  [along(): lax.ppermute(block, axis, [pair for pair in pairs if sources is None or p...]
    ppermute x16 -> x14, waiting for transfers between devices: 25.8 us -> 33.8 us  [along(): lax.ppermute(block, axis, [pair for pair in pairs if sources is None or p...]
    pallas_call x5, Pallas kernels: 10.6 us -> 12.4 us  [the longest x1 4.2 us: on_device(): call(close_kernel, [SMEM] * 4 + [VMEM] * 2, (array((SPARE + 1, width, wid...]
    unnamed x14 -> x16, local copies, waits for them, and re-layouts: 3.95 us -> 4.16 us
  transfers between devices with their start and end apart: 18 -> 16, of which waited for: 13 -> 12; matrix products, arithmetic and copies ran while one was open for 0% -> 0% of each run, Pallas kernels for 6% -> 7%
where the time goes in v3:
time: 101 us; the launch traced here: 99.4 us
  starting transfers between devices  39.4 us (39%)
  waiting for transfers between devices  33.9 us (34%)
  Pallas kernels  21.1 us (21%)
  local copies, waits for them, and re-layouts  4.16 us (4%)
    ppermute x14, starting transfers between devices, along(): lax.ppermute(block, axis, [pair for pair in pairs if sources is None or p...  38 us
    ppermute x14, waiting for transfers between devices, along(): lax.ppermute(block, axis, [pair for pair in pairs if sources is None or p...  33.8 us
    pallas_call x1, Pallas kernels, on_device(): call(sweep_kernel, [SMEM] * 2 + [VMEM] + [ANY] * 12, array(four, F32), VM...  8.72 us
    pallas_call x1, Pallas kernels, on_device(): call(close_kernel, [SMEM] * 4 + [VMEM] * 2, (array((SPARE + 1, width, wid...  4.2 us
    unnamed x16, local copies, waits for them, and re-layouts  4.16 us
    pallas_call x1, Pallas kernels, on_device(): call(distant_kernel, [SMEM] * 4 + [VMEM] * 5, (array(four, F32), array(fo...  3.4 us
    pallas_call x1, Pallas kernels, on_device(): call(plan_kernel, [SMEM] * 4, array((PLAN,), jnp.int32), SMEM, [pltpu.SME...  2.28 us
  transfers between devices with their start and end apart: 16, of which 12 were waited for; matrix products, arithmetic and copies ran while one was open for 0% of the time, Pallas kernels for 7%

profile of v3, /device:TPU:6, one launch (start us, length us, event | category | flops | bytes accessed | tf_op | source)
XLA Modules:
  0.0 99.4 jit_solution(10438070391467536305)
XLA Ops:
  0.6 1.4 %copy-done.1 = bf16[16,192,192]{2,1,0:T(8,128)(2,1)S(1)} copy-done((bf16[16,192,192]{2,1,0:T(8,128)(2,1)S(1)}, bf16[16,192,192]{2,1,0:T(8,128)(2,1)}, u32[]{:S(2)}) %copy-start.1) | copy-done | bytes 1179672
  3.4 0.8 pack.1
  4.2 7.5 %collective-permute-start.1 = (bf16[4624,128]{1,0:T(8,128)(2,1)S(1)}, bf16[4624,128]{1,0:T(8,128)(2,1)}, u32[]{:S(2)}, u32[]{:S(2)}) collective-permute-start(bf16[4624,128]{1,0:T(8,128)(2,1)S(1)} %pack.1), channel_id=1, source_target_pairs={{4,0},{8,4},{12,8},{16,12},{20,16},{24,20},{28,24},{32,28},{36,32}... | collective-permute-start | bytes 3551240 | tf_op jit(solution)/shard_map/ppermute | solution.py:348
  11.7 1.9 %collective-permute-start = (bf16[4624,128]{1,0:T(8,128)(2,1)S(1)}, bf16[4624,128]{1,0:T(8,128)(2,1)}, u32[]{:S(2)}, u32[]{:S(2)}) collective-permute-start(bf16[4624,128]{1,0:T(8,128)(2,1)S(1)} %pack.1), channel_id=1, source_target_pairs={{0,4},{4,8},{8,12},{12,16},{16,20},{20,24},{24,28},{28,32},{32,36}... | collective-permute-start | bytes 3551240 | tf_op jit(solution)/shard_map/ppermute | solution.py:348
  13.7 1.4 %copy-done.2 = bf16[16,192,192]{2,1,0:T(8,128)(2,1)S(1)} copy-done((bf16[16,192,192]{2,1,0:T(8,128)(2,1)S(1)}, bf16[16,192,192]{2,1,0:T(8,128)(2,1)}, u32[]{:S(2)}) %copy-start.2) | copy-done | bytes 1179672
  15.1 4.2 %close.1 = (f32[17,192,192]{2,1,0:T(8,128)S(1)}, bf16[16,192,192]{2,1,0:T(8,128)(2,1)S(1)}) custom-call(s32[2]{0:T(128)S(1)} %pad_add_fusion.ids, s32[16]{0:T(128)S(1)} %bitcast.12, s32[16]{0:T(128)S(1)} %copy-done.6, s32[4,4]{1,0:T(4,128)S(1)} %copy-done.4, bf16[16,192,192]{2,1,0:T(8,128)(2,1)S(1)} %bitcast.10, bf16[16,192,192]{2,1,0:T(8,128)(2,1)S(1)} %copy-done.2), custom_call_target="tpu_custom_call" | custom-call | tf_op jit(solution)/shard_map/close/pallas_call | solution.py:379
  19.3 6.1 %collective-permute-done.1.right = bf16[4624,128]{1,0:T(8,128)(2,1)} collective-permute-done((bf16[4624,128]{1,0:T(8,128)(2,1)S(1)}, bf16[4624,128]{1,0:T(8,128)(2,1)}, u32[]{:S(2)}, u32[]{:S(2)}) %collective-permute-start.1) | collective-permute-done | bytes 1183776 | tf_op jit(solution)/shard_map/ppermute | solution.py:348
  25.4 6.0 %collective-permute-done.left = bf16[4624,128]{1,0:T(8,128)(2,1)} collective-permute-done((bf16[4624,128]{1,0:T(8,128)(2,1)S(1)}, bf16[4624,128]{1,0:T(8,128)(2,1)}, u32[]{:S(2)}, u32[]{:S(2)}) %collective-permute-start) | collective-permute-done | bytes 1183776 | tf_op jit(solution)/shard_map/ppermute | solution.py:348
  31.5 3.4 %distant.1 = (f32[4,192,192]{2,1,0:T(8,128)S(1)}, bf16[4,288,128]{2,1,0:T(8,128)(2,1)S(1)}, bf16[4,288,128]{2,1,0:T(8,128)(2,1)S(1)}, s32[16]{0:T(128)S(1)}) custom-call(s32[2]{0:T(128)S(1)} %pad_add_fusion.ids, s32[16]{0:T(128)S(1)} %bitcast.13, s32[16]{0:T(128)S(1)} %copy-done.6, s32[4,4]{1,0:T(4,128)S(1)} %copy-done.4, ...), custom_call_target="tpu_custom_call" | custom-call | tf_op jit(solution)/shard_map/distant/pallas_call | solution.py:388
  34.9 0.7 collective-permute-start.3
  36.3 1.9 %collective-permute-start.2 = (s32[16]{0:T(128)S(1)}, s32[16]{0:T(128)S(1)}, u32[]{:S(2)}, u32[]{:S(2)}) collective-permute-start(s32[16]{0:T(128)S(1)} %get-tuple-element.13.near), channel_id=1, source_target_pairs={{0,4},{4,8},{8,12},{12,16},{16,20},{20,24},{24,28},{28,32},{32,36}... | collective-permute-start | bytes 200 | tf_op jit(solution)/shard_map/ppermute | solution.py:348
  38.2 5.1 %collective-permute-done.2.far = s32[16]{0:T(128)S(1)} collective-permute-done((s32[16]{0:T(128)S(1)}, s32[16]{0:T(128)S(1)}, u32[]{:S(2)}, u32[]{:S(2)}) %collective-permute-start.2) | collective-permute-done | bytes 96 | tf_op jit(solution)/shard_map/ppermute | solution.py:348
  43.3 2.3 %plan.1 = s32[256]{0:T(256)S(1)} custom-call(s32[2]{0:T(128)S(1)} %pad_add_fusion.ids, s32[4,4]{1,0:T(4,128)S(1)} %copy-done.4, s32[16]{0:T(128)S(1)} %get-tuple-element.13.near, s32[16]{0:T(128)S(1)} %collective-permute-done.2.far), custom_call_target="tpu_custom_call" | custom-call | tf_op jit(solution)/shard_map/plan/pallas_call | solution.py:408
  45.6 1.7 %combine.1 = (f32[4,192,192]{2,1,0:T(8,128)}, bf16[4,288,128]{2,1,0:T(8,128)(2,1)S(1)}, f32[4,192,192]{2,1,0:T(8,128)S(1)}) custom-call(s32[256]{0:T(256)S(1)} %plan.1, f32[4,192,192]{2,1,0:T(8,128)S(1)} %get-tuple-element.14.mine, bf16[4,288,128]{2,1,0:T(8,128)(2,1)S(1)} %collective-permute-done.3.ahead, bf16[4,288,128]{2,1,0:T(8,128)(2,1)S(1)} %collective-permute-done.4.behind), custom_call_target="tpu_custom_call" | custom-call | tf_op jit(solution)/shard_map/combine/pallas_call | solution.py:417
  47.3 10.0 %collective-permute-start.9 = (bf16[4,288,128]{2,1,0:T(8,128)(2,1)S(1)}, bf16[4,288,128]{2,1,0:T(8,128)(2,1)S(1)}, u32[]{:S(2)}, u32[]{:S(2)}) collective-permute-start(bf16[4,288,128]{2,1,0:T(8,128)(2,1)S(1)} %get-tuple-element.19.refs_8_), channel_id=1, source_target_pairs={{0,2},{1,3},{2,0},{3,1},{4,6},{5,7},{6,4},{7,5},{8,10},{9,11},{10,... | collective-permute-start | bytes 884744 | tf_op jit(solution)/shard_map/ppermute | solution.py:348
  57.3 1.9 %collective-permute-start.5 = (bf16[4,288,128]{2,1,0:T(8,128)(2,1)S(1)}, bf16[4,288,128]{2,1,0:T(8,128)(2,1)S(1)}, u32[]{:S(2)}, u32[]{:S(2)}) collective-permute-start(bf16[4,288,128]{2,1,0:T(8,128)(2,1)S(1)} %get-tuple-element.19.refs_8_), channel_id=1, source_target_pairs={{0,4},{4,8},{8,12},{12,16},{16,20},{20,24},{24,28},{28,32},{32,36}... | collective-permute-start | bytes 884744 | tf_op jit(solution)/shard_map/ppermute | solution.py:348
  59.3 2.6 %collective-permute-start.14 = (bf16[4,288,128]{2,1,0:T(8,128)(2,1)S(1)}, bf16[4,288,128]{2,1,0:T(8,128)(2,1)S(1)}, u32[]{:S(2)}, u32[]{:S(2)}) collective-permute-start(bf16[4,288,128]{2,1,0:T(8,128)(2,1)S(1)} %get-tuple-element.19.refs_8_), channel_id=1, source_target_pairs={{0,3},{1,0},{2,1},{3,2},{4,7},{5,4},{6,5},{7,6},{8,11},{9,8},{10,9... | collective-permute-start | bytes 884744 | tf_op jit(solution)/shard_map/ppermute | solution.py:348
  61.9 2.4 %collective-permute-done.9.refs_11_ = bf16[4,288,128]{2,1,0:T(8,128)(2,1)S(1)} collective-permute-done((bf16[4,288,128]{2,1,0:T(8,128)(2,1)S(1)}, bf16[4,288,128]{2,1,0:T(8,128)(2,1)S(1)}, u32[]{:S(2)}, u32[]{:S(2)}) %collective-permute-start.9) | collective-permute-done | bytes 294944 | tf_op jit(solution)/shard_map/ppermute | solution.py:348
  64.2 1.9 %collective-permute-start.10 = (bf16[4,288,128]{2,1,0:T(8,128)(2,1)S(1)}, bf16[4,288,128]{2,1,0:T(8,128)(2,1)S(1)}, u32[]{:S(2)}, u32[]{:S(2)}) collective-permute-start(bf16[4,288,128]{2,1,0:T(8,128)(2,1)S(1)} %collective-permute-done.9.refs_11_), channel_id=1, source_target_pairs={{0,4},{4,8},{8,12},{12,16},{16,20},{20,24},{24,28},{28,32},{32,36}... | collective-permute-start | bytes 884744 | tf_op jit(solution)/shard_map/ppermute | solution.py:348
  66.2 1.3 %collective-permute-done.5.refs_4_ = bf16[4,288,128]{2,1,0:T(8,128)(2,1)S(1)} collective-permute-done((bf16[4,288,128]{2,1,0:T(8,128)(2,1)S(1)}, bf16[4,288,128]{2,1,0:T(8,128)(2,1)S(1)}, u32[]{:S(2)}, u32[]{:S(2)}) %collective-permute-start.5) | collective-permute-done | bytes 294944 | tf_op jit(solution)/shard_map/ppermute | solution.py:348
  67.5 1.9 %collective-permute-start.6 = (bf16[4,288,128]{2,1,0:T(8,128)(2,1)S(1)}, bf16[4,288,128]{2,1,0:T(8,128)(2,1)S(1)}, u32[]{:S(2)}, u32[]{:S(2)}) collective-permute-start(bf16[4,288,128]{2,1,0:T(8,128)(2,1)S(1)} %collective-permute-done.5.refs_4_), channel_id=1, source_target_pairs={{0,4},{4,8},{8,12},{12,16},{16,20},{20,24},{24,28},{28,32},{32,36}... | collective-permute-start | bytes 884744 | tf_op jit(solution)/shard_map/ppermute | solution.py:348
  69.4 1.9 %collective-permute-start.15 = (bf16[4,288,128]{2,1,0:T(8,128)(2,1)S(1)}, bf16[4,288,128]{2,1,0:T(8,128)(2,1)S(1)}, u32[]{:S(2)}, u32[]{:S(2)}) collective-permute-start(bf16[4,288,128]{2,1,0:T(8,128)(2,1)S(1)} %collective-permute-done.14.refs_10_), channel_id=1, source_target_pairs={{0,4},{4,8},{8,12},{12,16},{16,20},{20,24},{24,28},{28,32},{32,36}... | collective-permute-start | bytes 884744 | tf_op jit(solution)/shard_map/ppermute | solution.py:348
  71.3 1.9 %collective-permute-start.13 = (bf16[4,288,128]{2,1,0:T(8,128)(2,1)S(1)}, bf16[4,288,128]{2,1,0:T(8,128)(2,1)S(1)}, u32[]{:S(2)}, u32[]{:S(2)}) collective-permute-start(bf16[4,288,128]{2,1,0:T(8,128)(2,1)S(1)} %collective-permute-done.12.refs_9_), channel_id=1, source_target_pairs={{0,4},{4,8},{8,12},{12,16},{16,20},{20,24},{24,28},{28,32},{32,36}... | collective-permute-start | bytes 884744 | tf_op jit(solution)/shard_map/ppermute | solution.py:348
  73.3 1.1 %collective-permute-done.10.refs_7_ = bf16[4,288,128]{2,1,0:T(8,128)(2,1)S(1)} collective-permute-done((bf16[4,288,128]{2,1,0:T(8,128)(2,1)S(1)}, bf16[4,288,128]{2,1,0:T(8,128)(2,1)S(1)}, u32[]{:S(2)}, u32[]{:S(2)}) %collective-permute-start.10) | collective-permute-done | bytes 294944 | tf_op jit(solution)/shard_map/ppermute | solution.py:348
  74.4 1.9 %collective-permute-start.11 = (bf16[4,288,128]{2,1,0:T(8,128)(2,1)S(1)}, bf16[4,288,128]{2,1,0:T(8,128)(2,1)S(1)}, u32[]{:S(2)}, u32[]{:S(2)}) collective-permute-start(bf16[4,288,128]{2,1,0:T(8,128)(2,1)S(1)} %collective-permute-done.10.refs_7_), channel_id=1, source_target_pairs={{0,4},{4,8},{8,12},{12,16},{16,20},{20,24},{24,28},{28,32},{32,36}... | collective-permute-start | bytes 884744 | tf_op jit(solution)/shard_map/ppermute | solution.py:348
  76.3 1.3 %collective-permute-done.6.refs_0_ = bf16[4,288,128]{2,1,0:T(8,128)(2,1)S(1)} collective-permute-done((bf16[4,288,128]{2,1,0:T(8,128)(2,1)S(1)}, bf16[4,288,128]{2,1,0:T(8,128)(2,1)S(1)}, u32[]{:S(2)}, u32[]{:S(2)}) %collective-permute-start.6) | collective-permute-done | bytes 294944 | tf_op jit(solution)/shard_map/ppermute | solution.py:348
  77.6 1.3 %collective-permute-start.8 = (bf16[4,288,128]{2,1,0:T(8,128)(2,1)S(1)}, bf16[4,288,128]{2,1,0:T(8,128)(2,1)S(1)}, u32[]{:S(2)}, u32[]{:S(2)}) collective-permute-start(bf16[4,288,128]{2,1,0:T(8,128)(2,1)S(1)} %collective-permute-done.6.refs_0_), channel_id=1, source_target_pairs={{1,0},{2,1},{3,2},{5,4},{6,5},{7,6},{9,8},{10,9},{11,10},{13,12},{... | collective-permute-start | bytes 884744 | tf_op jit(solution)/shard_map/ppermute | solution.py:348
  78.9 1.3 %collective-permute-start.7 = (bf16[4,288,128]{2,1,0:T(8,128)(2,1)S(1)}, bf16[4,288,128]{2,1,0:T(8,128)(2,1)S(1)}, u32[]{:S(2)}, u32[]{:S(2)}) collective-permute-start(bf16[4,288,128]{2,1,0:T(8,128)(2,1)S(1)} %collective-permute-done.6.refs_0_), channel_id=1, source_target_pairs={{1,2},{2,3},{3,0},{5,6},{6,7},{7,4},{9,10},{10,11},{11,8},{13,14},... | collective-permute-start | bytes 884744 | tf_op jit(solution)/shard_map/ppermute | solution.py:348
  80.8 3.2 %collective-permute-done.13.refs_5_ = bf16[4,288,128]{2,1,0:T(8,128)(2,1)S(1)} collective-permute-done((bf16[4,288,128]{2,1,0:T(8,128)(2,1)S(1)}, bf16[4,288,128]{2,1,0:T(8,128)(2,1)S(1)}, u32[]{:S(2)}, u32[]{:S(2)}) %collective-permute-start.13) | collective-permute-done | bytes 294944 | tf_op jit(solution)/shard_map/ppermute | solution.py:348
  83.9 3.2 %collective-permute-done.11.refs_3_ = bf16[4,288,128]{2,1,0:T(8,128)(2,1)S(1)} collective-permute-done((bf16[4,288,128]{2,1,0:T(8,128)(2,1)S(1)}, bf16[4,288,128]{2,1,0:T(8,128)(2,1)S(1)}, u32[]{:S(2)}, u32[]{:S(2)}) %collective-permute-start.11) | collective-permute-done | bytes 294944 | tf_op jit(solution)/shard_map/ppermute | solution.py:348
  87.7 3.0 %collective-permute-done.7.refs_1_ = bf16[4,288,128]{2,1,0:T(8,128)(2,1)S(1)} collective-permute-done((bf16[4,288,128]{2,1,0:T(8,128)(2,1)S(1)}, bf16[4,288,128]{2,1,0:T(8,128)(2,1)S(1)}, u32[]{:S(2)}, u32[]{:S(2)}) %collective-permute-start.7) | collective-permute-done | bytes 294944 | tf_op jit(solution)/shard_map/ppermute | solution.py:348
  90.7 8.7 %sweep.1 = f32[4,192,192]{2,1,0:T(8,128)} custom-call(s32[2]{0:T(128)S(1)} %pad_add_fusion.ids, s32[256]{0:T(256)S(1)} %plan.1, f32[4,192,192]{2,1,0:T(8,128)S(1)} %get-tuple-element.18.coarse, bf16[4,288,128]{2,1,0:T(8,128)(2,1)S(1)} %collective-permute-done.6.refs_0_, bf16[4,288,128]{2,1,0:T(8,128)(2,1)S(1)} %collective-permute-done.7.refs_1_, ...), custom_call_target="tpu_custom_call" | custom-call | tf_op jit(solution)/shard_map/sweep/pallas_call | solution.py:432
  (23 shorter events, 3.3 us)
Async XLA Ops:
  0.6 1.4 %copy-start.1 = (bf16[16,192,192]{2,1,0:T(8,128)(2,1)S(1)}, bf16[16,192,192]{2,1,0:T(8,128)(2,1)}, u32[]{:S(2)}) copy-start(bf16[16,192,192]{2,1,0:T(8,128)(2,1)} %tiles.1) | copy-start | bytes 3538948
  2.0 0.7 copy-start.3
  2.7 0.7 copy-start.5
  3.4 10.3 %copy-start = (bf16[16,1,192,192]{3,2,1,0:T(8,128)(2,1)S(1)}, bf16[16,1,192,192]{3,2,1,0:T(8,128)(2,1)}, u32[]{:S(2)}) copy-start(bf16[16,1,192,192]{3,2,1,0:T(8,128)(2,1)} %param.5) | copy-start | bytes 3538948
  3.4 10.3 %copy-start.4 = (s32[4,4]{1,0:T(4,128)S(1)}, s32[4,4]{1,0:T(4,128)}, u32[]{:S(2)}) copy-start(s32[4,4]{1,0:T(4,128)} %pattern.7) | copy-start | bytes 196
  3.4 10.3 %copy-start.6 = (s32[16]{0:T(128)S(1)}, s32[16]{0:T(128)}, u32[]{:S(2)}) copy-start(s32[16]{0:T(128)} %labels.5) | copy-start | bytes 196
  3.4 10.3 %copy-start.7 = (s32[16,1]{0,1:T(1,128)S(1)}, s32[16,1]{0,1:T(1,128)}, u32[]{:S(2)}) copy-start(s32[16,1]{0,1:T(1,128)} %param.6) | copy-start | bytes 196
  4.2 21.2 %collective-permute-start.1 = (bf16[4624,128]{1,0:T(8,128)(2,1)S(1)}, bf16[4624,128]{1,0:T(8,128)(2,1)}, u32[]{:S(2)}, u32[]{:S(2)}) collective-permute-start(bf16[4624,128]{1,0:T(8,128)(2,1)S(1)} %pack.1), channel_id=1, source_target_pairs={{4,0},{8,4},{12,8},{16,12},{20,16},{24,20},{28,24},{32,28},{36,32}... | collective-permute-start | bytes 3551240 | tf_op jit(solution)/shard_map/ppermute | solution.py:348
  11.7 19.8 %collective-permute-start = (bf16[4624,128]{1,0:T(8,128)(2,1)S(1)}, bf16[4624,128]{1,0:T(8,128)(2,1)}, u32[]{:S(2)}, u32[]{:S(2)}) collective-permute-start(bf16[4624,128]{1,0:T(8,128)(2,1)S(1)} %pack.1), channel_id=1, source_target_pairs={{0,4},{4,8},{8,12},{12,16},{16,20},{20,24},{24,28},{28,32},{32,36}... | collective-permute-start | bytes 3551240 | tf_op jit(solution)/shard_map/ppermute | solution.py:348
  13.7 1.4 %copy-start.2 = (bf16[16,192,192]{2,1,0:T(8,128)(2,1)S(1)}, bf16[16,192,192]{2,1,0:T(8,128)(2,1)}, u32[]{:S(2)}) copy-start(bf16[16,192,192]{2,1,0:T(8,128)(2,1)} %tiles.1) | copy-start | bytes 3538948
  34.9 10.7 %collective-permute-start.3 = (bf16[4,288,128]{2,1,0:T(8,128)(2,1)S(1)}, bf16[4,288,128]{2,1,0:T(8,128)(2,1)S(1)}, u32[]{:S(2)}, u32[]{:S(2)}) collective-permute-start(bf16[4,288,128]{2,1,0:T(8,128)(2,1)S(1)} %get-tuple-element.15), channel_id=1, source_target_pairs={{1,2},{2,3},{3,1},{5,6},{6,7},{7,5},{9,10},{10,11},{11,9},{13,14},... | collective-permute-start | bytes 884744 | tf_op jit(solution)/shard_map/ppermute | solution.py:405
  35.6 10.0 %collective-permute-start.4 = (bf16[4,288,128]{2,1,0:T(8,128)(2,1)S(1)}, bf16[4,288,128]{2,1,0:T(8,128)(2,1)S(1)}, u32[]{:S(2)}, u32[]{:S(2)}) collective-permute-start(bf16[4,288,128]{2,1,0:T(8,128)(2,1)S(1)} %get-tuple-element.16), channel_id=1, source_target_pairs={{1,3},{2,1},{3,2},{5,7},{6,5},{7,6},{9,11},{10,9},{11,10},{13,15},... | collective-permute-start | bytes 884744 | tf_op jit(solution)/shard_map/ppermute | solution.py:406
  36.3 7.0 %collective-permute-start.2 = (s32[16]{0:T(128)S(1)}, s32[16]{0:T(128)S(1)}, u32[]{:S(2)}, u32[]{:S(2)}) collective-permute-start(s32[16]{0:T(128)S(1)} %get-tuple-element.13.near), channel_id=1, source_target_pairs={{0,4},{4,8},{8,12},{12,16},{16,20},{20,24},{24,28},{28,32},{32,36}... | collective-permute-start | bytes 200 | tf_op jit(solution)/shard_map/ppermute | solution.py:348
  47.3 17.0 %collective-permute-start.9 = (bf16[4,288,128]{2,1,0:T(8,128)(2,1)S(1)}, bf16[4,288,128]{2,1,0:T(8,128)(2,1)S(1)}, u32[]{:S(2)}, u32[]{:S(2)}) collective-permute-start(bf16[4,288,128]{2,1,0:T(8,128)(2,1)S(1)} %get-tuple-element.19.refs_8_), channel_id=1, source_target_pairs={{0,2},{1,3},{2,0},{3,1},{4,6},{5,7},{6,4},{7,5},{8,10},{9,11},{10,... | collective-permute-start | bytes 884744 | tf_op jit(solution)/shard_map/ppermute | solution.py:348
  57.3 10.1 %collective-permute-start.5 = (bf16[4,288,128]{2,1,0:T(8,128)(2,1)S(1)}, bf16[4,288,128]{2,1,0:T(8,128)(2,1)S(1)}, u32[]{:S(2)}, u32[]{:S(2)}) collective-permute-start(bf16[4,288,128]{2,1,0:T(8,128)(2,1)S(1)} %get-tuple-element.19.refs_8_), channel_id=1, source_target_pairs={{0,4},{4,8},{8,12},{12,16},{16,20},{20,24},{24,28},{28,32},{32,36}... | collective-permute-start | bytes 884744 | tf_op jit(solution)/shard_map/ppermute | solution.py:348
  59.3 10.1 %collective-permute-start.14 = (bf16[4,288,128]{2,1,0:T(8,128)(2,1)S(1)}, bf16[4,288,128]{2,1,0:T(8,128)(2,1)S(1)}, u32[]{:S(2)}, u32[]{:S(2)}) collective-permute-start(bf16[4,288,128]{2,1,0:T(8,128)(2,1)S(1)} %get-tuple-element.19.refs_8_), channel_id=1, source_target_pairs={{0,3},{1,0},{2,1},{3,2},{4,7},{5,4},{6,5},{7,6},{8,11},{9,8},{10,9... | collective-permute-start | bytes 884744 | tf_op jit(solution)/shard_map/ppermute | solution.py:348
  61.9 9.5 %collective-permute-start.12 = (bf16[4,288,128]{2,1,0:T(8,128)(2,1)S(1)}, bf16[4,288,128]{2,1,0:T(8,128)(2,1)S(1)}, u32[]{:S(2)}, u32[]{:S(2)}) collective-permute-start(bf16[4,288,128]{2,1,0:T(8,128)(2,1)S(1)} %get-tuple-element.19.refs_8_), channel_id=1, source_target_pairs={{0,1},{1,2},{2,3},{3,0},{4,5},{5,6},{6,7},{7,4},{8,9},{9,10},{10,1... | collective-permute-start | bytes 884744 | tf_op jit(solution)/shard_map/ppermute | solution.py:348
  64.2 10.1 %collective-permute-start.10 = (bf16[4,288,128]{2,1,0:T(8,128)(2,1)S(1)}, bf16[4,288,128]{2,1,0:T(8,128)(2,1)S(1)}, u32[]{:S(2)}, u32[]{:S(2)}) collective-permute-start(bf16[4,288,128]{2,1,0:T(8,128)(2,1)S(1)} %collective-permute-done.9.refs_11_), channel_id=1, source_target_pairs={{0,4},{4,8},{8,12},{12,16},{16,20},{20,24},{24,28},{28,32},{32,36}... | collective-permute-start | bytes 884744 | tf_op jit(solution)/shard_map/ppermute | solution.py:348
  67.5 10.1 %collective-permute-start.6 = (bf16[4,288,128]{2,1,0:T(8,128)(2,1)S(1)}, bf16[4,288,128]{2,1,0:T(8,128)(2,1)S(1)}, u32[]{:S(2)}, u32[]{:S(2)}) collective-permute-start(bf16[4,288,128]{2,1,0:T(8,128)(2,1)S(1)} %collective-permute-done.5.refs_4_), channel_id=1, source_target_pairs={{0,4},{4,8},{8,12},{12,16},{16,20},{20,24},{24,28},{28,32},{32,36}... | collective-permute-start | bytes 884744 | tf_op jit(solution)/shard_map/ppermute | solution.py:348
  69.4 11.4 %collective-permute-start.15 = (bf16[4,288,128]{2,1,0:T(8,128)(2,1)S(1)}, bf16[4,288,128]{2,1,0:T(8,128)(2,1)S(1)}, u32[]{:S(2)}, u32[]{:S(2)}) collective-permute-start(bf16[4,288,128]{2,1,0:T(8,128)(2,1)S(1)} %collective-permute-done.14.refs_10_), channel_id=1, source_target_pairs={{0,4},{4,8},{8,12},{12,16},{16,20},{20,24},{24,28},{28,32},{32,36}... | collective-permute-start | bytes 884744 | tf_op jit(solution)/shard_map/ppermute | solution.py:348
  71.3 12.6 %collective-permute-start.13 = (bf16[4,288,128]{2,1,0:T(8,128)(2,1)S(1)}, bf16[4,288,128]{2,1,0:T(8,128)(2,1)S(1)}, u32[]{:S(2)}, u32[]{:S(2)}) collective-permute-start(bf16[4,288,128]{2,1,0:T(8,128)(2,1)S(1)} %collective-permute-done.12.refs_9_), channel_id=1, source_target_pairs={{0,4},{4,8},{8,12},{12,16},{16,20},{20,24},{24,28},{28,32},{32,36}... | collective-permute-start | bytes 884744 | tf_op jit(solution)/shard_map/ppermute | solution.py:348
  74.4 12.7 %collective-permute-start.11 = (bf16[4,288,128]{2,1,0:T(8,128)(2,1)S(1)}, bf16[4,288,128]{2,1,0:T(8,128)(2,1)S(1)}, u32[]{:S(2)}, u32[]{:S(2)}) collective-permute-start(bf16[4,288,128]{2,1,0:T(8,128)(2,1)S(1)} %collective-permute-done.10.refs_7_), channel_id=1, source_target_pairs={{0,4},{4,8},{8,12},{12,16},{16,20},{20,24},{24,28},{28,32},{32,36}... | collective-permute-start | bytes 884744 | tf_op jit(solution)/shard_map/ppermute | solution.py:348
  77.6 10.1 %collective-permute-start.8 = (bf16[4,288,128]{2,1,0:T(8,128)(2,1)S(1)}, bf16[4,288,128]{2,1,0:T(8,128)(2,1)S(1)}, u32[]{:S(2)}, u32[]{:S(2)}) collective-permute-start(bf16[4,288,128]{2,1,0:T(8,128)(2,1)S(1)} %collective-permute-done.6.refs_0_), channel_id=1, source_target_pairs={{1,0},{2,1},{3,2},{5,4},{6,5},{7,6},{9,8},{10,9},{11,10},{13,12},{... | collective-permute-start | bytes 884744 | tf_op jit(solution)/shard_map/ppermute | solution.py:348
  78.9 11.8 %collective-permute-start.7 = (bf16[4,288,128]{2,1,0:T(8,128)(2,1)S(1)}, bf16[4,288,128]{2,1,0:T(8,128)(2,1)S(1)}, u32[]{:S(2)}, u32[]{:S(2)}) collective-permute-start(bf16[4,288,128]{2,1,0:T(8,128)(2,1)S(1)} %collective-permute-done.6.refs_0_), channel_id=1, source_target_pairs={{1,2},{2,3},{3,0},{5,6},{6,7},{7,4},{9,10},{10,11},{11,8},{13,14},... | collective-permute-start | bytes 884744 | tf_op jit(solution)/shard_map/ppermute | solution.py:348

commit v4 on v3

--- a/solution.py
+++ b/solution.py
@@ -372,7 +372,7 @@
     cols = fine_cols.reshape(-1)
     tiles = fine_tiles.reshape(rows, width, width)
     halo_shape = (rows * packed[0] + 16, 128)
-    halo = call(pack_kernel, [SMEM] * 2 + [VMEM], array(halo_shape, BF16), VMEM, [], "pack", 10)(
+    halo = call(pack_kernel, [SMEM] * 2 + [VMEM], array(halo_shape, BF16), VMEM, [], "pack", 60)(
         agg_of, coarse_cols, prolong
     )
     left, right = along(halo, "agg", 1), along(halo, "agg", -1)
@@ -427,7 +427,7 @@
     here = [sent] + [along(sent, "col", d, True) for d in (1, -1, 2)]
     before = [along(x, "agg", 1) for x in here]
     others = (1, 2, 3)
-    second = along(before[0], "agg", 1)
+    second = along(sent, "agg", 2)
     further = [second] + [along(second, "col", d, True, others) for d in (1, -1)] + [along(before[3], "agg", 1)]
     factor = call(
         sweep_kernel,

time: 101 us -> 96.9 us (0.959)
  waiting for transfers between devices: 33.9 us -> 30.5 us
  local copies, waits for them, and re-layouts: 4.16 us -> 1.42 us
  Pallas kernels: 21.1 us -> 23.1 us
    ppermute x14, waiting for transfers between devices: 33.8 us -> 30.5 us  [along(): lax.ppermute(block, axis, [pair for pair in pairs if sources is None or p...]
    unnamed x16 -> x10, local copies, waits for them, and re-layouts: 4.16 us -> 1.42 us
    pallas_call x1, Pallas kernels: 0.82 us -> 2.82 us  [on_device(): call(pack_kernel, [SMEM] * 2 + [VMEM], array(halo_shape, BF16), VMEM, [],...]
where the time goes in v4:
time: 96.9 us; the launch traced here: 95.3 us
  starting transfers between devices  39.4 us (41%)
  waiting for transfers between devices  30.5 us (31%)
  Pallas kernels  23.1 us (24%)
  local copies, waits for them, and re-layouts  1.42 us (1%)
    ppermute x14, starting transfers between devices, along(): lax.ppermute(block, axis, [pair for pair in pairs if sources is None or p...  38 us
    ppermute x14, waiting for transfers between devices, along(): lax.ppermute(block, axis, [pair for pair in pairs if sources is None or p...  30.5 us
    pallas_call x1, Pallas kernels, on_device(): call(sweep_kernel, [SMEM] * 2 + [VMEM] + [ANY] * 12, array(four, F32), VM...  9.01 us
    pallas_call x1, Pallas kernels, on_device(): call(close_kernel, [SMEM] * 4 + [VMEM] * 2, (array((SPARE + 1, width, wid...  4.22 us
    pallas_call x1, Pallas kernels, on_device(): call(distant_kernel, [SMEM] * 4 + [VMEM] * 5, (array(four, F32), array(fo...  3.04 us
    pallas_call x1, Pallas kernels, on_device(): call(pack_kernel, [SMEM] * 2 + [VMEM], array(halo_shape, BF16), VMEM, [],...  2.82 us
    pallas_call x1, Pallas kernels, on_device(): call(plan_kernel, [SMEM] * 4, array((PLAN,), jnp.int32), SMEM, [pltpu.SME...  2.28 us
  transfers between devices with their start and end apart: 16, of which 12 were waited for; matrix products, arithmetic and copies ran while one was open for 0% of the time, Pallas kernels for 7%

profile of v4, /device:TPU:6, one launch (start us, length us, event | category | flops | bytes accessed | tf_op | source)
XLA Modules:
  0.0 95.3 jit_solution(462270619740438182)
XLA Ops:
  0.7 2.8 %pack.1 = bf16[4624,128]{1,0:T(8,128)(2,1)} custom-call(s32[16]{0:T(128)} %labels.5, s32[4,4]{1,0:T(4,128)} %pattern.7, bf16[16,192,192]{2,1,0:T(8,128)(2,1)} %tiles.1), custom_call_target="tpu_custom_call" | custom-call | tf_op jit(solution)/shard_map/pack/pallas_call | solution.py:375
  3.5 7.5 %collective-permute-start.1 = (bf16[4624,128]{1,0:T(8,128)(2,1)}, bf16[4624,128]{1,0:T(8,128)(2,1)S(1)}, u32[]{:S(2)}, u32[]{:S(2)}) collective-permute-start(bf16[4624,128]{1,0:T(8,128)(2,1)} %pack.1), channel_id=1, source_target_pairs={{4,0},{8,4},{12,8},{16,12},{20,16},{24,20},{28,24},{32,28},{36,32}... | collective-permute-start | bytes 3551240 | tf_op jit(solution)/shard_map/ppermute | solution.py:348
  11.0 1.9 %collective-permute-start = (bf16[4624,128]{1,0:T(8,128)(2,1)}, bf16[4624,128]{1,0:T(8,128)(2,1)}, u32[]{:S(2)}, u32[]{:S(2)}) collective-permute-start(bf16[4624,128]{1,0:T(8,128)(2,1)} %pack.1), channel_id=1, source_target_pairs={{0,4},{4,8},{8,12},{12,16},{16,20},{20,24},{24,28},{28,32},{32,36}... | collective-permute-start | bytes 3551240 | tf_op jit(solution)/shard_map/ppermute | solution.py:348
  13.0 1.4 %copy-done.1 = bf16[16,192,192]{2,1,0:T(8,128)(2,1)S(1)} copy-done((bf16[16,192,192]{2,1,0:T(8,128)(2,1)S(1)}, bf16[16,192,192]{2,1,0:T(8,128)(2,1)}, u32[]{:S(2)}) %copy-start.1) | copy-done | bytes 1179672
  14.4 4.2 %close.1 = (f32[17,192,192]{2,1,0:T(8,128)S(1)}, bf16[16,192,192]{2,1,0:T(8,128)(2,1)S(1)}) custom-call(s32[2]{0:T(128)S(1)} %pad_add_fusion.ids, s32[16]{0:T(128)S(1)} %bitcast.12, s32[16]{0:T(128)S(1)} %copy-done.3, s32[4,4]{1,0:T(4,128)S(1)} %copy-done.2, bf16[16,192,192]{2,1,0:T(8,128)(2,1)S(1)} %bitcast.10, bf16[16,192,192]{2,1,0:T(8,128)(2,1)S(1)} %copy-done.1), custom_call_target="tpu_custom_call" | custom-call | tf_op jit(solution)/shard_map/close/pallas_call | solution.py:379
  18.6 6.4 %collective-permute-done.1.right = bf16[4624,128]{1,0:T(8,128)(2,1)S(1)} collective-permute-done((bf16[4624,128]{1,0:T(8,128)(2,1)}, bf16[4624,128]{1,0:T(8,128)(2,1)S(1)}, u32[]{:S(2)}, u32[]{:S(2)}) %collective-permute-start.1) | collective-permute-done | bytes 1183776 | tf_op jit(solution)/shard_map/ppermute | solution.py:348
  25.0 5.9 %collective-permute-done.left = bf16[4624,128]{1,0:T(8,128)(2,1)} collective-permute-done((bf16[4624,128]{1,0:T(8,128)(2,1)}, bf16[4624,128]{1,0:T(8,128)(2,1)}, u32[]{:S(2)}, u32[]{:S(2)}) %collective-permute-start) | collective-permute-done | bytes 1183776 | tf_op jit(solution)/shard_map/ppermute | solution.py:348
  30.9 3.0 %distant.1 = (f32[4,192,192]{2,1,0:T(8,128)S(1)}, bf16[4,288,128]{2,1,0:T(8,128)(2,1)S(1)}, bf16[4,288,128]{2,1,0:T(8,128)(2,1)S(1)}, s32[16]{0:T(128)S(1)}) custom-call(s32[2]{0:T(128)S(1)} %pad_add_fusion.ids, s32[16]{0:T(128)S(1)} %bitcast.13, s32[16]{0:T(128)S(1)} %copy-done.3, s32[4,4]{1,0:T(4,128)S(1)} %copy-done.2, ...), custom_call_target="tpu_custom_call" | custom-call | tf_op jit(solution)/shard_map/distant/pallas_call | solution.py:388
  34.0 0.7 collective-permute-start.3
  34.7 0.7 collective-permute-start.4
  35.4 1.9 %collective-permute-start.2 = (s32[16]{0:T(128)S(1)}, s32[16]{0:T(128)S(1)}, u32[]{:S(2)}, u32[]{:S(2)}) collective-permute-start(s32[16]{0:T(128)S(1)} %get-tuple-element.13.near), channel_id=1, source_target_pairs={{0,4},{4,8},{8,12},{12,16},{16,20},{20,24},{24,28},{28,32},{32,36}... | collective-permute-start | bytes 200 | tf_op jit(solution)/shard_map/ppermute | solution.py:348
  37.3 5.1 %collective-permute-done.2.far = s32[16]{0:T(128)S(1)} collective-permute-done((s32[16]{0:T(128)S(1)}, s32[16]{0:T(128)S(1)}, u32[]{:S(2)}, u32[]{:S(2)}) %collective-permute-start.2) | collective-permute-done | bytes 96 | tf_op jit(solution)/shard_map/ppermute | solution.py:348
  42.4 2.3 %plan.1 = s32[256]{0:T(256)S(1)} custom-call(s32[2]{0:T(128)S(1)} %pad_add_fusion.ids, s32[4,4]{1,0:T(4,128)S(1)} %copy-done.2, s32[16]{0:T(128)S(1)} %get-tuple-element.13.near, s32[16]{0:T(128)S(1)} %collective-permute-done.2.far), custom_call_target="tpu_custom_call" | custom-call | tf_op jit(solution)/shard_map/plan/pallas_call | solution.py:408
  44.7 1.7 %combine.1 = (f32[4,192,192]{2,1,0:T(8,128)}, bf16[4,288,128]{2,1,0:T(8,128)(2,1)S(1)}, f32[4,192,192]{2,1,0:T(8,128)S(1)}) custom-call(s32[256]{0:T(256)S(1)} %plan.1, f32[4,192,192]{2,1,0:T(8,128)S(1)} %get-tuple-element.14.mine, bf16[4,288,128]{2,1,0:T(8,128)(2,1)S(1)} %collective-permute-done.3.ahead, bf16[4,288,128]{2,1,0:T(8,128)(2,1)S(1)} %collective-permute-done.4.behind), custom_call_target="tpu_custom_call" | custom-call | tf_op jit(solution)/shard_map/combine/pallas_call | solution.py:417
  46.4 10.1 %collective-permute-start.8 = (bf16[4,288,128]{2,1,0:T(8,128)(2,1)S(1)}, bf16[4,288,128]{2,1,0:T(8,128)(2,1)S(1)}, u32[]{:S(2)}, u32[]{:S(2)}) collective-permute-start(bf16[4,288,128]{2,1,0:T(8,128)(2,1)S(1)} %get-tuple-element.19.refs_8_), channel_id=1, source_target_pairs={{0,2},{1,3},{2,0},{3,1},{4,6},{5,7},{6,4},{7,5},{8,10},{9,11},{10,... | collective-permute-start | bytes 884744 | tf_op jit(solution)/shard_map/ppermute | solution.py:348
  56.5 2.6 %collective-permute-start.14 = (bf16[4,288,128]{2,1,0:T(8,128)(2,1)S(1)}, bf16[4,288,128]{2,1,0:T(8,128)(2,1)S(1)}, u32[]{:S(2)}, u32[]{:S(2)}) collective-permute-start(bf16[4,288,128]{2,1,0:T(8,128)(2,1)S(1)} %get-tuple-element.19.refs_8_), channel_id=1, source_target_pairs={{0,3},{1,0},{2,1},{3,2},{4,7},{5,4},{6,5},{7,6},{8,11},{9,8},{10,9... | collective-permute-start | bytes 884744 | tf_op jit(solution)/shard_map/ppermute | solution.py:348
  59.1 1.9 %collective-permute-start.5 = (bf16[4,288,128]{2,1,0:T(8,128)(2,1)S(1)}, bf16[4,288,128]{2,1,0:T(8,128)(2,1)S(1)}, u32[]{:S(2)}, u32[]{:S(2)}) collective-permute-start(bf16[4,288,128]{2,1,0:T(8,128)(2,1)S(1)} %get-tuple-element.19.refs_8_), channel_id=1, source_target_pairs={{0,8},{4,12},{8,16},{12,20},{16,24},{20,28},{24,32},{28,36},{32,40... | collective-permute-start | bytes 884744 | tf_op jit(solution)/shard_map/ppermute | solution.py:348
  61.0 1.9 %collective-permute-start.11 = (bf16[4,288,128]{2,1,0:T(8,128)(2,1)S(1)}, bf16[4,288,128]{2,1,0:T(8,128)(2,1)S(1)}, u32[]{:S(2)}, u32[]{:S(2)}) collective-permute-start(bf16[4,288,128]{2,1,0:T(8,128)(2,1)S(1)} %get-tuple-element.19.refs_8_), channel_id=1, source_target_pairs={{0,4},{4,8},{8,12},{12,16},{16,20},{20,24},{24,28},{28,32},{32,36}... | collective-permute-start | bytes 884744 | tf_op jit(solution)/shard_map/ppermute | solution.py:348
  63.2 1.9 %collective-permute-start.9 = (bf16[4,288,128]{2,1,0:T(8,128)(2,1)S(1)}, bf16[4,288,128]{2,1,0:T(8,128)(2,1)S(1)}, u32[]{:S(2)}, u32[]{:S(2)}) collective-permute-start(bf16[4,288,128]{2,1,0:T(8,128)(2,1)S(1)} %collective-permute-done.8.refs_11_), channel_id=1, source_target_pairs={{0,4},{4,8},{8,12},{12,16},{16,20},{20,24},{24,28},{28,32},{32,36}... | collective-permute-start | bytes 884744 | tf_op jit(solution)/shard_map/ppermute | solution.py:348
  65.2 2.1 %collective-permute-done.14.refs_10_ = bf16[4,288,128]{2,1,0:T(8,128)(2,1)S(1)} collective-permute-done((bf16[4,288,128]{2,1,0:T(8,128)(2,1)S(1)}, bf16[4,288,128]{2,1,0:T(8,128)(2,1)S(1)}, u32[]{:S(2)}, u32[]{:S(2)}) %collective-permute-start.14) | collective-permute-done | bytes 294944 | tf_op jit(solution)/shard_map/ppermute | solution.py:348
  67.3 1.9 %collective-permute-start.15 = (bf16[4,288,128]{2,1,0:T(8,128)(2,1)S(1)}, bf16[4,288,128]{2,1,0:T(8,128)(2,1)S(1)}, u32[]{:S(2)}, u32[]{:S(2)}) collective-permute-start(bf16[4,288,128]{2,1,0:T(8,128)(2,1)S(1)} %collective-permute-done.14.refs_10_), channel_id=1, source_target_pairs={{0,4},{4,8},{8,12},{12,16},{16,20},{20,24},{24,28},{28,32},{32,36}... | collective-permute-start | bytes 884744 | tf_op jit(solution)/shard_map/ppermute | solution.py:348
  69.2 1.9 %collective-permute-start.13 = (bf16[4,288,128]{2,1,0:T(8,128)(2,1)S(1)}, bf16[4,288,128]{2,1,0:T(8,128)(2,1)S(1)}, u32[]{:S(2)}, u32[]{:S(2)}) collective-permute-start(bf16[4,288,128]{2,1,0:T(8,128)(2,1)S(1)} %collective-permute-done.12.refs_9_), channel_id=1, source_target_pairs={{0,4},{4,8},{8,12},{12,16},{16,20},{20,24},{24,28},{28,32},{32,36}... | collective-permute-start | bytes 884744 | tf_op jit(solution)/shard_map/ppermute | solution.py:348
  71.1 0.5 collective-permute-done.5.refs_0_
  71.6 1.3 %collective-permute-start.7 = (bf16[4,288,128]{2,1,0:T(8,128)(2,1)S(1)}, bf16[4,288,128]{2,1,0:T(8,128)(2,1)S(1)}, u32[]{:S(2)}, u32[]{:S(2)}) collective-permute-start(bf16[4,288,128]{2,1,0:T(8,128)(2,1)S(1)} %collective-permute-done.5.refs_0_), channel_id=1, source_target_pairs={{1,0},{2,1},{3,2},{5,4},{6,5},{7,6},{9,8},{10,9},{11,10},{13,12},{... | collective-permute-start | bytes 884744 | tf_op jit(solution)/shard_map/ppermute | solution.py:348
  73.0 1.3 %collective-permute-start.6 = (bf16[4,288,128]{2,1,0:T(8,128)(2,1)S(1)}, bf16[4,288,128]{2,1,0:T(8,128)(2,1)S(1)}, u32[]{:S(2)}, u32[]{:S(2)}) collective-permute-start(bf16[4,288,128]{2,1,0:T(8,128)(2,1)S(1)} %collective-permute-done.5.refs_0_), channel_id=1, source_target_pairs={{1,2},{2,3},{3,0},{5,6},{6,7},{7,4},{9,10},{10,11},{11,8},{13,14},... | collective-permute-start | bytes 884744 | tf_op jit(solution)/shard_map/ppermute | solution.py:348
  74.2 1.9 %collective-permute-done.9.refs_7_ = bf16[4,288,128]{2,1,0:T(8,128)(2,1)S(1)} collective-permute-done((bf16[4,288,128]{2,1,0:T(8,128)(2,1)S(1)}, bf16[4,288,128]{2,1,0:T(8,128)(2,1)S(1)}, u32[]{:S(2)}, u32[]{:S(2)}) %collective-permute-start.9) | collective-permute-done | bytes 294944 | tf_op jit(solution)/shard_map/ppermute | solution.py:348
  76.1 1.9 %collective-permute-start.10 = (bf16[4,288,128]{2,1,0:T(8,128)(2,1)S(1)}, bf16[4,288,128]{2,1,0:T(8,128)(2,1)S(1)}, u32[]{:S(2)}, u32[]{:S(2)}) collective-permute-start(bf16[4,288,128]{2,1,0:T(8,128)(2,1)S(1)} %collective-permute-done.9.refs_7_), channel_id=1, source_target_pairs={{0,4},{4,8},{8,12},{12,16},{16,20},{20,24},{24,28},{28,32},{32,36}... | collective-permute-start | bytes 884744 | tf_op jit(solution)/shard_map/ppermute | solution.py:348
  78.0 1.2 %collective-permute-done.15.refs_6_ = bf16[4,288,128]{2,1,0:T(8,128)(2,1)S(1)} collective-permute-done((bf16[4,288,128]{2,1,0:T(8,128)(2,1)S(1)}, bf16[4,288,128]{2,1,0:T(8,128)(2,1)S(1)}, u32[]{:S(2)}, u32[]{:S(2)}) %collective-permute-start.15) | collective-permute-done | bytes 294944 | tf_op jit(solution)/shard_map/ppermute | solution.py:348
  79.3 3.2 %collective-permute-done.13.refs_5_ = bf16[4,288,128]{2,1,0:T(8,128)(2,1)S(1)} collective-permute-done((bf16[4,288,128]{2,1,0:T(8,128)(2,1)S(1)}, bf16[4,288,128]{2,1,0:T(8,128)(2,1)S(1)}, u32[]{:S(2)}, u32[]{:S(2)}) %collective-permute-start.13) | collective-permute-done | bytes 294944 | tf_op jit(solution)/shard_map/ppermute | solution.py:348
  82.4 2.4 %collective-permute-done.6.refs_1_ = bf16[4,288,128]{2,1,0:T(8,128)(2,1)S(1)} collective-permute-done((bf16[4,288,128]{2,1,0:T(8,128)(2,1)S(1)}, bf16[4,288,128]{2,1,0:T(8,128)(2,1)S(1)}, u32[]{:S(2)}, u32[]{:S(2)}) %collective-permute-start.6) | collective-permute-done | bytes 294944 | tf_op jit(solution)/shard_map/ppermute | solution.py:348
  84.9 1.4 %collective-permute-done.10.refs_3_ = bf16[4,288,128]{2,1,0:T(8,128)(2,1)S(1)} collective-permute-done((bf16[4,288,128]{2,1,0:T(8,128)(2,1)S(1)}, bf16[4,288,128]{2,1,0:T(8,128)(2,1)S(1)}, u32[]{:S(2)}, u32[]{:S(2)}) %collective-permute-start.10) | collective-permute-done | bytes 294944 | tf_op jit(solution)/shard_map/ppermute | solution.py:348
  86.3 9.0 %sweep.1 = f32[4,192,192]{2,1,0:T(8,128)} custom-call(s32[2]{0:T(128)S(1)} %pad_add_fusion.ids, s32[256]{0:T(256)S(1)} %plan.1, f32[4,192,192]{2,1,0:T(8,128)S(1)} %get-tuple-element.18.coarse, bf16[4,288,128]{2,1,0:T(8,128)(2,1)S(1)} %collective-permute-done.5.refs_0_, bf16[4,288,128]{2,1,0:T(8,128)(2,1)S(1)} %collective-permute-done.6.refs_1_, ...), custom_call_target="tpu_custom_call" | custom-call | tf_op jit(solution)/shard_map/sweep/pallas_call | solution.py:432
  (17 shorter events, 0.5 us)
Async XLA Ops:
  0.6 12.3 %copy-start.2 = (s32[4,4]{1,0:T(4,128)S(1)}, s32[4,4]{1,0:T(4,128)}, u32[]{:S(2)}) copy-start(s32[4,4]{1,0:T(4,128)} %pattern.7) | copy-start | bytes 196
  0.6 12.3 %copy-start.3 = (s32[16]{0:T(128)S(1)}, s32[16]{0:T(128)}, u32[]{:S(2)}) copy-start(s32[16]{0:T(128)} %labels.5) | copy-start | bytes 196
  0.7 12.3 %copy-start.4 = (s32[16,1]{0,1:T(1,128)S(1)}, s32[16,1]{0,1:T(1,128)}, u32[]{:S(2)}) copy-start(s32[16,1]{0,1:T(1,128)} %param.6) | copy-start | bytes 196
  0.7 12.3 %copy-start = (bf16[16,1,192,192]{3,2,1,0:T(8,128)(2,1)S(1)}, bf16[16,1,192,192]{3,2,1,0:T(8,128)(2,1)}, u32[]{:S(2)}) copy-start(bf16[16,1,192,192]{3,2,1,0:T(8,128)(2,1)} %param.5) | copy-start | bytes 3538948
  3.5 21.5 %collective-permute-start.1 = (bf16[4624,128]{1,0:T(8,128)(2,1)}, bf16[4624,128]{1,0:T(8,128)(2,1)S(1)}, u32[]{:S(2)}, u32[]{:S(2)}) collective-permute-start(bf16[4624,128]{1,0:T(8,128)(2,1)} %pack.1), channel_id=1, source_target_pairs={{4,0},{8,4},{12,8},{16,12},{20,16},{24,20},{28,24},{32,28},{36,32}... | collective-permute-start | bytes 3551240 | tf_op jit(solution)/shard_map/ppermute | solution.py:348
  11.0 20.0 %collective-permute-start = (bf16[4624,128]{1,0:T(8,128)(2,1)}, bf16[4624,128]{1,0:T(8,128)(2,1)}, u32[]{:S(2)}, u32[]{:S(2)}) collective-permute-start(bf16[4624,128]{1,0:T(8,128)(2,1)} %pack.1), channel_id=1, source_target_pairs={{0,4},{4,8},{8,12},{12,16},{16,20},{20,24},{24,28},{28,32},{32,36}... | collective-permute-start | bytes 3551240 | tf_op jit(solution)/shard_map/ppermute | solution.py:348
  13.0 1.4 %copy-start.1 = (bf16[16,192,192]{2,1,0:T(8,128)(2,1)S(1)}, bf16[16,192,192]{2,1,0:T(8,128)(2,1)}, u32[]{:S(2)}) copy-start(bf16[16,192,192]{2,1,0:T(8,128)(2,1)} %tiles.1) | copy-start | bytes 3538948
  34.0 10.7 %collective-permute-start.3 = (bf16[4,288,128]{2,1,0:T(8,128)(2,1)S(1)}, bf16[4,288,128]{2,1,0:T(8,128)(2,1)S(1)}, u32[]{:S(2)}, u32[]{:S(2)}) collective-permute-start(bf16[4,288,128]{2,1,0:T(8,128)(2,1)S(1)} %get-tuple-element.15), channel_id=1, source_target_pairs={{1,2},{2,3},{3,1},{5,6},{6,7},{7,5},{9,10},{10,11},{11,9},{13,14},... | collective-permute-start | bytes 884744 | tf_op jit(solution)/shard_map/ppermute | solution.py:405
  34.7 10.0 %collective-permute-start.4 = (bf16[4,288,128]{2,1,0:T(8,128)(2,1)S(1)}, bf16[4,288,128]{2,1,0:T(8,128)(2,1)S(1)}, u32[]{:S(2)}, u32[]{:S(2)}) collective-permute-start(bf16[4,288,128]{2,1,0:T(8,128)(2,1)S(1)} %get-tuple-element.16), channel_id=1, source_target_pairs={{1,3},{2,1},{3,2},{5,7},{6,5},{7,6},{9,11},{10,9},{11,10},{13,15},... | collective-permute-start | bytes 884744 | tf_op jit(solution)/shard_map/ppermute | solution.py:406
  35.4 7.0 %collective-permute-start.2 = (s32[16]{0:T(128)S(1)}, s32[16]{0:T(128)S(1)}, u32[]{:S(2)}, u32[]{:S(2)}) collective-permute-start(s32[16]{0:T(128)S(1)} %get-tuple-element.13.near), channel_id=1, source_target_pairs={{0,4},{4,8},{8,12},{12,16},{16,20},{20,24},{24,28},{28,32},{32,36}... | collective-permute-start | bytes 200 | tf_op jit(solution)/shard_map/ppermute | solution.py:348
  46.4 16.8 %collective-permute-start.8 = (bf16[4,288,128]{2,1,0:T(8,128)(2,1)S(1)}, bf16[4,288,128]{2,1,0:T(8,128)(2,1)S(1)}, u32[]{:S(2)}, u32[]{:S(2)}) collective-permute-start(bf16[4,288,128]{2,1,0:T(8,128)(2,1)S(1)} %get-tuple-element.19.refs_8_), channel_id=1, source_target_pairs={{0,2},{1,3},{2,0},{3,1},{4,6},{5,7},{6,4},{7,5},{8,10},{9,11},{10,... | collective-permute-start | bytes 884744 | tf_op jit(solution)/shard_map/ppermute | solution.py:348
  56.5 10.8 %collective-permute-start.14 = (bf16[4,288,128]{2,1,0:T(8,128)(2,1)S(1)}, bf16[4,288,128]{2,1,0:T(8,128)(2,1)S(1)}, u32[]{:S(2)}, u32[]{:S(2)}) collective-permute-start(bf16[4,288,128]{2,1,0:T(8,128)(2,1)S(1)} %get-tuple-element.19.refs_8_), channel_id=1, source_target_pairs={{0,3},{1,0},{2,1},{3,2},{4,7},{5,4},{6,5},{7,6},{8,11},{9,8},{10,9... | collective-permute-start | bytes 884744 | tf_op jit(solution)/shard_map/ppermute | solution.py:348
  59.1 10.1 %collective-permute-start.12 = (bf16[4,288,128]{2,1,0:T(8,128)(2,1)S(1)}, bf16[4,288,128]{2,1,0:T(8,128)(2,1)S(1)}, u32[]{:S(2)}, u32[]{:S(2)}) collective-permute-start(bf16[4,288,128]{2,1,0:T(8,128)(2,1)S(1)} %get-tuple-element.19.refs_8_), channel_id=1, source_target_pairs={{0,1},{1,2},{2,3},{3,0},{4,5},{5,6},{6,7},{7,4},{8,9},{9,10},{10,1... | collective-permute-start | bytes 884744 | tf_op jit(solution)/shard_map/ppermute | solution.py:348
  59.1 12.5 %collective-permute-start.5 = (bf16[4,288,128]{2,1,0:T(8,128)(2,1)S(1)}, bf16[4,288,128]{2,1,0:T(8,128)(2,1)S(1)}, u32[]{:S(2)}, u32[]{:S(2)}) collective-permute-start(bf16[4,288,128]{2,1,0:T(8,128)(2,1)S(1)} %get-tuple-element.19.refs_8_), channel_id=1, source_target_pairs={{0,8},{4,12},{8,16},{12,20},{16,24},{20,28},{24,32},{28,36},{32,40... | collective-permute-start | bytes 884744 | tf_op jit(solution)/shard_map/ppermute | solution.py:348
  61.0 12.0 %collective-permute-start.11 = (bf16[4,288,128]{2,1,0:T(8,128)(2,1)S(1)}, bf16[4,288,128]{2,1,0:T(8,128)(2,1)S(1)}, u32[]{:S(2)}, u32[]{:S(2)}) collective-permute-start(bf16[4,288,128]{2,1,0:T(8,128)(2,1)S(1)} %get-tuple-element.19.refs_8_), channel_id=1, source_target_pairs={{0,4},{4,8},{8,12},{12,16},{16,20},{20,24},{24,28},{28,32},{32,36}... | collective-permute-start | bytes 884744 | tf_op jit(solution)/shard_map/ppermute | solution.py:348
  63.2 12.9 %collective-permute-start.9 = (bf16[4,288,128]{2,1,0:T(8,128)(2,1)S(1)}, bf16[4,288,128]{2,1,0:T(8,128)(2,1)S(1)}, u32[]{:S(2)}, u32[]{:S(2)}) collective-permute-start(bf16[4,288,128]{2,1,0:T(8,128)(2,1)S(1)} %collective-permute-done.8.refs_11_), channel_id=1, source_target_pairs={{0,4},{4,8},{8,12},{12,16},{16,20},{20,24},{24,28},{28,32},{32,36}... | collective-permute-start | bytes 884744 | tf_op jit(solution)/shard_map/ppermute | solution.py:348
  67.3 12.0 %collective-permute-start.15 = (bf16[4,288,128]{2,1,0:T(8,128)(2,1)S(1)}, bf16[4,288,128]{2,1,0:T(8,128)(2,1)S(1)}, u32[]{:S(2)}, u32[]{:S(2)}) collective-permute-start(bf16[4,288,128]{2,1,0:T(8,128)(2,1)S(1)} %collective-permute-done.14.refs_10_), channel_id=1, source_target_pairs={{0,4},{4,8},{8,12},{12,16},{16,20},{20,24},{24,28},{28,32},{32,36}... | collective-permute-start | bytes 884744 | tf_op jit(solution)/shard_map/ppermute | solution.py:348
  69.2 13.2 %collective-permute-start.13 = (bf16[4,288,128]{2,1,0:T(8,128)(2,1)S(1)}, bf16[4,288,128]{2,1,0:T(8,128)(2,1)S(1)}, u32[]{:S(2)}, u32[]{:S(2)}) collective-permute-start(bf16[4,288,128]{2,1,0:T(8,128)(2,1)S(1)} %collective-permute-done.12.refs_9_), channel_id=1, source_target_pairs={{0,4},{4,8},{8,12},{12,16},{16,20},{20,24},{24,28},{28,32},{32,36}... | collective-permute-start | bytes 884744 | tf_op jit(solution)/shard_map/ppermute | solution.py:348
  71.6 10.8 %collective-permute-start.7 = (bf16[4,288,128]{2,1,0:T(8,128)(2,1)S(1)}, bf16[4,288,128]{2,1,0:T(8,128)(2,1)S(1)}, u32[]{:S(2)}, u32[]{:S(2)}) collective-permute-start(bf16[4,288,128]{2,1,0:T(8,128)(2,1)S(1)} %collective-permute-done.5.refs_0_), channel_id=1, source_target_pairs={{1,0},{2,1},{3,2},{5,4},{6,5},{7,6},{9,8},{10,9},{11,10},{13,12},{... | collective-permute-start | bytes 884744 | tf_op jit(solution)/shard_map/ppermute | solution.py:348
  73.0 11.9 %collective-permute-start.6 = (bf16[4,288,128]{2,1,0:T(8,128)(2,1)S(1)}, bf16[4,288,128]{2,1,0:T(8,128)(2,1)S(1)}, u32[]{:S(2)}, u32[]{:S(2)}) collective-permute-start(bf16[4,288,128]{2,1,0:T(8,128)(2,1)S(1)} %collective-permute-done.5.refs_0_), channel_id=1, source_target_pairs={{1,2},{2,3},{3,0},{5,6},{6,7},{7,4},{9,10},{10,11},{11,8},{13,14},... | collective-permute-start | bytes 884744 | tf_op jit(solution)/shard_map/ppermute | solution.py:348
  76.1 10.1 %collective-permute-start.10 = (bf16[4,288,128]{2,1,0:T(8,128)(2,1)S(1)}, bf16[4,288,128]{2,1,0:T(8,128)(2,1)S(1)}, u32[]{:S(2)}, u32[]{:S(2)}) collective-permute-start(bf16[4,288,128]{2,1,0:T(8,128)(2,1)S(1)} %collective-permute-done.9.refs_7_), channel_id=1, source_target_pairs={{0,4},{4,8},{8,12},{12,16},{16,20},{20,24},{24,28},{28,32},{32,36}... | collective-permute-start | bytes 884744 | tf_op jit(solution)/shard_map/ppermute | solution.py:348

commit v5 on v4

--- a/solution.py
+++ b/solution.py
@@ -45,7 +45,12 @@
     ref[half:, 128:] = packed[width:, rest:]
 
 
-def pack_kernel(labels, pattern, tiles, packed):
+def pack_kernel(labels, pattern, source, packed, tiles, sems):
+    copies = []
+    for k in range(4):
+        part = pl.ds(4 * k, 4)
+        copies.append(pltpu.make_async_copy(source.at[part], tiles.at[part], sems.at[k]))
+        copies[-1].start()
     count, size = tiles.shape[0], tiles.shape[1] * tiles.shape[2] // 128
     line, lane = iota((16, 128), 0), iota((16, 128), 1)
     about = jnp.zeros((16, 128), F32)
@@ -57,6 +62,8 @@
             about = jnp.where((line == 1) & (lane == 4 * r + q), offset.astype(F32), about)
     packed[count * size :] = about.astype(BF16)
     for i in range(count):
+        if i % 4 == 0:
+            copies[i // 4].wait()
         store_packed(packed.at[pl.ds(i * size, size)], tiles[i])
 
 
@@ -256,13 +263,9 @@
 
 
 def sweep_kernel(ids, plan, coarse, *refs):
-    pieces, (out, arrived, first, work, high, low, pivots, pivots_next, sems) = refs[:12], refs[12:]
+    pieces, (out, first, work, high, low, pivots, pivots_next) = refs[:12], refs[12:]
     col = ids[1]
     width = coarse.shape[-1]
-    copies = []
-    for k, piece in enumerate(pieces):
-        copies.append(pltpu.make_async_copy(piece, arrived.at[pl.ds(4 * k, 4)], sems.at[k]))
-        copies[-1].start()
     first[ZERO1] = jnp.zeros((width, width), BF16)
     lines, columns = iota((width, width), 0), iota((width, width), 1)
     upper, lower, equal = columns > lines, lines > columns, lines == columns
@@ -270,11 +273,10 @@
     def reciprocal(tile):
         return 1.0 / jnp.maximum(jnp.sum(jnp.where(equal, tile, 0.0), axis=0, keepdims=True), 1.0)
 
-    for k, copy in enumerate(copies):
-        copy.wait()
+    for k, piece in enumerate(pieces):
         start = ((col + (0, 3, 1, 2)[k % 4]) & 3) * ROWS + k // 4 * 4
         for r in range(4):
-            store_unpacked(first.at[start + r], arrived[4 * k + r], width)
+            store_unpacked(first.at[start + r], piece[r], width)
 
     def prepare(k, carry):
         diagonal = first[4 + k].astype(F32)
@@ -372,9 +374,15 @@
     cols = fine_cols.reshape(-1)
     tiles = fine_tiles.reshape(rows, width, width)
     halo_shape = (rows * packed[0] + 16, 128)
-    halo = call(pack_kernel, [SMEM] * 2 + [VMEM], array(halo_shape, BF16), VMEM, [], "pack", 60)(
-        agg_of, coarse_cols, prolong
-    )
+    halo = call(
+        pack_kernel,
+        [SMEM] * 2 + [ANY],
+        array(halo_shape, BF16),
+        VMEM,
+        [pltpu.VMEM((rows, width, width), BF16), pltpu.SemaphoreType.DMA((4,))],
+        "pack",
+        60,
+    )(agg_of, coarse_cols, prolong)
     left, right = along(halo, "agg", 1), along(halo, "agg", -1)
     total, turned = call(
         close_kernel,
@@ -431,18 +439,16 @@
     further = [second] + [along(second, "col", d, True, others) for d in (1, -1)] + [along(before[3], "agg", 1)]
     factor = call(
         sweep_kernel,
-        [SMEM] * 2 + [VMEM] + [ANY] * 12,
+        [SMEM] * 2 + [VMEM] * 13,
         array(four, F32),
         VMEM,
         [
-            pltpu.VMEM((48, *packed), BF16),
             pltpu.VMEM((65, width, width), BF16),
             pltpu.VMEM((33, width, width), F32),
             pltpu.VMEM((49, width, width), BF16),
             pltpu.VMEM((49, width, width), BF16),
             pltpu.VMEM((8, 1, width), F32),
             pltpu.VMEM((8, 1, width), F32),
-            pltpu.SemaphoreType.DMA((12,)),
         ],
         "sweep",
         34,

time: 96.9 us -> 95.1 us (0.981)
  the two profiles are of different devices: /device:TPU:6 before, /device:TPU:66 now
where the time goes in v5:
time: 95.1 us; the launch traced here: 94.4 us
  starting transfers between devices  45.9 us (48%)
  waiting for transfers between devices  23.7 us (25%)
  Pallas kernels  22.4 us (24%)
  local copies, waits for them, and re-layouts  1.42 us (1%)
    ppermute x14, starting transfers between devices, along(): lax.ppermute(block, axis, [pair for pair in pairs if sources is None or p...  44.5 us
    ppermute x14, waiting for transfers between devices, along(): lax.ppermute(block, axis, [pair for pair in pairs if sources is None or p...  23.7 us
    pallas_call x1, Pallas kernels, on_device(): call(sweep_kernel, [SMEM] * 2 + [VMEM] * 13, array(four, F32), VMEM, [plt...  7.75 us
    pallas_call x1, Pallas kernels, on_device(): call(close_kernel, [SMEM] * 4 + [VMEM] * 2, (array((SPARE + 1, width, wid...  4.22 us
    pallas_call x1, Pallas kernels, on_device(): call(pack_kernel, [SMEM] * 2 + [ANY], array(halo_shape, BF16), VMEM, [plt...  3.34 us
    pallas_call x1, Pallas kernels, on_device(): call(distant_kernel, [SMEM] * 4 + [VMEM] * 5, (array(four, F32), array(fo...  3.04 us
    pallas_call x1, Pallas kernels, on_device(): call(plan_kernel, [SMEM] * 4, array((PLAN,), jnp.int32), SMEM, [pltpu.SME...  2.36 us
  transfers between devices with their start and end apart: 16, of which 7 were waited for; matrix products, arithmetic and copies ran while one was open for 0% of the time, Pallas kernels for 7%

profile of v5, /device:TPU:66, one launch (start us, length us, event | category | flops | bytes accessed | tf_op | source)
XLA Modules:
  0.0 94.4 jit_solution(12730794686715588998)
XLA Ops:
  0.7 3.3 %pack.1 = bf16[4624,128]{1,0:T(8,128)(2,1)} custom-call(s32[16]{0:T(128)} %labels.5, s32[4,4]{1,0:T(4,128)} %pattern.7, bf16[16,192,192]{2,1,0:T(8,128)(2,1)} %source.1), custom_call_target="tpu_custom_call" | custom-call | tf_op jit(solution)/shard_map/pack/pallas_call | solution.py:377
  4.0 1.9 %collective-permute-start.1 = (bf16[4624,128]{1,0:T(8,128)(2,1)}, bf16[4624,128]{1,0:T(8,128)(2,1)S(1)}, u32[]{:S(2)}, u32[]{:S(2)}) collective-permute-start(bf16[4624,128]{1,0:T(8,128)(2,1)} %pack.1), channel_id=1, source_target_pairs={{4,0},{8,4},{12,8},{16,12},{20,16},{24,20},{28,24},{32,28},{36,32}... | collective-permute-start | bytes 3551240 | tf_op jit(solution)/shard_map/ppermute | solution.py:350
  5.9 2.4 %collective-permute-start = (bf16[4624,128]{1,0:T(8,128)(2,1)}, bf16[4624,128]{1,0:T(8,128)(2,1)}, u32[]{:S(2)}, u32[]{:S(2)}) collective-permute-start(bf16[4624,128]{1,0:T(8,128)(2,1)} %pack.1), channel_id=1, source_target_pairs={{0,4},{4,8},{8,12},{12,16},{16,20},{20,24},{24,28},{28,32},{32,36}... | collective-permute-start | bytes 3551240 | tf_op jit(solution)/shard_map/ppermute | solution.py:350
  8.4 0.1 pad_add_fusion.ids
  8.5 0.0 copy-start.1
  8.5 1.4 %copy-done.1 = bf16[16,192,192]{2,1,0:T(8,128)(2,1)S(1)} copy-done((bf16[16,192,192]{2,1,0:T(8,128)(2,1)S(1)}, bf16[16,192,192]{2,1,0:T(8,128)(2,1)}, u32[]{:S(2)}) %copy-start.1) | copy-done | bytes 1179672
  9.9 4.2 %close.1 = (f32[17,192,192]{2,1,0:T(8,128)S(1)}, bf16[16,192,192]{2,1,0:T(8,128)(2,1)S(1)}) custom-call(s32[2]{0:T(128)S(1)} %pad_add_fusion.ids, s32[16]{0:T(128)S(1)} %bitcast.12, s32[16]{0:T(128)S(1)} %copy-done.3, s32[4,4]{1,0:T(4,128)S(1)} %copy-done.2, bf16[16,192,192]{2,1,0:T(8,128)(2,1)S(1)} %bitcast.10, bf16[16,192,192]{2,1,0:T(8,128)(2,1)S(1)} %copy-done.1), custom_call_target="tpu_custom_call" | custom-call | tf_op jit(solution)/shard_map/close/pallas_call | solution.py:387
  14.1 5.9 %collective-permute-done.1.right = bf16[4624,128]{1,0:T(8,128)(2,1)S(1)} collective-permute-done((bf16[4624,128]{1,0:T(8,128)(2,1)}, bf16[4624,128]{1,0:T(8,128)(2,1)S(1)}, u32[]{:S(2)}, u32[]{:S(2)}) %collective-permute-start.1) | collective-permute-done | bytes 1183776 | tf_op jit(solution)/shard_map/ppermute | solution.py:350
  20.0 3.8 %collective-permute-done.left = bf16[4624,128]{1,0:T(8,128)(2,1)} collective-permute-done((bf16[4624,128]{1,0:T(8,128)(2,1)}, bf16[4624,128]{1,0:T(8,128)(2,1)}, u32[]{:S(2)}, u32[]{:S(2)}) %collective-permute-start) | collective-permute-done | bytes 1183776 | tf_op jit(solution)/shard_map/ppermute | solution.py:350
  23.8 3.0 %distant.1 = (f32[4,192,192]{2,1,0:T(8,128)S(1)}, bf16[4,288,128]{2,1,0:T(8,128)(2,1)S(1)}, bf16[4,288,128]{2,1,0:T(8,128)(2,1)S(1)}, s32[16]{0:T(128)S(1)}) custom-call(s32[2]{0:T(128)S(1)} %pad_add_fusion.ids, s32[16]{0:T(128)S(1)} %bitcast.13, s32[16]{0:T(128)S(1)} %copy-done.3, s32[4,4]{1,0:T(4,128)S(1)} %copy-done.2, ...), custom_call_target="tpu_custom_call" | custom-call | tf_op jit(solution)/shard_map/distant/pallas_call | solution.py:396
  26.9 0.7 collective-permute-start.3
  27.6 0.7 collective-permute-start.4
  28.3 1.9 %collective-permute-start.2 = (s32[16]{0:T(128)S(1)}, s32[16]{0:T(128)S(1)}, u32[]{:S(2)}, u32[]{:S(2)}) collective-permute-start(s32[16]{0:T(128)S(1)} %get-tuple-element.13.near), channel_id=1, source_target_pairs={{0,4},{4,8},{8,12},{12,16},{16,20},{20,24},{24,28},{28,32},{32,36}... | collective-permute-start | bytes 200 | tf_op jit(solution)/shard_map/ppermute | solution.py:350
  30.2 3.0 %collective-permute-done.2.far = s32[16]{0:T(128)S(1)} collective-permute-done((s32[16]{0:T(128)S(1)}, s32[16]{0:T(128)S(1)}, u32[]{:S(2)}, u32[]{:S(2)}) %collective-permute-start.2) | collective-permute-done | bytes 96 | tf_op jit(solution)/shard_map/ppermute | solution.py:350
  33.1 2.4 %plan.1 = s32[256]{0:T(256)S(1)} custom-call(s32[2]{0:T(128)S(1)} %pad_add_fusion.ids, s32[4,4]{1,0:T(4,128)S(1)} %copy-done.2, s32[16]{0:T(128)S(1)} %get-tuple-element.13.near, s32[16]{0:T(128)S(1)} %collective-permute-done.2.far), custom_call_target="tpu_custom_call" | custom-call | tf_op jit(solution)/shard_map/plan/pallas_call | solution.py:416
  35.5 0.0 collective-permute-done.4.behind
  35.5 1.7 %combine.1 = (f32[4,192,192]{2,1,0:T(8,128)}, bf16[4,288,128]{2,1,0:T(8,128)(2,1)S(1)}, f32[4,192,192]{2,1,0:T(8,128)S(1)}) custom-call(s32[256]{0:T(256)S(1)} %plan.1, f32[4,192,192]{2,1,0:T(8,128)S(1)} %get-tuple-element.14.mine, bf16[4,288,128]{2,1,0:T(8,128)(2,1)S(1)} %collective-permute-done.3.ahead, bf16[4,288,128]{2,1,0:T(8,128)(2,1)S(1)} %collective-permute-done.4.behind), custom_call_target="tpu_custom_call" | custom-call | tf_op jit(solution)/shard_map/combine/pallas_call | solution.py:425
  37.2 14.2 %collective-permute-start.8 = (bf16[4,288,128]{2,1,0:T(8,128)(2,1)S(1)}, bf16[4,288,128]{2,1,0:T(8,128)(2,1)S(1)}, u32[]{:S(2)}, u32[]{:S(2)}) collective-permute-start(bf16[4,288,128]{2,1,0:T(8,128)(2,1)S(1)} %get-tuple-element.19.refs_8_), channel_id=1, source_target_pairs={{0,2},{1,3},{2,0},{3,1},{4,6},{5,7},{6,4},{7,5},{8,10},{9,11},{10,... | collective-permute-start | bytes 884744 | tf_op jit(solution)/shard_map/ppermute | solution.py:350
  51.4 2.0 %collective-permute-start.14 = (bf16[4,288,128]{2,1,0:T(8,128)(2,1)S(1)}, bf16[4,288,128]{2,1,0:T(8,128)(2,1)S(1)}, u32[]{:S(2)}, u32[]{:S(2)}) collective-permute-start(bf16[4,288,128]{2,1,0:T(8,128)(2,1)S(1)} %get-tuple-element.19.refs_8_), channel_id=1, source_target_pairs={{0,3},{1,0},{2,1},{3,2},{4,7},{5,4},{6,5},{7,6},{8,11},{9,8},{10,9... | collective-permute-start | bytes 884744 | tf_op jit(solution)/shard_map/ppermute | solution.py:350
  53.5 5.0 %collective-permute-start.5 = (bf16[4,288,128]{2,1,0:T(8,128)(2,1)S(1)}, bf16[4,288,128]{2,1,0:T(8,128)(2,1)S(1)}, u32[]{:S(2)}, u32[]{:S(2)}) collective-permute-start(bf16[4,288,128]{2,1,0:T(8,128)(2,1)S(1)} %get-tuple-element.19.refs_8_), channel_id=1, source_target_pairs={{0,8},{4,12},{8,16},{12,20},{16,24},{20,28},{24,32},{28,36},{32,40... | collective-permute-start | bytes 884744 | tf_op jit(solution)/shard_map/ppermute | solution.py:350
  58.5 1.9 %collective-permute-start.11 = (bf16[4,288,128]{2,1,0:T(8,128)(2,1)S(1)}, bf16[4,288,128]{2,1,0:T(8,128)(2,1)S(1)}, u32[]{:S(2)}, u32[]{:S(2)}) collective-permute-start(bf16[4,288,128]{2,1,0:T(8,128)(2,1)S(1)} %get-tuple-element.19.refs_8_), channel_id=1, source_target_pairs={{0,4},{4,8},{8,12},{12,16},{16,20},{20,24},{24,28},{28,32},{32,36}... | collective-permute-start | bytes 884744 | tf_op jit(solution)/shard_map/ppermute | solution.py:350
  60.5 3.5 %collective-permute-start.9 = (bf16[4,288,128]{2,1,0:T(8,128)(2,1)S(1)}, bf16[4,288,128]{2,1,0:T(8,128)(2,1)S(1)}, u32[]{:S(2)}, u32[]{:S(2)}) collective-permute-start(bf16[4,288,128]{2,1,0:T(8,128)(2,1)S(1)} %collective-permute-done.8.refs_11_), channel_id=1, source_target_pairs={{0,4},{4,8},{8,12},{12,16},{16,20},{20,24},{24,28},{28,32},{32,36}... | collective-permute-start | bytes 884744 | tf_op jit(solution)/shard_map/ppermute | solution.py:350
  63.9 0.4 collective-permute-done.14.refs_10_
  64.4 2.0 %collective-permute-start.15 = (bf16[4,288,128]{2,1,0:T(8,128)(2,1)S(1)}, bf16[4,288,128]{2,1,0:T(8,128)(2,1)S(1)}, u32[]{:S(2)}, u32[]{:S(2)}) collective-permute-start(bf16[4,288,128]{2,1,0:T(8,128)(2,1)S(1)} %collective-permute-done.14.refs_10_), channel_id=1, source_target_pairs={{0,4},{4,8},{8,12},{12,16},{16,20},{20,24},{24,28},{28,32},{32,36}... | collective-permute-start | bytes 884744 | tf_op jit(solution)/shard_map/ppermute | solution.py:350
  66.4 5.1 %collective-permute-start.13 = (bf16[4,288,128]{2,1,0:T(8,128)(2,1)S(1)}, bf16[4,288,128]{2,1,0:T(8,128)(2,1)S(1)}, u32[]{:S(2)}, u32[]{:S(2)}) collective-permute-start(bf16[4,288,128]{2,1,0:T(8,128)(2,1)S(1)} %collective-permute-done.12.refs_9_), channel_id=1, source_target_pairs={{0,4},{4,8},{8,12},{12,16},{16,20},{20,24},{24,28},{28,32},{32,36}... | collective-permute-start | bytes 884744 | tf_op jit(solution)/shard_map/ppermute | solution.py:350
  71.5 1.3 %collective-permute-start.7 = (bf16[4,288,128]{2,1,0:T(8,128)(2,1)S(1)}, bf16[4,288,128]{2,1,0:T(8,128)(2,1)S(1)}, u32[]{:S(2)}, u32[]{:S(2)}) collective-permute-start(bf16[4,288,128]{2,1,0:T(8,128)(2,1)S(1)} %collective-permute-done.5.refs_0_), channel_id=1, source_target_pairs={{1,0},{2,1},{3,2},{5,4},{6,5},{7,6},{9,8},{10,9},{11,10},{13,12},{... | collective-permute-start | bytes 884744 | tf_op jit(solution)/shard_map/ppermute | solution.py:350
  72.8 1.3 %collective-permute-start.6 = (bf16[4,288,128]{2,1,0:T(8,128)(2,1)S(1)}, bf16[4,288,128]{2,1,0:T(8,128)(2,1)S(1)}, u32[]{:S(2)}, u32[]{:S(2)}) collective-permute-start(bf16[4,288,128]{2,1,0:T(8,128)(2,1)S(1)} %collective-permute-done.5.refs_0_), channel_id=1, source_target_pairs={{1,2},{2,3},{3,0},{5,6},{6,7},{7,4},{9,10},{10,11},{11,8},{13,14},... | collective-permute-start | bytes 884744 | tf_op jit(solution)/shard_map/ppermute | solution.py:350
  74.1 1.9 %collective-permute-start.10 = (bf16[4,288,128]{2,1,0:T(8,128)(2,1)S(1)}, bf16[4,288,128]{2,1,0:T(8,128)(2,1)S(1)}, u32[]{:S(2)}, u32[]{:S(2)}) collective-permute-start(bf16[4,288,128]{2,1,0:T(8,128)(2,1)S(1)} %collective-permute-done.9.refs_7_), channel_id=1, source_target_pairs={{0,4},{4,8},{8,12},{12,16},{16,20},{20,24},{24,28},{28,32},{32,36}... | collective-permute-start | bytes 884744 | tf_op jit(solution)/shard_map/ppermute | solution.py:350
  76.1 0.3 collective-permute-done.13.refs_5_
  76.4 5.9 %collective-permute-done.7.refs_2_ = bf16[4,288,128]{2,1,0:T(8,128)(2,1)S(1)} collective-permute-done((bf16[4,288,128]{2,1,0:T(8,128)(2,1)S(1)}, bf16[4,288,128]{2,1,0:T(8,128)(2,1)S(1)}, u32[]{:S(2)}, u32[]{:S(2)}) %collective-permute-start.7) | collective-permute-done | bytes 294944 | tf_op jit(solution)/shard_map/ppermute | solution.py:350
  82.3 4.3 %collective-permute-done.6.refs_1_ = bf16[4,288,128]{2,1,0:T(8,128)(2,1)S(1)} collective-permute-done((bf16[4,288,128]{2,1,0:T(8,128)(2,1)S(1)}, bf16[4,288,128]{2,1,0:T(8,128)(2,1)S(1)}, u32[]{:S(2)}, u32[]{:S(2)}) %collective-permute-start.6) | collective-permute-done | bytes 294944 | tf_op jit(solution)/shard_map/ppermute | solution.py:350
  86.7 7.8 %sweep.1 = f32[4,192,192]{2,1,0:T(8,128)} custom-call(s32[2]{0:T(128)S(1)} %pad_add_fusion.ids, s32[256]{0:T(256)S(1)} %plan.1, f32[4,192,192]{2,1,0:T(8,128)S(1)} %get-tuple-element.18.coarse, bf16[4,288,128]{2,1,0:T(8,128)(2,1)S(1)} %collective-permute-done.5.refs_0_, bf16[4,288,128]{2,1,0:T(8,128)(2,1)S(1)} %collective-permute-done.6.refs_1_, ...), custom_call_target="tpu_custom_call" | custom-call | tf_op jit(solution)/shard_map/sweep/pallas_call | solution.py:440
  (17 shorter events, 0.0 us)
Async XLA Ops:
  0.6 7.8 %copy-start.2 = (s32[4,4]{1,0:T(4,128)S(1)}, s32[4,4]{1,0:T(4,128)}, u32[]{:S(2)}) copy-start(s32[4,4]{1,0:T(4,128)} %pattern.7) | copy-start | bytes 196
  0.6 7.8 %copy-start.3 = (s32[16]{0:T(128)S(1)}, s32[16]{0:T(128)}, u32[]{:S(2)}) copy-start(s32[16]{0:T(128)} %labels.5) | copy-start | bytes 196
  0.7 7.8 %copy-start.4 = (s32[16,1]{0,1:T(1,128)S(1)}, s32[16,1]{0,1:T(1,128)}, u32[]{:S(2)}) copy-start(s32[16,1]{0,1:T(1,128)} %param.6) | copy-start | bytes 196
  0.7 7.8 %copy-start = (bf16[16,1,192,192]{3,2,1,0:T(8,128)(2,1)S(1)}, bf16[16,1,192,192]{3,2,1,0:T(8,128)(2,1)}, u32[]{:S(2)}) copy-start(bf16[16,1,192,192]{3,2,1,0:T(8,128)(2,1)} %param.5) | copy-start | bytes 3538948
  4.0 16.0 %collective-permute-start.1 = (bf16[4624,128]{1,0:T(8,128)(2,1)}, bf16[4624,128]{1,0:T(8,128)(2,1)S(1)}, u32[]{:S(2)}, u32[]{:S(2)}) collective-permute-start(bf16[4624,128]{1,0:T(8,128)(2,1)} %pack.1), channel_id=1, source_target_pairs={{4,0},{8,4},{12,8},{16,12},{20,16},{24,20},{28,24},{32,28},{36,32}... | collective-permute-start | bytes 3551240 | tf_op jit(solution)/shard_map/ppermute | solution.py:350
  5.9 17.9 %collective-permute-start = (bf16[4624,128]{1,0:T(8,128)(2,1)}, bf16[4624,128]{1,0:T(8,128)(2,1)}, u32[]{:S(2)}, u32[]{:S(2)}) collective-permute-start(bf16[4624,128]{1,0:T(8,128)(2,1)} %pack.1), channel_id=1, source_target_pairs={{0,4},{4,8},{8,12},{12,16},{16,20},{20,24},{24,28},{28,32},{32,36}... | collective-permute-start | bytes 3551240 | tf_op jit(solution)/shard_map/ppermute | solution.py:350
  8.5 1.4 %copy-start.1 = (bf16[16,192,192]{2,1,0:T(8,128)(2,1)S(1)}, bf16[16,192,192]{2,1,0:T(8,128)(2,1)}, u32[]{:S(2)}) copy-start(bf16[16,192,192]{2,1,0:T(8,128)(2,1)} %source.1) | copy-start | bytes 3538948
  26.9 8.6 %collective-permute-start.3 = (bf16[4,288,128]{2,1,0:T(8,128)(2,1)S(1)}, bf16[4,288,128]{2,1,0:T(8,128)(2,1)S(1)}, u32[]{:S(2)}, u32[]{:S(2)}) collective-permute-start(bf16[4,288,128]{2,1,0:T(8,128)(2,1)S(1)} %get-tuple-element.15), channel_id=1, source_target_pairs={{1,2},{2,3},{3,1},{5,6},{6,7},{7,5},{9,10},{10,11},{11,9},{13,14},... | collective-permute-start | bytes 884744 | tf_op jit(solution)/shard_map/ppermute | solution.py:413
  27.6 8.0 %collective-permute-start.4 = (bf16[4,288,128]{2,1,0:T(8,128)(2,1)S(1)}, bf16[4,288,128]{2,1,0:T(8,128)(2,1)S(1)}, u32[]{:S(2)}, u32[]{:S(2)}) collective-permute-start(bf16[4,288,128]{2,1,0:T(8,128)(2,1)S(1)} %get-tuple-element.16), channel_id=1, source_target_pairs={{1,3},{2,1},{3,2},{5,7},{6,5},{7,6},{9,11},{10,9},{11,10},{13,15},... | collective-permute-start | bytes 884744 | tf_op jit(solution)/shard_map/ppermute | solution.py:414
  28.3 4.9 %collective-permute-start.2 = (s32[16]{0:T(128)S(1)}, s32[16]{0:T(128)S(1)}, u32[]{:S(2)}, u32[]{:S(2)}) collective-permute-start(s32[16]{0:T(128)S(1)} %get-tuple-element.13.near), channel_id=1, source_target_pairs={{0,4},{4,8},{8,12},{12,16},{16,20},{20,24},{24,28},{28,32},{32,36}... | collective-permute-start | bytes 200 | tf_op jit(solution)/shard_map/ppermute | solution.py:350
  37.2 23.2 %collective-permute-start.8 = (bf16[4,288,128]{2,1,0:T(8,128)(2,1)S(1)}, bf16[4,288,128]{2,1,0:T(8,128)(2,1)S(1)}, u32[]{:S(2)}, u32[]{:S(2)}) collective-permute-start(bf16[4,288,128]{2,1,0:T(8,128)(2,1)S(1)} %get-tuple-element.19.refs_8_), channel_id=1, source_target_pairs={{0,2},{1,3},{2,0},{3,1},{4,6},{5,7},{6,4},{7,5},{8,10},{9,11},{10,... | collective-permute-start | bytes 884744 | tf_op jit(solution)/shard_map/ppermute | solution.py:350
  51.4 12.9 %collective-permute-start.14 = (bf16[4,288,128]{2,1,0:T(8,128)(2,1)S(1)}, bf16[4,288,128]{2,1,0:T(8,128)(2,1)S(1)}, u32[]{:S(2)}, u32[]{:S(2)}) collective-permute-start(bf16[4,288,128]{2,1,0:T(8,128)(2,1)S(1)} %get-tuple-element.19.refs_8_), channel_id=1, source_target_pairs={{0,3},{1,0},{2,1},{3,2},{4,7},{5,4},{6,5},{7,6},{8,11},{9,8},{10,9... | collective-permute-start | bytes 884744 | tf_op jit(solution)/shard_map/ppermute | solution.py:350
  53.5 12.9 %collective-permute-start.12 = (bf16[4,288,128]{2,1,0:T(8,128)(2,1)S(1)}, bf16[4,288,128]{2,1,0:T(8,128)(2,1)S(1)}, u32[]{:S(2)}, u32[]{:S(2)}) collective-permute-start(bf16[4,288,128]{2,1,0:T(8,128)(2,1)S(1)} %get-tuple-element.19.refs_8_), channel_id=1, source_target_pairs={{0,1},{1,2},{2,3},{3,0},{4,5},{5,6},{6,7},{7,4},{8,9},{9,10},{10,1... | collective-permute-start | bytes 884744 | tf_op jit(solution)/shard_map/ppermute | solution.py:350
  53.5 18.0 %collective-permute-start.5 = (bf16[4,288,128]{2,1,0:T(8,128)(2,1)S(1)}, bf16[4,288,128]{2,1,0:T(8,128)(2,1)S(1)}, u32[]{:S(2)}, u32[]{:S(2)}) collective-permute-start(bf16[4,288,128]{2,1,0:T(8,128)(2,1)S(1)} %get-tuple-element.19.refs_8_), channel_id=1, source_target_pairs={{0,8},{4,12},{8,16},{12,20},{16,24},{20,28},{24,32},{28,36},{32,40... | collective-permute-start | bytes 884744 | tf_op jit(solution)/shard_map/ppermute | solution.py:350
  58.5 14.3 %collective-permute-start.11 = (bf16[4,288,128]{2,1,0:T(8,128)(2,1)S(1)}, bf16[4,288,128]{2,1,0:T(8,128)(2,1)S(1)}, u32[]{:S(2)}, u32[]{:S(2)}) collective-permute-start(bf16[4,288,128]{2,1,0:T(8,128)(2,1)S(1)} %get-tuple-element.19.refs_8_), channel_id=1, source_target_pairs={{0,4},{4,8},{8,12},{12,16},{16,20},{20,24},{24,28},{28,32},{32,36}... | collective-permute-start | bytes 884744 | tf_op jit(solution)/shard_map/ppermute | solution.py:350
  60.5 13.7 %collective-permute-start.9 = (bf16[4,288,128]{2,1,0:T(8,128)(2,1)S(1)}, bf16[4,288,128]{2,1,0:T(8,128)(2,1)S(1)}, u32[]{:S(2)}, u32[]{:S(2)}) collective-permute-start(bf16[4,288,128]{2,1,0:T(8,128)(2,1)S(1)} %collective-permute-done.8.refs_11_), channel_id=1, source_target_pairs={{0,4},{4,8},{8,12},{12,16},{16,20},{20,24},{24,28},{28,32},{32,36}... | collective-permute-start | bytes 884744 | tf_op jit(solution)/shard_map/ppermute | solution.py:350
  64.4 11.7 %collective-permute-start.15 = (bf16[4,288,128]{2,1,0:T(8,128)(2,1)S(1)}, bf16[4,288,128]{2,1,0:T(8,128)(2,1)S(1)}, u32[]{:S(2)}, u32[]{:S(2)}) collective-permute-start(bf16[4,288,128]{2,1,0:T(8,128)(2,1)S(1)} %collective-permute-done.14.refs_10_), channel_id=1, source_target_pairs={{0,4},{4,8},{8,12},{12,16},{16,20},{20,24},{24,28},{28,32},{32,36}... | collective-permute-start | bytes 884744 | tf_op jit(solution)/shard_map/ppermute | solution.py:350
  66.4 10.0 %collective-permute-start.13 = (bf16[4,288,128]{2,1,0:T(8,128)(2,1)S(1)}, bf16[4,288,128]{2,1,0:T(8,128)(2,1)S(1)}, u32[]{:S(2)}, u32[]{:S(2)}) collective-permute-start(bf16[4,288,128]{2,1,0:T(8,128)(2,1)S(1)} %collective-permute-done.12.refs_9_), channel_id=1, source_target_pairs={{0,4},{4,8},{8,12},{12,16},{16,20},{20,24},{24,28},{28,32},{32,36}... | collective-permute-start | bytes 884744 | tf_op jit(solution)/shard_map/ppermute | solution.py:350
  71.5 10.8 %collective-permute-start.7 = (bf16[4,288,128]{2,1,0:T(8,128)(2,1)S(1)}, bf16[4,288,128]{2,1,0:T(8,128)(2,1)S(1)}, u32[]{:S(2)}, u32[]{:S(2)}) collective-permute-start(bf16[4,288,128]{2,1,0:T(8,128)(2,1)S(1)} %collective-permute-done.5.refs_0_), channel_id=1, source_target_pairs={{1,0},{2,1},{3,2},{5,4},{6,5},{7,6},{9,8},{10,9},{11,10},{13,12},{... | collective-permute-start | bytes 884744 | tf_op jit(solution)/shard_map/ppermute | solution.py:350
  72.8 13.9 %collective-permute-start.6 = (bf16[4,288,128]{2,1,0:T(8,128)(2,1)S(1)}, bf16[4,288,128]{2,1,0:T(8,128)(2,1)S(1)}, u32[]{:S(2)}, u32[]{:S(2)}) collective-permute-start(bf16[4,288,128]{2,1,0:T(8,128)(2,1)S(1)} %collective-permute-done.5.refs_0_), channel_id=1, source_target_pairs={{1,2},{2,3},{3,0},{5,6},{6,7},{7,4},{9,10},{10,11},{11,8},{13,14},... | collective-permute-start | bytes 884744 | tf_op jit(solution)/shard_map/ppermute | solution.py:350
  74.1 12.5 %collective-permute-start.10 = (bf16[4,288,128]{2,1,0:T(8,128)(2,1)S(1)}, bf16[4,288,128]{2,1,0:T(8,128)(2,1)S(1)}, u32[]{:S(2)}, u32[]{:S(2)}) collective-permute-start(bf16[4,288,128]{2,1,0:T(8,128)(2,1)S(1)} %collective-permute-done.9.refs_7_), channel_id=1, source_target_pairs={{0,4},{4,8},{8,12},{12,16},{16,20},{20,24},{24,28},{28,32},{32,36}... | collective-permute-start | bytes 884744 | tf_op jit(solution)/shard_map/ppermute | solution.py:350

commit v6 on v4

--- a/solution.py
+++ b/solution.py
@@ -21,6 +21,7 @@
 PLAN = 256
 STEP = 4
 ZERO1 = 64
+ZERO2 = 48
 SPARE = 16
 
 
@@ -222,6 +223,8 @@
         kind = jnp.where(lower, 1, jnp.where(target == index, 2, 0))
         plan[KINDS + r] = kind | (diagonal << 8)
     plan[1] = count
+    for u in range(STEP - 1):
+        plan[LIST2 + count + u] = ZERO2 | (ZERO2 << 8)
 
     def tile(t, carry):
         @pl.when(need[t] == 1)
@@ -256,25 +259,22 @@
 
 
 def sweep_kernel(ids, plan, coarse, *refs):
-    pieces, (out, arrived, first, work, high, low, pivots, pivots_next, sems) = refs[:12], refs[12:]
+    pieces, (out, first, work, high, low, pivots, pivots_next) = refs[:12], refs[12:]
     col = ids[1]
     width = coarse.shape[-1]
-    copies = []
-    for k, piece in enumerate(pieces):
-        copies.append(pltpu.make_async_copy(piece, arrived.at[pl.ds(4 * k, 4)], sems.at[k]))
-        copies[-1].start()
     first[ZERO1] = jnp.zeros((width, width), BF16)
+    high[ZERO2] = jnp.zeros((width, width), BF16)
+    low[ZERO2] = jnp.zeros((width, width), BF16)
     lines, columns = iota((width, width), 0), iota((width, width), 1)
     upper, lower, equal = columns > lines, lines > columns, lines == columns
 
     def reciprocal(tile):
         return 1.0 / jnp.maximum(jnp.sum(jnp.where(equal, tile, 0.0), axis=0, keepdims=True), 1.0)
 
-    for k, copy in enumerate(copies):
-        copy.wait()
+    for k, piece in enumerate(pieces):
         start = ((col + (0, 3, 1, 2)[k % 4]) & 3) * ROWS + k // 4 * 4
         for r in range(4):
-            store_unpacked(first.at[start + r], arrived[4 * k + r], width)
+            store_unpacked(first.at[start + r], piece[r], width)
 
     def prepare(k, carry):
         diagonal = first[4 + k].astype(F32)
@@ -283,7 +283,7 @@
         pivots[k] = reciprocal(diagonal)
         return carry
 
-    lax.fori_loop(0, 8, prepare, 0)
+    lax.fori_loop(0, 8, prepare, 0, unroll=2)
 
     def begin(k, carry):
         t = plan[TILES + k] & 255
@@ -328,15 +328,18 @@
     out[...] = coarse[...]
 
     def again(k, carry):
-        entry = plan[LIST2 + k]
-        x, y, r = entry & 255, (entry >> 8) & 255, entry >> 16
-        product = jnp.dot(high[x], high[y], preferred_element_type=F32)
-        product += jnp.dot(high[x], low[y], preferred_element_type=F32)
-        product += jnp.dot(low[x], high[y], preferred_element_type=F32)
-        out[r] -= product
-        return carry
-
-    lax.fori_loop(0, plan[1], again, 0)
+        entries = entries_of(plan, LIST2, k)
+        products = []
+        for e in entries:
+            x, y = e & 255, (e >> 8) & 255
+            product = jnp.dot(high[x], high[y], preferred_element_type=F32)
+            product += jnp.dot(high[x], low[y], preferred_element_type=F32)
+            products.append(product + jnp.dot(low[x], high[y], preferred_element_type=F32))
+        for e, product in zip(entries, products):
+            out[e >> 16] -= product
+        return carry
+
+    lax.fori_loop(0, (plan[1] + STEP - 1) // STEP, again, 0)
     for r in range(4):
         entry = plan[KINDS + r]
         out[r] = scaled(out[r], entry & 255, pivots_next[entry >> 8])
@@ -431,18 +434,16 @@
     further = [second] + [along(second, "col", d, True, others) for d in (1, -1)] + [along(before[3], "agg", 1)]
     factor = call(
         sweep_kernel,
-        [SMEM] * 2 + [VMEM] + [ANY] * 12,
+        [SMEM] * 2 + [VMEM] * 13,
         array(four, F32),
         VMEM,
         [
-            pltpu.VMEM((48, *packed), BF16),
             pltpu.VMEM((65, width, width), BF16),
             pltpu.VMEM((33, width, width), F32),
             pltpu.VMEM((49, width, width), BF16),
             pltpu.VMEM((49, width, width), BF16),
             pltpu.VMEM((8, 1, width), F32),
             pltpu.VMEM((8, 1, width), F32),
-            pltpu.SemaphoreType.DMA((12,)),
         ],
         "sweep",
         34,

time: 96.9 us -> 93.7 us (0.967)
  Pallas kernels: 23.1 us -> 19.9 us
    pallas_call x1, Pallas kernels: 9.01 us -> 5.88 us  [on_device(): call(sweep_kernel, [SMEM] * 2 + [VMEM] * 13, array(four, F32), VMEM, [plt...]
where the time goes in v6:
time: 93.7 us; the launch traced here: 92 us
  starting transfers between devices  39.3 us (42%)
  waiting for transfers between devices  30.5 us (33%)
  Pallas kernels  19.9 us (21%)
  local copies, waits for them, and re-layouts  1.42 us (2%)
    ppermute x14, starting transfers between devices, along(): lax.ppermute(block, axis, [pair for pair in pairs if sources is None or p...  38 us
    ppermute x14, waiting for transfers between devices, along(): lax.ppermute(block, axis, [pair for pair in pairs if sources is None or p...  30.5 us
    pallas_call x1, Pallas kernels, on_device(): call(sweep_kernel, [SMEM] * 2 + [VMEM] * 13, array(four, F32), VMEM, [plt...  5.88 us
    pallas_call x1, Pallas kernels, on_device(): call(close_kernel, [SMEM] * 4 + [VMEM] * 2, (array((SPARE + 1, width, wid...  4.22 us
    pallas_call x1, Pallas kernels, on_device(): call(distant_kernel, [SMEM] * 4 + [VMEM] * 5, (array(four, F32), array(fo...  3.04 us
    pallas_call x1, Pallas kernels, on_device(): call(pack_kernel, [SMEM] * 2 + [VMEM], array(halo_shape, BF16), VMEM, [],...  2.82 us
    pallas_call x1, Pallas kernels, on_device(): call(plan_kernel, [SMEM] * 4, array((PLAN,), jnp.int32), SMEM, [pltpu.SME...  2.2 us
  transfers between devices with their start and end apart: 16, of which 12 were waited for; matrix products, arithmetic and copies ran while one was open for 0% of the time, Pallas kernels for 7%

profile of v6, /device:TPU:6, one launch (start us, length us, event | category | flops | bytes accessed | tf_op | source)
XLA Modules:
  0.0 92.0 jit_solution(5818763146980810285)
XLA Ops:
  0.7 2.8 %pack.1 = bf16[4624,128]{1,0:T(8,128)(2,1)} custom-call(s32[16]{0:T(128)} %labels.5, s32[4,4]{1,0:T(4,128)} %pattern.7, bf16[16,192,192]{2,1,0:T(8,128)(2,1)} %tiles.1), custom_call_target="tpu_custom_call" | custom-call | tf_op jit(solution)/shard_map/pack/pallas_call | solution.py:378
  3.5 7.5 %collective-permute-start.1 = (bf16[4624,128]{1,0:T(8,128)(2,1)}, bf16[4624,128]{1,0:T(8,128)(2,1)S(1)}, u32[]{:S(2)}, u32[]{:S(2)}) collective-permute-start(bf16[4624,128]{1,0:T(8,128)(2,1)} %pack.1), channel_id=1, source_target_pairs={{4,0},{8,4},{12,8},{16,12},{20,16},{24,20},{28,24},{32,28},{36,32}... | collective-permute-start | bytes 3551240 | tf_op jit(solution)/shard_map/ppermute | solution.py:351
  11.0 1.9 %collective-permute-start = (bf16[4624,128]{1,0:T(8,128)(2,1)}, bf16[4624,128]{1,0:T(8,128)(2,1)}, u32[]{:S(2)}, u32[]{:S(2)}) collective-permute-start(bf16[4624,128]{1,0:T(8,128)(2,1)} %pack.1), channel_id=1, source_target_pairs={{0,4},{4,8},{8,12},{12,16},{16,20},{20,24},{24,28},{28,32},{32,36}... | collective-permute-start | bytes 3551240 | tf_op jit(solution)/shard_map/ppermute | solution.py:351
  13.0 1.4 %copy-done.1 = bf16[16,192,192]{2,1,0:T(8,128)(2,1)S(1)} copy-done((bf16[16,192,192]{2,1,0:T(8,128)(2,1)S(1)}, bf16[16,192,192]{2,1,0:T(8,128)(2,1)}, u32[]{:S(2)}) %copy-start.1) | copy-done | bytes 1179672
  14.4 4.2 %close.1 = (f32[17,192,192]{2,1,0:T(8,128)S(1)}, bf16[16,192,192]{2,1,0:T(8,128)(2,1)S(1)}) custom-call(s32[2]{0:T(128)S(1)} %pad_add_fusion.ids, s32[16]{0:T(128)S(1)} %bitcast.12, s32[16]{0:T(128)S(1)} %copy-done.3, s32[4,4]{1,0:T(4,128)S(1)} %copy-done.2, bf16[16,192,192]{2,1,0:T(8,128)(2,1)S(1)} %bitcast.10, bf16[16,192,192]{2,1,0:T(8,128)(2,1)S(1)} %copy-done.1), custom_call_target="tpu_custom_call" | custom-call | tf_op jit(solution)/shard_map/close/pallas_call | solution.py:382
  18.6 6.4 %collective-permute-done.1.right = bf16[4624,128]{1,0:T(8,128)(2,1)S(1)} collective-permute-done((bf16[4624,128]{1,0:T(8,128)(2,1)}, bf16[4624,128]{1,0:T(8,128)(2,1)S(1)}, u32[]{:S(2)}, u32[]{:S(2)}) %collective-permute-start.1) | collective-permute-done | bytes 1183776 | tf_op jit(solution)/shard_map/ppermute | solution.py:351
  25.0 5.9 %collective-permute-done.left = bf16[4624,128]{1,0:T(8,128)(2,1)} collective-permute-done((bf16[4624,128]{1,0:T(8,128)(2,1)}, bf16[4624,128]{1,0:T(8,128)(2,1)}, u32[]{:S(2)}, u32[]{:S(2)}) %collective-permute-start) | collective-permute-done | bytes 1183776 | tf_op jit(solution)/shard_map/ppermute | solution.py:351
  30.9 3.0 %distant.1 = (f32[4,192,192]{2,1,0:T(8,128)S(1)}, bf16[4,288,128]{2,1,0:T(8,128)(2,1)S(1)}, bf16[4,288,128]{2,1,0:T(8,128)(2,1)S(1)}, s32[16]{0:T(128)S(1)}) custom-call(s32[2]{0:T(128)S(1)} %pad_add_fusion.ids, s32[16]{0:T(128)S(1)} %bitcast.13, s32[16]{0:T(128)S(1)} %copy-done.3, s32[4,4]{1,0:T(4,128)S(1)} %copy-done.2, ...), custom_call_target="tpu_custom_call" | custom-call | tf_op jit(solution)/shard_map/distant/pallas_call | solution.py:391
  34.0 0.7 collective-permute-start.3
  34.7 0.7 collective-permute-start.4
  35.4 1.9 %collective-permute-start.2 = (s32[16]{0:T(128)S(1)}, s32[16]{0:T(128)S(1)}, u32[]{:S(2)}, u32[]{:S(2)}) collective-permute-start(s32[16]{0:T(128)S(1)} %get-tuple-element.13.near), channel_id=1, source_target_pairs={{0,4},{4,8},{8,12},{12,16},{16,20},{20,24},{24,28},{28,32},{32,36}... | collective-permute-start | bytes 200 | tf_op jit(solution)/shard_map/ppermute | solution.py:351
  37.3 5.1 %collective-permute-done.2.far = s32[16]{0:T(128)S(1)} collective-permute-done((s32[16]{0:T(128)S(1)}, s32[16]{0:T(128)S(1)}, u32[]{:S(2)}, u32[]{:S(2)}) %collective-permute-start.2) | collective-permute-done | bytes 96 | tf_op jit(solution)/shard_map/ppermute | solution.py:351
  42.4 2.2 %plan.1 = s32[256]{0:T(256)S(1)} custom-call(s32[2]{0:T(128)S(1)} %pad_add_fusion.ids, s32[4,4]{1,0:T(4,128)S(1)} %copy-done.2, s32[16]{0:T(128)S(1)} %get-tuple-element.13.near, s32[16]{0:T(128)S(1)} %collective-permute-done.2.far), custom_call_target="tpu_custom_call" | custom-call | tf_op jit(solution)/shard_map/plan/pallas_call | solution.py:411
  44.6 1.7 %combine.1 = (f32[4,192,192]{2,1,0:T(8,128)}, bf16[4,288,128]{2,1,0:T(8,128)(2,1)S(1)}, f32[4,192,192]{2,1,0:T(8,128)S(1)}) custom-call(s32[256]{0:T(256)S(1)} %plan.1, f32[4,192,192]{2,1,0:T(8,128)S(1)} %get-tuple-element.14.mine, bf16[4,288,128]{2,1,0:T(8,128)(2,1)S(1)} %collective-permute-done.3.ahead, bf16[4,288,128]{2,1,0:T(8,128)(2,1)S(1)} %collective-permute-done.4.behind), custom_call_target="tpu_custom_call" | custom-call | tf_op jit(solution)/shard_map/combine/pallas_call | solution.py:420
  46.3 10.2 %collective-permute-start.8 = (bf16[4,288,128]{2,1,0:T(8,128)(2,1)S(1)}, bf16[4,288,128]{2,1,0:T(8,128)(2,1)S(1)}, u32[]{:S(2)}, u32[]{:S(2)}) collective-permute-start(bf16[4,288,128]{2,1,0:T(8,128)(2,1)S(1)} %get-tuple-element.19.refs_8_), channel_id=1, source_target_pairs={{0,2},{1,3},{2,0},{3,1},{4,6},{5,7},{6,4},{7,5},{8,10},{9,11},{10,... | collective-permute-start | bytes 884744 | tf_op jit(solution)/shard_map/ppermute | solution.py:351
  56.5 2.4 %collective-permute-start.14 = (bf16[4,288,128]{2,1,0:T(8,128)(2,1)S(1)}, bf16[4,288,128]{2,1,0:T(8,128)(2,1)S(1)}, u32[]{:S(2)}, u32[]{:S(2)}) collective-permute-start(bf16[4,288,128]{2,1,0:T(8,128)(2,1)S(1)} %get-tuple-element.19.refs_8_), channel_id=1, source_target_pairs={{0,3},{1,0},{2,1},{3,2},{4,7},{5,4},{6,5},{7,6},{8,11},{9,8},{10,9... | collective-permute-start | bytes 884744 | tf_op jit(solution)/shard_map/ppermute | solution.py:351
  59.0 1.9 %collective-permute-start.5 = (bf16[4,288,128]{2,1,0:T(8,128)(2,1)S(1)}, bf16[4,288,128]{2,1,0:T(8,128)(2,1)S(1)}, u32[]{:S(2)}, u32[]{:S(2)}) collective-permute-start(bf16[4,288,128]{2,1,0:T(8,128)(2,1)S(1)} %get-tuple-element.19.refs_8_), channel_id=1, source_target_pairs={{0,8},{4,12},{8,16},{12,20},{16,24},{20,28},{24,32},{28,36},{32,40... | collective-permute-start | bytes 884744 | tf_op jit(solution)/shard_map/ppermute | solution.py:351
  60.9 1.9 %collective-permute-start.11 = (bf16[4,288,128]{2,1,0:T(8,128)(2,1)S(1)}, bf16[4,288,128]{2,1,0:T(8,128)(2,1)S(1)}, u32[]{:S(2)}, u32[]{:S(2)}) collective-permute-start(bf16[4,288,128]{2,1,0:T(8,128)(2,1)S(1)} %get-tuple-element.19.refs_8_), channel_id=1, source_target_pairs={{0,4},{4,8},{8,12},{12,16},{16,20},{20,24},{24,28},{28,32},{32,36}... | collective-permute-start | bytes 884744 | tf_op jit(solution)/shard_map/ppermute | solution.py:351
  63.2 1.9 %collective-permute-start.9 = (bf16[4,288,128]{2,1,0:T(8,128)(2,1)S(1)}, bf16[4,288,128]{2,1,0:T(8,128)(2,1)S(1)}, u32[]{:S(2)}, u32[]{:S(2)}) collective-permute-start(bf16[4,288,128]{2,1,0:T(8,128)(2,1)S(1)} %collective-permute-done.8.refs_11_), channel_id=1, source_target_pairs={{0,4},{4,8},{8,12},{12,16},{16,20},{20,24},{24,28},{28,32},{32,36}... | collective-permute-start | bytes 884744 | tf_op jit(solution)/shard_map/ppermute | solution.py:351
  65.2 0.8 collective-permute-done.14.refs_10_
  65.9 1.9 %collective-permute-start.15 = (bf16[4,288,128]{2,1,0:T(8,128)(2,1)S(1)}, bf16[4,288,128]{2,1,0:T(8,128)(2,1)S(1)}, u32[]{:S(2)}, u32[]{:S(2)}) collective-permute-start(bf16[4,288,128]{2,1,0:T(8,128)(2,1)S(1)} %collective-permute-done.14.refs_10_), channel_id=1, source_target_pairs={{0,4},{4,8},{8,12},{12,16},{16,20},{20,24},{24,28},{28,32},{32,36}... | collective-permute-start | bytes 884744 | tf_op jit(solution)/shard_map/ppermute | solution.py:351
  67.9 1.9 %collective-permute-start.13 = (bf16[4,288,128]{2,1,0:T(8,128)(2,1)S(1)}, bf16[4,288,128]{2,1,0:T(8,128)(2,1)S(1)}, u32[]{:S(2)}, u32[]{:S(2)}) collective-permute-start(bf16[4,288,128]{2,1,0:T(8,128)(2,1)S(1)} %collective-permute-done.12.refs_9_), channel_id=1, source_target_pairs={{0,4},{4,8},{8,12},{12,16},{16,20},{20,24},{24,28},{28,32},{32,36}... | collective-permute-start | bytes 884744 | tf_op jit(solution)/shard_map/ppermute | solution.py:351
  69.8 1.7 %collective-permute-done.5.refs_0_ = bf16[4,288,128]{2,1,0:T(8,128)(2,1)S(1)} collective-permute-done((bf16[4,288,128]{2,1,0:T(8,128)(2,1)S(1)}, bf16[4,288,128]{2,1,0:T(8,128)(2,1)S(1)}, u32[]{:S(2)}, u32[]{:S(2)}) %collective-permute-start.5) | collective-permute-done | bytes 294944 | tf_op jit(solution)/shard_map/ppermute | solution.py:351
  71.5 1.3 %collective-permute-start.7 = (bf16[4,288,128]{2,1,0:T(8,128)(2,1)S(1)}, bf16[4,288,128]{2,1,0:T(8,128)(2,1)S(1)}, u32[]{:S(2)}, u32[]{:S(2)}) collective-permute-start(bf16[4,288,128]{2,1,0:T(8,128)(2,1)S(1)} %collective-permute-done.5.refs_0_), channel_id=1, source_target_pairs={{1,0},{2,1},{3,2},{5,4},{6,5},{7,6},{9,8},{10,9},{11,10},{13,12},{... | collective-permute-start | bytes 884744 | tf_op jit(solution)/shard_map/ppermute | solution.py:351
  72.8 1.3 %collective-permute-start.6 = (bf16[4,288,128]{2,1,0:T(8,128)(2,1)S(1)}, bf16[4,288,128]{2,1,0:T(8,128)(2,1)S(1)}, u32[]{:S(2)}, u32[]{:S(2)}) collective-permute-start(bf16[4,288,128]{2,1,0:T(8,128)(2,1)S(1)} %collective-permute-done.5.refs_0_), channel_id=1, source_target_pairs={{1,2},{2,3},{3,0},{5,6},{6,7},{7,4},{9,10},{10,11},{11,8},{13,14},... | collective-permute-start | bytes 884744 | tf_op jit(solution)/shard_map/ppermute | solution.py:351
  74.1 1.9 %collective-permute-done.9.refs_7_ = bf16[4,288,128]{2,1,0:T(8,128)(2,1)S(1)} collective-permute-done((bf16[4,288,128]{2,1,0:T(8,128)(2,1)S(1)}, bf16[4,288,128]{2,1,0:T(8,128)(2,1)S(1)}, u32[]{:S(2)}, u32[]{:S(2)}) %collective-permute-start.9) | collective-permute-done | bytes 294944 | tf_op jit(solution)/shard_map/ppermute | solution.py:351
  76.0 1.9 %collective-permute-start.10 = (bf16[4,288,128]{2,1,0:T(8,128)(2,1)S(1)}, bf16[4,288,128]{2,1,0:T(8,128)(2,1)S(1)}, u32[]{:S(2)}, u32[]{:S(2)}) collective-permute-start(bf16[4,288,128]{2,1,0:T(8,128)(2,1)S(1)} %collective-permute-done.9.refs_7_), channel_id=1, source_target_pairs={{0,4},{4,8},{8,12},{12,16},{16,20},{20,24},{24,28},{28,32},{32,36}... | collective-permute-start | bytes 884744 | tf_op jit(solution)/shard_map/ppermute | solution.py:351
  77.9 1.2 %collective-permute-done.15.refs_6_ = bf16[4,288,128]{2,1,0:T(8,128)(2,1)S(1)} collective-permute-done((bf16[4,288,128]{2,1,0:T(8,128)(2,1)S(1)}, bf16[4,288,128]{2,1,0:T(8,128)(2,1)S(1)}, u32[]{:S(2)}, u32[]{:S(2)}) %collective-permute-start.15) | collective-permute-done | bytes 294944 | tf_op jit(solution)/shard_map/ppermute | solution.py:351
  79.2 3.2 %collective-permute-done.13.refs_5_ = bf16[4,288,128]{2,1,0:T(8,128)(2,1)S(1)} collective-permute-done((bf16[4,288,128]{2,1,0:T(8,128)(2,1)S(1)}, bf16[4,288,128]{2,1,0:T(8,128)(2,1)S(1)}, u32[]{:S(2)}, u32[]{:S(2)}) %collective-permute-start.13) | collective-permute-done | bytes 294944 | tf_op jit(solution)/shard_map/ppermute | solution.py:351
  82.3 2.5 %collective-permute-done.6.refs_1_ = bf16[4,288,128]{2,1,0:T(8,128)(2,1)S(1)} collective-permute-done((bf16[4,288,128]{2,1,0:T(8,128)(2,1)S(1)}, bf16[4,288,128]{2,1,0:T(8,128)(2,1)S(1)}, u32[]{:S(2)}, u32[]{:S(2)}) %collective-permute-start.6) | collective-permute-done | bytes 294944 | tf_op jit(solution)/shard_map/ppermute | solution.py:351
  84.8 1.3 %collective-permute-done.10.refs_3_ = bf16[4,288,128]{2,1,0:T(8,128)(2,1)S(1)} collective-permute-done((bf16[4,288,128]{2,1,0:T(8,128)(2,1)S(1)}, bf16[4,288,128]{2,1,0:T(8,128)(2,1)S(1)}, u32[]{:S(2)}, u32[]{:S(2)}) %collective-permute-start.10) | collective-permute-done | bytes 294944 | tf_op jit(solution)/shard_map/ppermute | solution.py:351
  86.1 5.9 %sweep.1 = f32[4,192,192]{2,1,0:T(8,128)} custom-call(s32[2]{0:T(128)S(1)} %pad_add_fusion.ids, s32[256]{0:T(256)S(1)} %plan.1, f32[4,192,192]{2,1,0:T(8,128)S(1)} %get-tuple-element.18.coarse, bf16[4,288,128]{2,1,0:T(8,128)(2,1)S(1)} %collective-permute-done.5.refs_0_, bf16[4,288,128]{2,1,0:T(8,128)(2,1)S(1)} %collective-permute-done.6.refs_1_, ...), custom_call_target="tpu_custom_call" | custom-call | tf_op jit(solution)/shard_map/sweep/pallas_call | solution.py:435
  (17 shorter events, 0.6 us)
Async XLA Ops:
  0.6 12.3 %copy-start.2 = (s32[4,4]{1,0:T(4,128)S(1)}, s32[4,4]{1,0:T(4,128)}, u32[]{:S(2)}) copy-start(s32[4,4]{1,0:T(4,128)} %pattern.7) | copy-start | bytes 196
  0.6 12.3 %copy-start.3 = (s32[16]{0:T(128)S(1)}, s32[16]{0:T(128)}, u32[]{:S(2)}) copy-start(s32[16]{0:T(128)} %labels.5) | copy-start | bytes 196
  0.7 12.3 %copy-start.4 = (s32[16,1]{0,1:T(1,128)S(1)}, s32[16,1]{0,1:T(1,128)}, u32[]{:S(2)}) copy-start(s32[16,1]{0,1:T(1,128)} %param.6) | copy-start | bytes 196
  0.7 12.3 %copy-start = (bf16[16,1,192,192]{3,2,1,0:T(8,128)(2,1)S(1)}, bf16[16,1,192,192]{3,2,1,0:T(8,128)(2,1)}, u32[]{:S(2)}) copy-start(bf16[16,1,192,192]{3,2,1,0:T(8,128)(2,1)} %param.5) | copy-start | bytes 3538948
  3.5 21.5 %collective-permute-start.1 = (bf16[4624,128]{1,0:T(8,128)(2,1)}, bf16[4624,128]{1,0:T(8,128)(2,1)S(1)}, u32[]{:S(2)}, u32[]{:S(2)}) collective-permute-start(bf16[4624,128]{1,0:T(8,128)(2,1)} %pack.1), channel_id=1, source_target_pairs={{4,0},{8,4},{12,8},{16,12},{20,16},{24,20},{28,24},{32,28},{36,32}... | collective-permute-start | bytes 3551240 | tf_op jit(solution)/shard_map/ppermute | solution.py:351
  11.0 20.0 %collective-permute-start = (bf16[4624,128]{1,0:T(8,128)(2,1)}, bf16[4624,128]{1,0:T(8,128)(2,1)}, u32[]{:S(2)}, u32[]{:S(2)}) collective-permute-start(bf16[4624,128]{1,0:T(8,128)(2,1)} %pack.1), channel_id=1, source_target_pairs={{0,4},{4,8},{8,12},{12,16},{16,20},{20,24},{24,28},{28,32},{32,36}... | collective-permute-start | bytes 3551240 | tf_op jit(solution)/shard_map/ppermute | solution.py:351
  13.0 1.4 %copy-start.1 = (bf16[16,192,192]{2,1,0:T(8,128)(2,1)S(1)}, bf16[16,192,192]{2,1,0:T(8,128)(2,1)}, u32[]{:S(2)}) copy-start(bf16[16,192,192]{2,1,0:T(8,128)(2,1)} %tiles.1) | copy-start | bytes 3538948
  34.0 10.6 %collective-permute-start.3 = (bf16[4,288,128]{2,1,0:T(8,128)(2,1)S(1)}, bf16[4,288,128]{2,1,0:T(8,128)(2,1)S(1)}, u32[]{:S(2)}, u32[]{:S(2)}) collective-permute-start(bf16[4,288,128]{2,1,0:T(8,128)(2,1)S(1)} %get-tuple-element.15), channel_id=1, source_target_pairs={{1,2},{2,3},{3,1},{5,6},{6,7},{7,5},{9,10},{10,11},{11,9},{13,14},... | collective-permute-start | bytes 884744 | tf_op jit(solution)/shard_map/ppermute | solution.py:408
  34.7 9.9 %collective-permute-start.4 = (bf16[4,288,128]{2,1,0:T(8,128)(2,1)S(1)}, bf16[4,288,128]{2,1,0:T(8,128)(2,1)S(1)}, u32[]{:S(2)}, u32[]{:S(2)}) collective-permute-start(bf16[4,288,128]{2,1,0:T(8,128)(2,1)S(1)} %get-tuple-element.16), channel_id=1, source_target_pairs={{1,3},{2,1},{3,2},{5,7},{6,5},{7,6},{9,11},{10,9},{11,10},{13,15},... | collective-permute-start | bytes 884744 | tf_op jit(solution)/shard_map/ppermute | solution.py:409
  35.4 7.0 %collective-permute-start.2 = (s32[16]{0:T(128)S(1)}, s32[16]{0:T(128)S(1)}, u32[]{:S(2)}, u32[]{:S(2)}) collective-permute-start(s32[16]{0:T(128)S(1)} %get-tuple-element.13.near), channel_id=1, source_target_pairs={{0,4},{4,8},{8,12},{12,16},{16,20},{20,24},{24,28},{28,32},{32,36}... | collective-permute-start | bytes 200 | tf_op jit(solution)/shard_map/ppermute | solution.py:351
  46.3 16.9 %collective-permute-start.8 = (bf16[4,288,128]{2,1,0:T(8,128)(2,1)S(1)}, bf16[4,288,128]{2,1,0:T(8,128)(2,1)S(1)}, u32[]{:S(2)}, u32[]{:S(2)}) collective-permute-start(bf16[4,288,128]{2,1,0:T(8,128)(2,1)S(1)} %get-tuple-element.19.refs_8_), channel_id=1, source_target_pairs={{0,2},{1,3},{2,0},{3,1},{4,6},{5,7},{6,4},{7,5},{8,10},{9,11},{10,... | collective-permute-start | bytes 884744 | tf_op jit(solution)/shard_map/ppermute | solution.py:351
  56.5 9.4 %collective-permute-start.14 = (bf16[4,288,128]{2,1,0:T(8,128)(2,1)S(1)}, bf16[4,288,128]{2,1,0:T(8,128)(2,1)S(1)}, u32[]{:S(2)}, u32[]{:S(2)}) collective-permute-start(bf16[4,288,128]{2,1,0:T(8,128)(2,1)S(1)} %get-tuple-element.19.refs_8_), channel_id=1, source_target_pairs={{0,3},{1,0},{2,1},{3,2},{4,7},{5,4},{6,5},{7,6},{8,11},{9,8},{10,9... | collective-permute-start | bytes 884744 | tf_op jit(solution)/shard_map/ppermute | solution.py:351
  59.0 8.9 %collective-permute-start.12 = (bf16[4,288,128]{2,1,0:T(8,128)(2,1)S(1)}, bf16[4,288,128]{2,1,0:T(8,128)(2,1)S(1)}, u32[]{:S(2)}, u32[]{:S(2)}) collective-permute-start(bf16[4,288,128]{2,1,0:T(8,128)(2,1)S(1)} %get-tuple-element.19.refs_8_), channel_id=1, source_target_pairs={{0,1},{1,2},{2,3},{3,0},{4,5},{5,6},{6,7},{7,4},{8,9},{9,10},{10,1... | collective-permute-start | bytes 884744 | tf_op jit(solution)/shard_map/ppermute | solution.py:351
  59.0 12.5 %collective-permute-start.5 = (bf16[4,288,128]{2,1,0:T(8,128)(2,1)S(1)}, bf16[4,288,128]{2,1,0:T(8,128)(2,1)S(1)}, u32[]{:S(2)}, u32[]{:S(2)}) collective-permute-start(bf16[4,288,128]{2,1,0:T(8,128)(2,1)S(1)} %get-tuple-element.19.refs_8_), channel_id=1, source_target_pairs={{0,8},{4,12},{8,16},{12,20},{16,24},{20,28},{24,32},{28,36},{32,40... | collective-permute-start | bytes 884744 | tf_op jit(solution)/shard_map/ppermute | solution.py:351
  60.9 12.0 %collective-permute-start.11 = (bf16[4,288,128]{2,1,0:T(8,128)(2,1)S(1)}, bf16[4,288,128]{2,1,0:T(8,128)(2,1)S(1)}, u32[]{:S(2)}, u32[]{:S(2)}) collective-permute-start(bf16[4,288,128]{2,1,0:T(8,128)(2,1)S(1)} %get-tuple-element.19.refs_8_), channel_id=1, source_target_pairs={{0,4},{4,8},{8,12},{12,16},{16,20},{20,24},{24,28},{28,32},{32,36}... | collective-permute-start | bytes 884744 | tf_op jit(solution)/shard_map/ppermute | solution.py:351
  63.2 12.8 %collective-permute-start.9 = (bf16[4,288,128]{2,1,0:T(8,128)(2,1)S(1)}, bf16[4,288,128]{2,1,0:T(8,128)(2,1)S(1)}, u32[]{:S(2)}, u32[]{:S(2)}) collective-permute-start(bf16[4,288,128]{2,1,0:T(8,128)(2,1)S(1)} %collective-permute-done.8.refs_11_), channel_id=1, source_target_pairs={{0,4},{4,8},{8,12},{12,16},{16,20},{20,24},{24,28},{28,32},{32,36}... | collective-permute-start | bytes 884744 | tf_op jit(solution)/shard_map/ppermute | solution.py:351
  65.9 13.2 %collective-permute-start.15 = (bf16[4,288,128]{2,1,0:T(8,128)(2,1)S(1)}, bf16[4,288,128]{2,1,0:T(8,128)(2,1)S(1)}, u32[]{:S(2)}, u32[]{:S(2)}) collective-permute-start(bf16[4,288,128]{2,1,0:T(8,128)(2,1)S(1)} %collective-permute-done.14.refs_10_), channel_id=1, source_target_pairs={{0,4},{4,8},{8,12},{12,16},{16,20},{20,24},{24,28},{28,32},{32,36}... | collective-permute-start | bytes 884744 | tf_op jit(solution)/shard_map/ppermute | solution.py:351
  67.9 14.5 %collective-permute-start.13 = (bf16[4,288,128]{2,1,0:T(8,128)(2,1)S(1)}, bf16[4,288,128]{2,1,0:T(8,128)(2,1)S(1)}, u32[]{:S(2)}, u32[]{:S(2)}) collective-permute-start(bf16[4,288,128]{2,1,0:T(8,128)(2,1)S(1)} %collective-permute-done.12.refs_9_), channel_id=1, source_target_pairs={{0,4},{4,8},{8,12},{12,16},{16,20},{20,24},{24,28},{28,32},{32,36}... | collective-permute-start | bytes 884744 | tf_op jit(solution)/shard_map/ppermute | solution.py:351
  71.5 10.8 %collective-permute-start.7 = (bf16[4,288,128]{2,1,0:T(8,128)(2,1)S(1)}, bf16[4,288,128]{2,1,0:T(8,128)(2,1)S(1)}, u32[]{:S(2)}, u32[]{:S(2)}) collective-permute-start(bf16[4,288,128]{2,1,0:T(8,128)(2,1)S(1)} %collective-permute-done.5.refs_0_), channel_id=1, source_target_pairs={{1,0},{2,1},{3,2},{5,4},{6,5},{7,6},{9,8},{10,9},{11,10},{13,12},{... | collective-permute-start | bytes 884744 | tf_op jit(solution)/shard_map/ppermute | solution.py:351
  72.8 12.0 %collective-permute-start.6 = (bf16[4,288,128]{2,1,0:T(8,128)(2,1)S(1)}, bf16[4,288,128]{2,1,0:T(8,128)(2,1)S(1)}, u32[]{:S(2)}, u32[]{:S(2)}) collective-permute-start(bf16[4,288,128]{2,1,0:T(8,128)(2,1)S(1)} %collective-permute-done.5.refs_0_), channel_id=1, source_target_pairs={{1,2},{2,3},{3,0},{5,6},{6,7},{7,4},{9,10},{10,11},{11,8},{13,14},... | collective-permute-start | bytes 884744 | tf_op jit(solution)/shard_map/ppermute | solution.py:351
  76.0 10.1 %collective-permute-start.10 = (bf16[4,288,128]{2,1,0:T(8,128)(2,1)S(1)}, bf16[4,288,128]{2,1,0:T(8,128)(2,1)S(1)}, u32[]{:S(2)}, u32[]{:S(2)}) collective-permute-start(bf16[4,288,128]{2,1,0:T(8,128)(2,1)S(1)} %collective-permute-done.9.refs_7_), channel_id=1, source_target_pairs={{0,4},{4,8},{8,12},{12,16},{16,20},{20,24},{24,28},{28,32},{32,36}... | collective-permute-start | bytes 884744 | tf_op jit(solution)/shard_map/ppermute | solution.py:351

commit v7 on v6

--- a/solution.py
+++ b/solution.py
@@ -254,7 +254,7 @@
     plan[0] = 0
     plan[2] = 0
     lax.fori_loop(0, 32, tile, 0)
-    for u in range(STEP - 1):
+    for u in range(2 * STEP - 1):
         plan[LIST1 + plan[0] + u] = ZERO1 | (ZERO1 << 8) | (32 << 16)
 
 
@@ -293,13 +293,13 @@
     lax.fori_loop(0, plan[2], begin, 0)
 
     def multiply(k, carry):
-        entries = entries_of(plan, LIST1, k)
+        entries = entries_of(plan, LIST1, 2 * k) + entries_of(plan, LIST1, 2 * k + 1)
         products = [jnp.dot(first[e & 255], first[(e >> 8) & 255], preferred_element_type=F32) for e in entries]
         for e, product in zip(entries, products):
             work[e >> 16] -= product
         return carry
 
-    lax.fori_loop(0, (plan[0] + STEP - 1) // STEP, multiply, 0)
+    lax.fori_loop(0, (plan[0] + 2 * STEP - 1) // (2 * STEP), multiply, 0)
 
     def scaled(tile, kind, row):
         factor = jnp.where((kind == 1) | ((kind == 2) & lower), row, 1.0)

time: 93.7 us -> 93.8 us (level)
  no operation moved by 1% of the time
where the time goes in v7:
time: 93.8 us; the launch traced here: 92.8 us
  starting transfers between devices  39.3 us (42%)
  waiting for transfers between devices  30.5 us (33%)
  Pallas kernels  20.7 us (22%)
  local copies, waits for them, and re-layouts  1.42 us (2%)
    ppermute x14, starting transfers between devices, along(): lax.ppermute(block, axis, [pair for pair in pairs if sources is None or p...  37.9 us
    ppermute x14, waiting for transfers between devices, along(): lax.ppermute(block, axis, [pair for pair in pairs if sources is None or p...  30.5 us
    pallas_call x1, Pallas kernels, on_device(): call(sweep_kernel, [SMEM] * 2 + [VMEM] * 13, array(four, F32), VMEM, [plt...  6.56 us
    pallas_call x1, Pallas kernels, on_device(): call(close_kernel, [SMEM] * 4 + [VMEM] * 2, (array((SPARE + 1, width, wid...  4.22 us
    pallas_call x1, Pallas kernels, on_device(): call(distant_kernel, [SMEM] * 4 + [VMEM] * 5, (array(four, F32), array(fo...  3.04 us
    pallas_call x1, Pallas kernels, on_device(): call(pack_kernel, [SMEM] * 2 + [VMEM], array(halo_shape, BF16), VMEM, [],...  2.82 us
    pallas_call x1, Pallas kernels, on_device(): call(plan_kernel, [SMEM] * 4, array((PLAN,), jnp.int32), SMEM, [pltpu.SME...  2.38 us
  transfers between devices with their start and end apart: 16, of which 12 were waited for; matrix products, arithmetic and copies ran while one was open for 0% of the time, Pallas kernels for 7%

profile of v7, /device:TPU:6, one launch (start us, length us, event | category | flops | bytes accessed | tf_op | source)
XLA Modules:
  0.0 92.8 jit_solution(14498296689375891758)
XLA Ops:
  0.7 2.8 %pack.1 = bf16[4624,128]{1,0:T(8,128)(2,1)} custom-call(s32[16]{0:T(128)} %labels.5, s32[4,4]{1,0:T(4,128)} %pattern.7, bf16[16,192,192]{2,1,0:T(8,128)(2,1)} %tiles.1), custom_call_target="tpu_custom_call" | custom-call | tf_op jit(solution)/shard_map/pack/pallas_call | solution.py:378
  3.5 7.5 %collective-permute-start.1 = (bf16[4624,128]{1,0:T(8,128)(2,1)}, bf16[4624,128]{1,0:T(8,128)(2,1)S(1)}, u32[]{:S(2)}, u32[]{:S(2)}) collective-permute-start(bf16[4624,128]{1,0:T(8,128)(2,1)} %pack.1), channel_id=1, source_target_pairs={{4,0},{8,4},{12,8},{16,12},{20,16},{24,20},{28,24},{32,28},{36,32}... | collective-permute-start | bytes 3551240 | tf_op jit(solution)/shard_map/ppermute | solution.py:351
  11.0 1.9 %collective-permute-start = (bf16[4624,128]{1,0:T(8,128)(2,1)}, bf16[4624,128]{1,0:T(8,128)(2,1)}, u32[]{:S(2)}, u32[]{:S(2)}) collective-permute-start(bf16[4624,128]{1,0:T(8,128)(2,1)} %pack.1), channel_id=1, source_target_pairs={{0,4},{4,8},{8,12},{12,16},{16,20},{20,24},{24,28},{28,32},{32,36}... | collective-permute-start | bytes 3551240 | tf_op jit(solution)/shard_map/ppermute | solution.py:351
  13.0 1.4 %copy-done.1 = bf16[16,192,192]{2,1,0:T(8,128)(2,1)S(1)} copy-done((bf16[16,192,192]{2,1,0:T(8,128)(2,1)S(1)}, bf16[16,192,192]{2,1,0:T(8,128)(2,1)}, u32[]{:S(2)}) %copy-start.1) | copy-done | bytes 1179672
  14.4 4.2 %close.1 = (f32[17,192,192]{2,1,0:T(8,128)S(1)}, bf16[16,192,192]{2,1,0:T(8,128)(2,1)S(1)}) custom-call(s32[2]{0:T(128)S(1)} %pad_add_fusion.ids, s32[16]{0:T(128)S(1)} %bitcast.12, s32[16]{0:T(128)S(1)} %copy-done.3, s32[4,4]{1,0:T(4,128)S(1)} %copy-done.2, bf16[16,192,192]{2,1,0:T(8,128)(2,1)S(1)} %bitcast.10, bf16[16,192,192]{2,1,0:T(8,128)(2,1)S(1)} %copy-done.1), custom_call_target="tpu_custom_call" | custom-call | tf_op jit(solution)/shard_map/close/pallas_call | solution.py:382
  18.6 6.4 %collective-permute-done.1.right = bf16[4624,128]{1,0:T(8,128)(2,1)S(1)} collective-permute-done((bf16[4624,128]{1,0:T(8,128)(2,1)}, bf16[4624,128]{1,0:T(8,128)(2,1)S(1)}, u32[]{:S(2)}, u32[]{:S(2)}) %collective-permute-start.1) | collective-permute-done | bytes 1183776 | tf_op jit(solution)/shard_map/ppermute | solution.py:351
  25.0 5.9 %collective-permute-done.left = bf16[4624,128]{1,0:T(8,128)(2,1)} collective-permute-done((bf16[4624,128]{1,0:T(8,128)(2,1)}, bf16[4624,128]{1,0:T(8,128)(2,1)}, u32[]{:S(2)}, u32[]{:S(2)}) %collective-permute-start) | collective-permute-done | bytes 1183776 | tf_op jit(solution)/shard_map/ppermute | solution.py:351
  30.9 3.0 %distant.1 = (f32[4,192,192]{2,1,0:T(8,128)S(1)}, bf16[4,288,128]{2,1,0:T(8,128)(2,1)S(1)}, bf16[4,288,128]{2,1,0:T(8,128)(2,1)S(1)}, s32[16]{0:T(128)S(1)}) custom-call(s32[2]{0:T(128)S(1)} %pad_add_fusion.ids, s32[16]{0:T(128)S(1)} %bitcast.13, s32[16]{0:T(128)S(1)} %copy-done.3, s32[4,4]{1,0:T(4,128)S(1)} %copy-done.2, ...), custom_call_target="tpu_custom_call" | custom-call | tf_op jit(solution)/shard_map/distant/pallas_call | solution.py:391
  34.0 0.7 collective-permute-start.3
  34.7 0.7 collective-permute-start.4
  35.4 1.9 %collective-permute-start.2 = (s32[16]{0:T(128)S(1)}, s32[16]{0:T(128)S(1)}, u32[]{:S(2)}, u32[]{:S(2)}) collective-permute-start(s32[16]{0:T(128)S(1)} %get-tuple-element.13.near), channel_id=1, source_target_pairs={{0,4},{4,8},{8,12},{12,16},{16,20},{20,24},{24,28},{28,32},{32,36}... | collective-permute-start | bytes 200 | tf_op jit(solution)/shard_map/ppermute | solution.py:351
  37.3 5.1 %collective-permute-done.2.far = s32[16]{0:T(128)S(1)} collective-permute-done((s32[16]{0:T(128)S(1)}, s32[16]{0:T(128)S(1)}, u32[]{:S(2)}, u32[]{:S(2)}) %collective-permute-start.2) | collective-permute-done | bytes 96 | tf_op jit(solution)/shard_map/ppermute | solution.py:351
  42.4 2.4 %plan.1 = s32[256]{0:T(256)S(1)} custom-call(s32[2]{0:T(128)S(1)} %pad_add_fusion.ids, s32[4,4]{1,0:T(4,128)S(1)} %copy-done.2, s32[16]{0:T(128)S(1)} %get-tuple-element.13.near, s32[16]{0:T(128)S(1)} %collective-permute-done.2.far), custom_call_target="tpu_custom_call" | custom-call | tf_op jit(solution)/shard_map/plan/pallas_call | solution.py:411
  44.8 1.7 %combine.1 = (f32[4,192,192]{2,1,0:T(8,128)}, bf16[4,288,128]{2,1,0:T(8,128)(2,1)S(1)}, f32[4,192,192]{2,1,0:T(8,128)S(1)}) custom-call(s32[256]{0:T(256)S(1)} %plan.1, f32[4,192,192]{2,1,0:T(8,128)S(1)} %get-tuple-element.14.mine, bf16[4,288,128]{2,1,0:T(8,128)(2,1)S(1)} %collective-permute-done.3.ahead, bf16[4,288,128]{2,1,0:T(8,128)(2,1)S(1)} %collective-permute-done.4.behind), custom_call_target="tpu_custom_call" | custom-call | tf_op jit(solution)/shard_map/combine/pallas_call | solution.py:420
  46.5 9.2 %collective-permute-start.8 = (bf16[4,288,128]{2,1,0:T(8,128)(2,1)S(1)}, bf16[4,288,128]{2,1,0:T(8,128)(2,1)S(1)}, u32[]{:S(2)}, u32[]{:S(2)}) collective-permute-start(bf16[4,288,128]{2,1,0:T(8,128)(2,1)S(1)} %get-tuple-element.19.refs_8_), channel_id=1, source_target_pairs={{0,2},{1,3},{2,0},{3,1},{4,6},{5,7},{6,4},{7,5},{8,10},{9,11},{10,... | collective-permute-start | bytes 884744 | tf_op jit(solution)/shard_map/ppermute | solution.py:351
  55.7 3.4 %collective-permute-start.14 = (bf16[4,288,128]{2,1,0:T(8,128)(2,1)S(1)}, bf16[4,288,128]{2,1,0:T(8,128)(2,1)S(1)}, u32[]{:S(2)}, u32[]{:S(2)}) collective-permute-start(bf16[4,288,128]{2,1,0:T(8,128)(2,1)S(1)} %get-tuple-element.19.refs_8_), channel_id=1, source_target_pairs={{0,3},{1,0},{2,1},{3,2},{4,7},{5,4},{6,5},{7,6},{8,11},{9,8},{10,9... | collective-permute-start | bytes 884744 | tf_op jit(solution)/shard_map/ppermute | solution.py:351
  59.1 1.9 %collective-permute-start.5 = (bf16[4,288,128]{2,1,0:T(8,128)(2,1)S(1)}, bf16[4,288,128]{2,1,0:T(8,128)(2,1)S(1)}, u32[]{:S(2)}, u32[]{:S(2)}) collective-permute-start(bf16[4,288,128]{2,1,0:T(8,128)(2,1)S(1)} %get-tuple-element.19.refs_8_), channel_id=1, source_target_pairs={{0,8},{4,12},{8,16},{12,20},{16,24},{20,28},{24,32},{28,36},{32,40... | collective-permute-start | bytes 884744 | tf_op jit(solution)/shard_map/ppermute | solution.py:351
  61.0 1.9 %collective-permute-start.11 = (bf16[4,288,128]{2,1,0:T(8,128)(2,1)S(1)}, bf16[4,288,128]{2,1,0:T(8,128)(2,1)S(1)}, u32[]{:S(2)}, u32[]{:S(2)}) collective-permute-start(bf16[4,288,128]{2,1,0:T(8,128)(2,1)S(1)} %get-tuple-element.19.refs_8_), channel_id=1, source_target_pairs={{0,4},{4,8},{8,12},{12,16},{16,20},{20,24},{24,28},{28,32},{32,36}... | collective-permute-start | bytes 884744 | tf_op jit(solution)/shard_map/ppermute | solution.py:351
  63.3 1.9 %collective-permute-start.9 = (bf16[4,288,128]{2,1,0:T(8,128)(2,1)S(1)}, bf16[4,288,128]{2,1,0:T(8,128)(2,1)S(1)}, u32[]{:S(2)}, u32[]{:S(2)}) collective-permute-start(bf16[4,288,128]{2,1,0:T(8,128)(2,1)S(1)} %collective-permute-done.8.refs_11_), channel_id=1, source_target_pairs={{0,4},{4,8},{8,12},{12,16},{16,20},{20,24},{24,28},{28,32},{32,36}... | collective-permute-start | bytes 884744 | tf_op jit(solution)/shard_map/ppermute | solution.py:351
  65.2 1.4 %collective-permute-done.14.refs_10_ = bf16[4,288,128]{2,1,0:T(8,128)(2,1)S(1)} collective-permute-done((bf16[4,288,128]{2,1,0:T(8,128)(2,1)S(1)}, bf16[4,288,128]{2,1,0:T(8,128)(2,1)S(1)}, u32[]{:S(2)}, u32[]{:S(2)}) %collective-permute-start.14) | collective-permute-done | bytes 294944 | tf_op jit(solution)/shard_map/ppermute | solution.py:351
  66.5 1.9 %collective-permute-start.15 = (bf16[4,288,128]{2,1,0:T(8,128)(2,1)S(1)}, bf16[4,288,128]{2,1,0:T(8,128)(2,1)S(1)}, u32[]{:S(2)}, u32[]{:S(2)}) collective-permute-start(bf16[4,288,128]{2,1,0:T(8,128)(2,1)S(1)} %collective-permute-done.14.refs_10_), channel_id=1, source_target_pairs={{0,4},{4,8},{8,12},{12,16},{16,20},{20,24},{24,28},{28,32},{32,36}... | collective-permute-start | bytes 884744 | tf_op jit(solution)/shard_map/ppermute | solution.py:351
  68.5 1.9 %collective-permute-start.13 = (bf16[4,288,128]{2,1,0:T(8,128)(2,1)S(1)}, bf16[4,288,128]{2,1,0:T(8,128)(2,1)S(1)}, u32[]{:S(2)}, u32[]{:S(2)}) collective-permute-start(bf16[4,288,128]{2,1,0:T(8,128)(2,1)S(1)} %collective-permute-done.12.refs_9_), channel_id=1, source_target_pairs={{0,4},{4,8},{8,12},{12,16},{16,20},{20,24},{24,28},{28,32},{32,36}... | collective-permute-start | bytes 884744 | tf_op jit(solution)/shard_map/ppermute | solution.py:351
  70.4 1.2 %collective-permute-done.5.refs_0_ = bf16[4,288,128]{2,1,0:T(8,128)(2,1)S(1)} collective-permute-done((bf16[4,288,128]{2,1,0:T(8,128)(2,1)S(1)}, bf16[4,288,128]{2,1,0:T(8,128)(2,1)S(1)}, u32[]{:S(2)}, u32[]{:S(2)}) %collective-permute-start.5) | collective-permute-done | bytes 294944 | tf_op jit(solution)/shard_map/ppermute | solution.py:351
  71.6 1.3 %collective-permute-start.7 = (bf16[4,288,128]{2,1,0:T(8,128)(2,1)S(1)}, bf16[4,288,128]{2,1,0:T(8,128)(2,1)S(1)}, u32[]{:S(2)}, u32[]{:S(2)}) collective-permute-start(bf16[4,288,128]{2,1,0:T(8,128)(2,1)S(1)} %collective-permute-done.5.refs_0_), channel_id=1, source_target_pairs={{1,0},{2,1},{3,2},{5,4},{6,5},{7,6},{9,8},{10,9},{11,10},{13,12},{... | collective-permute-start | bytes 884744 | tf_op jit(solution)/shard_map/ppermute | solution.py:351
  73.0 1.3 %collective-permute-start.6 = (bf16[4,288,128]{2,1,0:T(8,128)(2,1)S(1)}, bf16[4,288,128]{2,1,0:T(8,128)(2,1)S(1)}, u32[]{:S(2)}, u32[]{:S(2)}) collective-permute-start(bf16[4,288,128]{2,1,0:T(8,128)(2,1)S(1)} %collective-permute-done.5.refs_0_), channel_id=1, source_target_pairs={{1,2},{2,3},{3,0},{5,6},{6,7},{7,4},{9,10},{10,11},{11,8},{13,14},... | collective-permute-start | bytes 884744 | tf_op jit(solution)/shard_map/ppermute | solution.py:351
  74.3 1.9 %collective-permute-done.9.refs_7_ = bf16[4,288,128]{2,1,0:T(8,128)(2,1)S(1)} collective-permute-done((bf16[4,288,128]{2,1,0:T(8,128)(2,1)S(1)}, bf16[4,288,128]{2,1,0:T(8,128)(2,1)S(1)}, u32[]{:S(2)}, u32[]{:S(2)}) %collective-permute-start.9) | collective-permute-done | bytes 294944 | tf_op jit(solution)/shard_map/ppermute | solution.py:351
  76.1 1.9 %collective-permute-start.10 = (bf16[4,288,128]{2,1,0:T(8,128)(2,1)S(1)}, bf16[4,288,128]{2,1,0:T(8,128)(2,1)S(1)}, u32[]{:S(2)}, u32[]{:S(2)}) collective-permute-start(bf16[4,288,128]{2,1,0:T(8,128)(2,1)S(1)} %collective-permute-done.9.refs_7_), channel_id=1, source_target_pairs={{0,4},{4,8},{8,12},{12,16},{16,20},{20,24},{24,28},{28,32},{32,36}... | collective-permute-start | bytes 884744 | tf_op jit(solution)/shard_map/ppermute | solution.py:351
  78.0 1.2 %collective-permute-done.15.refs_6_ = bf16[4,288,128]{2,1,0:T(8,128)(2,1)S(1)} collective-permute-done((bf16[4,288,128]{2,1,0:T(8,128)(2,1)S(1)}, bf16[4,288,128]{2,1,0:T(8,128)(2,1)S(1)}, u32[]{:S(2)}, u32[]{:S(2)}) %collective-permute-start.15) | collective-permute-done | bytes 294944 | tf_op jit(solution)/shard_map/ppermute | solution.py:351
  79.3 3.2 %collective-permute-done.13.refs_5_ = bf16[4,288,128]{2,1,0:T(8,128)(2,1)S(1)} collective-permute-done((bf16[4,288,128]{2,1,0:T(8,128)(2,1)S(1)}, bf16[4,288,128]{2,1,0:T(8,128)(2,1)S(1)}, u32[]{:S(2)}, u32[]{:S(2)}) %collective-permute-start.13) | collective-permute-done | bytes 294944 | tf_op jit(solution)/shard_map/ppermute | solution.py:351
  82.5 2.4 %collective-permute-done.6.refs_1_ = bf16[4,288,128]{2,1,0:T(8,128)(2,1)S(1)} collective-permute-done((bf16[4,288,128]{2,1,0:T(8,128)(2,1)S(1)}, bf16[4,288,128]{2,1,0:T(8,128)(2,1)S(1)}, u32[]{:S(2)}, u32[]{:S(2)}) %collective-permute-start.6) | collective-permute-done | bytes 294944 | tf_op jit(solution)/shard_map/ppermute | solution.py:351
  84.9 1.4 %collective-permute-done.10.refs_3_ = bf16[4,288,128]{2,1,0:T(8,128)(2,1)S(1)} collective-permute-done((bf16[4,288,128]{2,1,0:T(8,128)(2,1)S(1)}, bf16[4,288,128]{2,1,0:T(8,128)(2,1)S(1)}, u32[]{:S(2)}, u32[]{:S(2)}) %collective-permute-start.10) | collective-permute-done | bytes 294944 | tf_op jit(solution)/shard_map/ppermute | solution.py:351
  86.3 6.6 %sweep.1 = f32[4,192,192]{2,1,0:T(8,128)} custom-call(s32[2]{0:T(128)S(1)} %pad_add_fusion.ids, s32[256]{0:T(256)S(1)} %plan.1, f32[4,192,192]{2,1,0:T(8,128)S(1)} %get-tuple-element.18.coarse, bf16[4,288,128]{2,1,0:T(8,128)(2,1)S(1)} %collective-permute-done.5.refs_0_, bf16[4,288,128]{2,1,0:T(8,128)(2,1)S(1)} %collective-permute-done.6.refs_1_, ...), custom_call_target="tpu_custom_call" | custom-call | tf_op jit(solution)/shard_map/sweep/pallas_call | solution.py:435
  (17 shorter events, 0.5 us)
Async XLA Ops:
  0.6 12.3 %copy-start.2 = (s32[4,4]{1,0:T(4,128)S(1)}, s32[4,4]{1,0:T(4,128)}, u32[]{:S(2)}) copy-start(s32[4,4]{1,0:T(4,128)} %pattern.7) | copy-start | bytes 196
  0.6 12.3 %copy-start.3 = (s32[16]{0:T(128)S(1)}, s32[16]{0:T(128)}, u32[]{:S(2)}) copy-start(s32[16]{0:T(128)} %labels.5) | copy-start | bytes 196
  0.7 12.3 %copy-start.4 = (s32[16,1]{0,1:T(1,128)S(1)}, s32[16,1]{0,1:T(1,128)}, u32[]{:S(2)}) copy-start(s32[16,1]{0,1:T(1,128)} %param.6) | copy-start | bytes 196
  0.7 12.3 %copy-start = (bf16[16,1,192,192]{3,2,1,0:T(8,128)(2,1)S(1)}, bf16[16,1,192,192]{3,2,1,0:T(8,128)(2,1)}, u32[]{:S(2)}) copy-start(bf16[16,1,192,192]{3,2,1,0:T(8,128)(2,1)} %param.5) | copy-start | bytes 3538948
  3.5 21.5 %collective-permute-start.1 = (bf16[4624,128]{1,0:T(8,128)(2,1)}, bf16[4624,128]{1,0:T(8,128)(2,1)S(1)}, u32[]{:S(2)}, u32[]{:S(2)}) collective-permute-start(bf16[4624,128]{1,0:T(8,128)(2,1)} %pack.1), channel_id=1, source_target_pairs={{4,0},{8,4},{12,8},{16,12},{20,16},{24,20},{28,24},{32,28},{36,32}... | collective-permute-start | bytes 3551240 | tf_op jit(solution)/shard_map/ppermute | solution.py:351
  11.0 20.0 %collective-permute-start = (bf16[4624,128]{1,0:T(8,128)(2,1)}, bf16[4624,128]{1,0:T(8,128)(2,1)}, u32[]{:S(2)}, u32[]{:S(2)}) collective-permute-start(bf16[4624,128]{1,0:T(8,128)(2,1)} %pack.1), channel_id=1, source_target_pairs={{0,4},{4,8},{8,12},{12,16},{16,20},{20,24},{24,28},{28,32},{32,36}... | collective-permute-start | bytes 3551240 | tf_op jit(solution)/shard_map/ppermute | solution.py:351
  13.0 1.4 %copy-start.1 = (bf16[16,192,192]{2,1,0:T(8,128)(2,1)S(1)}, bf16[16,192,192]{2,1,0:T(8,128)(2,1)}, u32[]{:S(2)}) copy-start(bf16[16,192,192]{2,1,0:T(8,128)(2,1)} %tiles.1) | copy-start | bytes 3538948
  34.0 10.8 %collective-permute-start.3 = (bf16[4,288,128]{2,1,0:T(8,128)(2,1)S(1)}, bf16[4,288,128]{2,1,0:T(8,128)(2,1)S(1)}, u32[]{:S(2)}, u32[]{:S(2)}) collective-permute-start(bf16[4,288,128]{2,1,0:T(8,128)(2,1)S(1)} %get-tuple-element.15), channel_id=1, source_target_pairs={{1,2},{2,3},{3,1},{5,6},{6,7},{7,5},{9,10},{10,11},{11,9},{13,14},... | collective-permute-start | bytes 884744 | tf_op jit(solution)/shard_map/ppermute | solution.py:408
  34.7 10.1 %collective-permute-start.4 = (bf16[4,288,128]{2,1,0:T(8,128)(2,1)S(1)}, bf16[4,288,128]{2,1,0:T(8,128)(2,1)S(1)}, u32[]{:S(2)}, u32[]{:S(2)}) collective-permute-start(bf16[4,288,128]{2,1,0:T(8,128)(2,1)S(1)} %get-tuple-element.16), channel_id=1, source_target_pairs={{1,3},{2,1},{3,2},{5,7},{6,5},{7,6},{9,11},{10,9},{11,10},{13,15},... | collective-permute-start | bytes 884744 | tf_op jit(solution)/shard_map/ppermute | solution.py:409
  35.4 7.0 %collective-permute-start.2 = (s32[16]{0:T(128)S(1)}, s32[16]{0:T(128)S(1)}, u32[]{:S(2)}, u32[]{:S(2)}) collective-permute-start(s32[16]{0:T(128)S(1)} %get-tuple-element.13.near), channel_id=1, source_target_pairs={{0,4},{4,8},{8,12},{12,16},{16,20},{20,24},{24,28},{28,32},{32,36}... | collective-permute-start | bytes 200 | tf_op jit(solution)/shard_map/ppermute | solution.py:351
  46.5 16.8 %collective-permute-start.8 = (bf16[4,288,128]{2,1,0:T(8,128)(2,1)S(1)}, bf16[4,288,128]{2,1,0:T(8,128)(2,1)S(1)}, u32[]{:S(2)}, u32[]{:S(2)}) collective-permute-start(bf16[4,288,128]{2,1,0:T(8,128)(2,1)S(1)} %get-tuple-element.19.refs_8_), channel_id=1, source_target_pairs={{0,2},{1,3},{2,0},{3,1},{4,6},{5,7},{6,4},{7,5},{8,10},{9,11},{10,... | collective-permute-start | bytes 884744 | tf_op jit(solution)/shard_map/ppermute | solution.py:351
  55.7 10.8 %collective-permute-start.14 = (bf16[4,288,128]{2,1,0:T(8,128)(2,1)S(1)}, bf16[4,288,128]{2,1,0:T(8,128)(2,1)S(1)}, u32[]{:S(2)}, u32[]{:S(2)}) collective-permute-start(bf16[4,288,128]{2,1,0:T(8,128)(2,1)S(1)} %get-tuple-element.19.refs_8_), channel_id=1, source_target_pairs={{0,3},{1,0},{2,1},{3,2},{4,7},{5,4},{6,5},{7,6},{8,11},{9,8},{10,9... | collective-permute-start | bytes 884744 | tf_op jit(solution)/shard_map/ppermute | solution.py:351
  59.1 9.4 %collective-permute-start.12 = (bf16[4,288,128]{2,1,0:T(8,128)(2,1)S(1)}, bf16[4,288,128]{2,1,0:T(8,128)(2,1)S(1)}, u32[]{:S(2)}, u32[]{:S(2)}) collective-permute-start(bf16[4,288,128]{2,1,0:T(8,128)(2,1)S(1)} %get-tuple-element.19.refs_8_), channel_id=1, source_target_pairs={{0,1},{1,2},{2,3},{3,0},{4,5},{5,6},{6,7},{7,4},{8,9},{9,10},{10,1... | collective-permute-start | bytes 884744 | tf_op jit(solution)/shard_map/ppermute | solution.py:351
  59.1 12.5 %collective-permute-start.5 = (bf16[4,288,128]{2,1,0:T(8,128)(2,1)S(1)}, bf16[4,288,128]{2,1,0:T(8,128)(2,1)S(1)}, u32[]{:S(2)}, u32[]{:S(2)}) collective-permute-start(bf16[4,288,128]{2,1,0:T(8,128)(2,1)S(1)} %get-tuple-element.19.refs_8_), channel_id=1, source_target_pairs={{0,8},{4,12},{8,16},{12,20},{16,24},{20,28},{24,32},{28,36},{32,40... | collective-permute-start | bytes 884744 | tf_op jit(solution)/shard_map/ppermute | solution.py:351
  61.0 12.0 %collective-permute-start.11 = (bf16[4,288,128]{2,1,0:T(8,128)(2,1)S(1)}, bf16[4,288,128]{2,1,0:T(8,128)(2,1)S(1)}, u32[]{:S(2)}, u32[]{:S(2)}) collective-permute-start(bf16[4,288,128]{2,1,0:T(8,128)(2,1)S(1)} %get-tuple-element.19.refs_8_), channel_id=1, source_target_pairs={{0,4},{4,8},{8,12},{12,16},{16,20},{20,24},{24,28},{28,32},{32,36}... | collective-permute-start | bytes 884744 | tf_op jit(solution)/shard_map/ppermute | solution.py:351
  63.3 12.9 %collective-permute-start.9 = (bf16[4,288,128]{2,1,0:T(8,128)(2,1)S(1)}, bf16[4,288,128]{2,1,0:T(8,128)(2,1)S(1)}, u32[]{:S(2)}, u32[]{:S(2)}) collective-permute-start(bf16[4,288,128]{2,1,0:T(8,128)(2,1)S(1)} %collective-permute-done.8.refs_11_), channel_id=1, source_target_pairs={{0,4},{4,8},{8,12},{12,16},{16,20},{20,24},{24,28},{28,32},{32,36}... | collective-permute-start | bytes 884744 | tf_op jit(solution)/shard_map/ppermute | solution.py:351
  66.5 12.8 %collective-permute-start.15 = (bf16[4,288,128]{2,1,0:T(8,128)(2,1)S(1)}, bf16[4,288,128]{2,1,0:T(8,128)(2,1)S(1)}, u32[]{:S(2)}, u32[]{:S(2)}) collective-permute-start(bf16[4,288,128]{2,1,0:T(8,128)(2,1)S(1)} %collective-permute-done.14.refs_10_), channel_id=1, source_target_pairs={{0,4},{4,8},{8,12},{12,16},{16,20},{20,24},{24,28},{28,32},{32,36}... | collective-permute-start | bytes 884744 | tf_op jit(solution)/shard_map/ppermute | solution.py:351
  68.5 14.0 %collective-permute-start.13 = (bf16[4,288,128]{2,1,0:T(8,128)(2,1)S(1)}, bf16[4,288,128]{2,1,0:T(8,128)(2,1)S(1)}, u32[]{:S(2)}, u32[]{:S(2)}) collective-permute-start(bf16[4,288,128]{2,1,0:T(8,128)(2,1)S(1)} %collective-permute-done.12.refs_9_), channel_id=1, source_target_pairs={{0,4},{4,8},{8,12},{12,16},{16,20},{20,24},{24,28},{28,32},{32,36}... | collective-permute-start | bytes 884744 | tf_op jit(solution)/shard_map/ppermute | solution.py:351
  71.6 10.8 %collective-permute-start.7 = (bf16[4,288,128]{2,1,0:T(8,128)(2,1)S(1)}, bf16[4,288,128]{2,1,0:T(8,128)(2,1)S(1)}, u32[]{:S(2)}, u32[]{:S(2)}) collective-permute-start(bf16[4,288,128]{2,1,0:T(8,128)(2,1)S(1)} %collective-permute-done.5.refs_0_), channel_id=1, source_target_pairs={{1,0},{2,1},{3,2},{5,4},{6,5},{7,6},{9,8},{10,9},{11,10},{13,12},{... | collective-permute-start | bytes 884744 | tf_op jit(solution)/shard_map/ppermute | solution.py:351
  73.0 11.9 %collective-permute-start.6 = (bf16[4,288,128]{2,1,0:T(8,128)(2,1)S(1)}, bf16[4,288,128]{2,1,0:T(8,128)(2,1)S(1)}, u32[]{:S(2)}, u32[]{:S(2)}) collective-permute-start(bf16[4,288,128]{2,1,0:T(8,128)(2,1)S(1)} %collective-permute-done.5.refs_0_), channel_id=1, source_target_pairs={{1,2},{2,3},{3,0},{5,6},{6,7},{7,4},{9,10},{10,11},{11,8},{13,14},... | collective-permute-start | bytes 884744 | tf_op jit(solution)/shard_map/ppermute | solution.py:351
  76.1 10.1 %collective-permute-start.10 = (bf16[4,288,128]{2,1,0:T(8,128)(2,1)S(1)}, bf16[4,288,128]{2,1,0:T(8,128)(2,1)S(1)}, u32[]{:S(2)}, u32[]{:S(2)}) collective-permute-start(bf16[4,288,128]{2,1,0:T(8,128)(2,1)S(1)} %collective-permute-done.9.refs_7_), channel_id=1, source_target_pairs={{0,4},{4,8},{8,12},{12,16},{16,20},{20,24},{24,28},{28,32},{32,36}... | collective-permute-start | bytes 884744 | tf_op jit(solution)/shard_map/ppermute | solution.py:351
